TPU v7x, 512 devices: a whole 4x8x8 slice. The times are simulated.
512 devices in a mesh: head: 8 (over y_lo, x), seq: 64 (over y_hi, z, core).
Axes of the slice: x: 4, y: 8 (y_hi: 4, y_lo: 2; y = y_hi * 2 + y_lo), z: 8, core: 2. Of those that a mesh axis runs over, the one named last changes fastest.
Arguments:
- queries: bfloat16 [2, 4096, 4096], P(None, 'seq', 'head'), may hold values from -256 to 256
- keys: bfloat16 [2, 4096, 4096], P(None, 'seq', 'head'), may hold values from -256 to 256
- values: bfloat16 [2, 4096, 4096], P(None, 'seq', 'head'), may hold values from -6 to 6
- token_rates: float32 [1, 16, 4096], P(None, 'head', 'seq'), may hold values from 0.1 to 1
- step_size: float32 [16], P('head'), may hold values from 0.3 to 1
- w_gate: bfloat16 [16, 256, 512], P('head', 'seq'), may hold values from -0.375 to 0.375
- w_up: bfloat16 [16, 256, 512], P('head', 'seq'), may hold values from -0.375 to 0.375
- w_down: bfloat16 [16, 512, 256], P('head', 'seq'), may hold values from -0.25 to 0.25
- norm_gain: float32 [4096], replicated, may hold values from 0.5 to 1.5
Outputs:
- mixed: bfloat16 [2, 4096, 4096], P(None, ('seq', 'head'))
All inputs are finite; a program needn't handle non-finite values.
Results may differ from a plain program's by a relative error of at most 0.0095.
Values may be sent and summed in bfloat16 or wider, within the bound.
No kernel may reach another device: no remote copies, remote signals or barrier semaphores. Data moves between devices by JAX's collectives and lax.ppermute only.
A program may use at most 64 MiB of HBM per device.

v0:
```python
import math

import jax
import jax.numpy as jnp
from jax import lax
from jax.sharding import PartitionSpec as P

DH = 256
DF = 512
WIN = 512
NS_STEPS = 5


def spread(block, axis, holder):
    block = jnp.where(lax.axis_index(axis) == holder, block, jnp.zeros_like(block))
    return lax.psum(block, axis)


def shifted(array, axis, by):
    count = lax.axis_size(axis)
    return lax.ppermute(array, axis, [(i, (i + by) % count) for i in range(count)])


def rms_norm(values_in):
    wide = values_in.astype(jnp.float32)
    mean_square = jnp.mean(wide * wide, axis=-1, keepdims=True)
    return (wide * lax.rsqrt(mean_square + 1e-06)).astype(jnp.bfloat16)


def newton(grad_in):
    norm_value = jnp.sqrt(jnp.sum(grad_in * grad_in))
    iterate = grad_in / (norm_value + 1e-07)
    for _ in range(NS_STEPS):
        gram = jnp.dot(
            iterate, iterate.T, precision=lax.Precision.HIGHEST, preferred_element_type=jnp.float32
        )
        poly = -4.775 * gram + 2.0315 * jnp.dot(
            gram, gram, precision=lax.Precision.HIGHEST, preferred_element_type=jnp.float32
        )
        iterate = 3.4445 * iterate + jnp.dot(
            poly, iterate, precision=lax.Precision.HIGHEST, preferred_element_type=jnp.float32
        )
    return iterate


def orthogonalize(summed, seq_count, seq_index):
    problems = summed.shape[0]
    stride = 1
    problem = jnp.clip(seq_index // stride + 0, 0, problems - 1)
    owned = [newton(lax.dynamic_index_in_dim(summed, problem, 0, keepdims=False))]
    results = []
    for problem_index in range(problems):
        results.append(
            spread(
                owned[problem_index // seq_count].astype(jnp.bfloat16),
                "seq",
                problem_index % seq_count * stride,
            ).astype(jnp.float32)
        )
    return jnp.stack(results)


def body(queries, keys, values, token_rates, step_size, w_gate, w_up, w_down, norm_gain):
    blocks_here, tok_rows, width_here = queries.shape
    head_count = width_here // DH
    seq_count = lax.axis_size("seq")
    seq_index = lax.axis_index("seq")
    gate_fast, up_fast, down_fast = (
        lax.all_gather(w_gate, "seq", axis=1, tiled=True),
        lax.all_gather(w_up, "seq", axis=1, tiled=True),
        lax.all_gather(w_down, "seq", axis=1, tiled=True),
    )
    reach_count = -(-WIN // tok_rows)
    earlier_blocks = []
    for distance in range(1, reach_count + 1):
        arrived = shifted((keys, values), "seq", distance)
        settled = []
        for part_arr in arrived:
            before = jnp.concatenate([jnp.zeros_like(part_arr[:1]), part_arr[:-1]], 0)
            settled.append(jnp.where(seq_index >= distance, part_arr, before))
        earlier_blocks.insert(0, settled)
    context_keys = jnp.concatenate([pair_item[0] for pair_item in earlier_blocks] + [keys], 1)
    context_values = jnp.concatenate([pair_item[1] for pair_item in earlier_blocks] + [values], 1)
    context_len = context_keys.shape[1]
    context_keys = context_keys.reshape(blocks_here, context_len, head_count, DH)
    context_values = context_values.reshape(blocks_here, context_len, head_count, DH)
    query_heads = queries.reshape(blocks_here, tok_rows, head_count, DH)
    key_heads = keys.reshape(blocks_here, tok_rows, head_count, DH)
    value_heads = values.reshape(blocks_here, tok_rows, head_count, DH)
    scores = jnp.einsum(
        "bihd,bjhd->bhij", query_heads, context_keys, preferred_element_type=jnp.float32
    ) * (1.0 / math.sqrt(DH))
    query_rows = jnp.arange(tok_rows, dtype=jnp.int32)
    key_rows = jnp.arange(context_len, dtype=jnp.int32)
    row_gap = reach_count * tok_rows + query_rows[:, None] - key_rows[None, :]
    block_ids = jnp.arange(blocks_here, dtype=jnp.int32)
    key_pos = (
        block_ids[:, None] * (tok_rows * seq_count)
        + seq_index * tok_rows
        - reach_count * tok_rows
        + key_rows[None, :]
    )
    allowed = ((row_gap >= 0) & (row_gap < WIN))[None, :, :] & (key_pos >= 0)[:, None, :]
    scores = jnp.where(allowed[:, None, :, :], scores, -1e30)
    row_top = jnp.max(scores, axis=-1, keepdims=True)
    exp_scores = jnp.exp(scores - row_top)
    attn_weights = (exp_scores / jnp.sum(exp_scores, axis=-1, keepdims=True)).astype(jnp.bfloat16)
    attention = jnp.einsum(
        "bhij,bjhd->bihd", attn_weights, context_values, preferred_element_type=jnp.float32
    )
    query_norm = rms_norm(query_heads)
    key_norm = rms_norm(key_heads[: blocks_here - 1])
    fast_parts = []
    for block_index in range(blocks_here):
        gate_query = jnp.einsum(
            "thd,hdf->htf", query_norm[block_index], gate_fast, preferred_element_type=jnp.float32
        )
        up_query = jnp.einsum(
            "thd,hdf->htf", query_norm[block_index], up_fast, preferred_element_type=jnp.float32
        )
        hidden = (jax.nn.silu(gate_query) * up_query).astype(jnp.bfloat16)
        fast_parts.append(
            jnp.einsum("htf,hfd->thd", hidden, down_fast, preferred_element_type=jnp.float32)
        )
        if block_index < blocks_here - 1:
            keys_now = key_norm[block_index]
            vals_now = value_heads[block_index]
            gate_pre = jnp.einsum(
                "thd,hdf->htf", keys_now, gate_fast, preferred_element_type=jnp.float32
            )
            up_pre = jnp.einsum(
                "thd,hdf->htf", keys_now, up_fast, preferred_element_type=jnp.float32
            )
            back = jnp.einsum(
                "thd,hfd->htf", vals_now, down_fast, preferred_element_type=jnp.float32
            )
            rate_col = token_rates[block_index][:, :, None]
            sigmoid_val = jax.nn.sigmoid(gate_pre)
            act_val = gate_pre * sigmoid_val
            d_gate = (
                rate_col * back * up_pre * sigmoid_val * (1.0 + gate_pre * (1.0 - sigmoid_val))
            ).astype(jnp.bfloat16)
            d_up = (rate_col * back * act_val).astype(jnp.bfloat16)
            h_rate = (rate_col * act_val * up_pre).astype(jnp.bfloat16)
            grad_gate = jnp.einsum(
                "thd,htf->hdf", keys_now, d_gate, preferred_element_type=jnp.float32
            )
            grad_up = jnp.einsum("thd,htf->hdf", keys_now, d_up, preferred_element_type=jnp.float32)
            grad_down_t = jnp.einsum(
                "thd,htf->hdf", vals_now, h_rate, preferred_element_type=jnp.float32
            )
            stacked = jnp.stack([grad_gate, grad_up, grad_down_t], 1).reshape(
                head_count * 3, DH, DF
            )
            summed = lax.psum(stacked, "seq")
            orthogonal = orthogonalize(summed, seq_count, seq_index).reshape(head_count, 3, DH, DF)
            step_col = step_size[:, None, None]
            gate_fast = (gate_fast.astype(jnp.float32) + step_col * orthogonal[:, 0]).astype(
                jnp.bfloat16
            )
            up_fast = (up_fast.astype(jnp.float32) + step_col * orthogonal[:, 1]).astype(
                jnp.bfloat16
            )
            down_fast = (
                down_fast.astype(jnp.float32) + step_col * jnp.swapaxes(orthogonal[:, 2], 1, 2)
            ).astype(jnp.bfloat16)
    fast_out = jnp.stack(fast_parts)
    combined = (
        (fast_out + attention).astype(jnp.bfloat16).reshape(blocks_here, tok_rows, width_here)
    )
    wide = lax.all_to_all(combined, "head", split_axis=1, concat_axis=2, tiled=True).astype(
        jnp.float32
    )
    mean_square = jnp.mean(wide * wide, axis=-1, keepdims=True)
    return (wide * lax.rsqrt(mean_square + 1e-06) * norm_gain).astype(jnp.bfloat16)


def solution(mesh):
    placed = (
        P(None, "seq", "head"),
        P(None, "seq", "head"),
        P(None, "seq", "head"),
        P(None, "head", "seq"),
        P("head"),
        P("head", "seq", None),
        P("head", "seq", None),
        P("head", "seq", None),
        P(),
    )
    return jax.shard_map(
        body, mesh=mesh, in_specs=placed, out_specs=P(None, ("seq", "head"), None), check_vma=False
    )
```

profile of v0, /device:TPU:1, one launch (start us, length us, event | category | flops | bytes accessed | tf_op | source)
XLA Modules:
  0.0 1475.3 jit_solution(10621219490444785268)
XLA Ops:
  6.5 11.6 collective-permute-start
  18.1 2.5 collective-permute-start.1
  20.6 6.6 collective-permute-start.2
  27.2 5.8 collective-permute-start.3
  33.0 4.0 collective-permute-start.4
  40.1 88.6 %all_gather.9 = bf16[2,256,512]{2,0,1:T(2,128)(2,1)S(1)} all-gather(bf16[2,4,512]{2,0,1:T(2,128)(2,1)S(1)} %copy.91), channel_id=1, replica_groups=mesh['head'=8,'seq'=64] {'seq'}, dimensions={1}, use_global_device_ids=true | all-gather | bytes 532480 | tf_op jit(solution)/shard_map/all_gather | solution.py:69
  128.6 80.5 %all_gather.10 = bf16[2,256,512]{2,0,1:T(2,128)(2,1)S(1)} all-gather(bf16[2,4,512]{2,0,1:T(2,128)(2,1)S(1)} %copy.93), channel_id=1, replica_groups=mesh['head'=8,'seq'=64] {'seq'}, dimensions={1}, use_global_device_ids=true | all-gather | bytes 532480 | tf_op jit(solution)/shard_map/all_gather | solution.py:70
  209.7 77.9 %all_gather.11 = bf16[2,512,256]{2,0,1:T(2,128)(2,1)S(1)} all-gather(bf16[2,8,256]{2,0,1:T(2,128)(2,1)S(1)} %copy.95), channel_id=1, replica_groups=mesh['head'=8,'seq'=64] {'seq'}, dimensions={1}, use_global_device_ids=true | all-gather | bytes 532480 | tf_op jit(solution)/shard_map/all_gather | solution.py:71
  290.2 2.0 copy.106
  294.4 1.9 collective-permute-start.5
  296.5 3.4 collective-permute-start.6
  299.9 1.9 collective-permute-start.8
  301.9 1.9 collective-permute-start.9
  303.8 4.7 collective-permute-start.10
  308.5 11.1 collective-permute-start.11
  319.7 3.0 collective-permute-start.12
  322.8 2.7 collective-permute-start.13
  325.5 3.4 collective-permute-done.9
  328.9 1.9 collective-permute-start.14
  330.8 5.3 collective-permute-done.10
  336.1 1.9 collective-permute-start.15
  338.0 2.3 collective-permute-done.11
  340.3 5.9 collective-permute-start.7
  346.3 2.0 convolution_bitcast_fusion.4
  351.2 9.3 collective-permute-done.14
  367.7 503.6 %all-reduce.20.cloned.1.call-done = f32[6,256,512]{2,1,0:T(8,128)} async-done(((f32[6,256,512]{2,1,0:T(8,128)}), f32[6,256,512]{2,1,0:T(8,128)}) %all-reduce.20.cloned.1.call-update) | async-done | bytes 3145744 | tf_op jit(solution)/shard_map/psum | solution.py:155
  873.8 1.8 fusion.43
  876.0 1.9 convolution_add_fusion.4
  883.9 1.9 select_bitcast_fusion
  893.8 555.3 %all-reduce.22.cloned.1.call-done = (bf16[1,256,512]{2,1,0:T(8,128)(2,1)}, bf16[1,256,512]{2,1,0:T(8,128)(2,1)}, bf16[1,256,512]{2,1,0:T(8,128)(2,1)}, bf16[1,25...) async-done(((bf16[1,256,512]{2,1,0:T(8,128)(2,1)}, bf16[1,256,512]{2,1,0:T(8,128)(2,1)}, bf16[1,256,512]{2,1,0:T(8,128)(2,1)}, ...) | async-done | bytes 1572880 | tf_op jit(solution)/shard_map/psum | solution.py:16
  1453.8 2.1 convolution_bitcast_fusion.3
  1457.9 9.3 all_to_all.4
  (206 shorter events, 42.0 us)
Async XLA Ops:
  6.5 33.5 %copy-start.35 = (bf16[2,4,512]{2,1,0:T(4,128)(2,1)S(1)}, bf16[2,4,512]{2,1,0:T(4,128)(2,1)}, u32[]{:S(2)}) copy-start(bf16[2,4,512]{2,1,0:T(4,128)(2,1)} %param.14) | copy-start | bytes 24580
  6.5 122.1 %copy-start.36 = (bf16[2,4,512]{2,1,0:T(4,128)(2,1)S(1)}, bf16[2,4,512]{2,1,0:T(4,128)(2,1)}, u32[]{:S(2)}) copy-start(bf16[2,4,512]{2,1,0:T(4,128)(2,1)} %param.15) | copy-start | bytes 24580
  6.5 864.8 %all-reduce.20.cloned.1.call-start = ((), (), s32[]{:S(2)}) async-start(), calls=%async_computation.1 | async-start | bytes 6291456 | tf_op jit(solution)/shard_map/psum | solution.py:155
  6.5 287.9 %collective-permute-start = (bf16[2,64,512]{2,1,0:T(8,128)(2,1)}, bf16[2,64,512]{2,1,0:T(8,128)(2,1)S(1)}, u32[]{:S(2)}, u32[]{:S(2)}) collective-permute-start(bf16[2,64,512]{2,1,0:T(8,128)(2,1)} %param.11), channel_id=1, source_target_pairs={{0,8},{1,9},{2,10},{3,11},{4,12},{5,13},{6,14},{7,15},{8,16},{9,17... | collective-permute-start | bytes 393224 | tf_op jit(solution)/shard_map/ppermute | solution.py:21
  18.1 278.3 %collective-permute-start.1 = (bf16[2,64,512]{2,1,0:T(8,128)(2,1)}, bf16[2,64,512]{2,1,0:T(8,128)(2,1)S(1)}, u32[]{:S(2)}, u32[]{:S(2)}) collective-permute-start(bf16[2,64,512]{2,1,0:T(8,128)(2,1)} %param.11), channel_id=1, source_target_pairs={{0,7},{1,8},{2,9},{3,10},{4,11},{5,12},{6,13},{7,14},{8,15},{9,16}... | collective-permute-start | bytes 393224 | tf_op jit(solution)/shard_map/ppermute | solution.py:21
  20.6 279.3 %collective-permute-start.2 = (bf16[2,64,512]{2,1,0:T(8,128)(2,1)}, bf16[2,64,512]{2,1,0:T(8,128)(2,1)S(1)}, u32[]{:S(2)}, u32[]{:S(2)}) collective-permute-start(bf16[2,64,512]{2,1,0:T(8,128)(2,1)} %param.11), channel_id=1, source_target_pairs={{0,6},{1,7},{2,8},{3,9},{4,10},{5,11},{6,12},{7,13},{8,14},{9,15},... | collective-permute-start | bytes 393224 | tf_op jit(solution)/shard_map/ppermute | solution.py:21
  27.2 274.7 %collective-permute-start.3 = (bf16[2,64,512]{2,1,0:T(8,128)(2,1)}, bf16[2,64,512]{2,1,0:T(8,128)(2,1)S(1)}, u32[]{:S(2)}, u32[]{:S(2)}) collective-permute-start(bf16[2,64,512]{2,1,0:T(8,128)(2,1)} %param.11), channel_id=1, source_target_pairs={{0,5},{1,6},{2,7},{3,8},{4,9},{5,10},{6,11},{7,12},{8,13},{9,14},{... | collective-permute-start | bytes 393224 | tf_op jit(solution)/shard_map/ppermute | solution.py:21
  33.0 270.8 %collective-permute-start.4 = (bf16[2,64,512]{2,1,0:T(8,128)(2,1)}, bf16[2,64,512]{2,1,0:T(8,128)(2,1)S(1)}, u32[]{:S(2)}, u32[]{:S(2)}) collective-permute-start(bf16[2,64,512]{2,1,0:T(8,128)(2,1)} %param.11), channel_id=1, source_target_pairs={{0,4},{1,5},{2,6},{3,7},{4,8},{5,9},{6,10},{7,11},{8,12},{9,13},{1... | collective-permute-start | bytes 393224 | tf_op jit(solution)/shard_map/ppermute | solution.py:21
  128.6 81.0 %copy-start.37 = (bf16[2,8,256]{2,1,0:T(8,128)(2,1)S(1)}, bf16[2,8,256]{2,1,0:T(8,128)(2,1)}, u32[]{:S(2)}) copy-start(bf16[2,8,256]{2,1,0:T(8,128)(2,1)} %param.16) | copy-start | bytes 24580
  209.4 78.9 %copy-start.38 = (f32[1,2,64]{2,1,0:T(2,128)S(1)}, f32[1,2,64]{2,1,0:T(2,128)}, u32[]{:S(2)}) copy-start(f32[1,2,64]{2,1,0:T(2,128)} %param.12) | copy-start | bytes 1540
  292.2 1156.9 %all-reduce.22.cloned.1.call-start = ((), (), s32[]{:S(2)}) async-start(), calls=%async_computation.2 | async-start | bytes 3145728 | tf_op jit(solution)/shard_map/psum | solution.py:16
  294.4 53.9 %copy-start.11 = (bf16[2,64,512]{2,1,0:T(8,128)(2,1)}, bf16[2,64,512]{2,1,0:T(8,128)(2,1)S(1)}, u32[]{:S(2)}) copy-start(bf16[2,64,512]{2,1,0:T(8,128)(2,1)S(1)} %collective-permute-done) | copy-start | bytes 393220
  294.4 14.1 collective-permute-start.5
  296.4 51.9 %copy-start.9 = (bf16[2,64,512]{2,1,0:T(8,128)(2,1)}, bf16[2,64,512]{2,1,0:T(8,128)(2,1)S(1)}, u32[]{:S(2)}) copy-start(bf16[2,64,512]{2,1,0:T(8,128)(2,1)S(1)} %collective-permute-done.1) | copy-start | bytes 393220
  296.5 23.2 %collective-permute-start.6 = (bf16[2,64,512]{2,1,0:T(8,128)(2,1)S(1)}, bf16[2,64,512]{2,1,0:T(8,128)(2,1)S(1)}, u32[]{:S(2)}, u32[]{:S(2)}) collective-permute-start(bf16[2,64,512]{2,1,0:T(8,128)(2,1)S(1)} %copy-done.27), channel_id=1, source_target_pairs={{0,2},{1,3},{2,4},{3,5},{4,6},{5,7},{6,8},{7,9},{8,10},{9,11},{10,... | collective-permute-start | bytes 393224 | tf_op jit(solution)/shard_map/ppermute | solution.py:21
  299.9 48.4 %copy-start.7 = (bf16[2,64,512]{2,1,0:T(8,128)(2,1)}, bf16[2,64,512]{2,1,0:T(8,128)(2,1)S(1)}, u32[]{:S(2)}) copy-start(bf16[2,64,512]{2,1,0:T(8,128)(2,1)S(1)} %collective-permute-done.2) | copy-start | bytes 393220
  299.9 22.8 %collective-permute-start.8 = (bf16[2,64,512]{2,1,0:T(8,128)(2,1)S(1)}, bf16[2,64,512]{2,1,0:T(8,128)(2,1)S(1)}, u32[]{:S(2)}, u32[]{:S(2)}) collective-permute-start(bf16[2,64,512]{2,1,0:T(8,128)(2,1)S(1)} %copy-done.1), channel_id=1, source_target_pairs={{0,8},{1,9},{2,10},{3,11},{4,12},{5,13},{6,14},{7,15},{8,16},{9,17... | collective-permute-start | bytes 393224 | tf_op jit(solution)/shard_map/ppermute | solution.py:21
  301.9 46.5 %copy-start.5 = (bf16[2,64,512]{2,1,0:T(8,128)(2,1)}, bf16[2,64,512]{2,1,0:T(8,128)(2,1)S(1)}, u32[]{:S(2)}) copy-start(bf16[2,64,512]{2,1,0:T(8,128)(2,1)S(1)} %collective-permute-done.3) | copy-start | bytes 393220
  301.9 27.0 %collective-permute-start.9 = (bf16[2,64,512]{2,1,0:T(8,128)(2,1)S(1)}, bf16[2,64,512]{2,1,0:T(8,128)(2,1)}, u32[]{:S(2)}, u32[]{:S(2)}) collective-permute-start(bf16[2,64,512]{2,1,0:T(8,128)(2,1)S(1)} %copy-done.1), channel_id=1, source_target_pairs={{0,7},{1,8},{2,9},{3,10},{4,11},{5,12},{6,13},{7,14},{8,15},{9,16}... | collective-permute-start | bytes 393224 | tf_op jit(solution)/shard_map/ppermute | solution.py:21
  303.8 44.6 %copy-start.3 = (bf16[2,64,512]{2,1,0:T(8,128)(2,1)}, bf16[2,64,512]{2,1,0:T(8,128)(2,1)S(1)}, u32[]{:S(2)}) copy-start(bf16[2,64,512]{2,1,0:T(8,128)(2,1)S(1)} %collective-permute-done.4) | copy-start | bytes 393220
  303.8 32.2 %collective-permute-start.10 = (bf16[2,64,512]{2,1,0:T(8,128)(2,1)S(1)}, bf16[2,64,512]{2,1,0:T(8,128)(2,1)S(1)}, u32[]{:S(2)}, u32[]{:S(2)}) collective-permute-start(bf16[2,64,512]{2,1,0:T(8,128)(2,1)S(1)} %copy-done.1), channel_id=1, source_target_pairs={{0,6},{1,7},{2,8},{3,9},{4,10},{5,11},{6,12},{7,13},{8,14},{9,15},... | collective-permute-start | bytes 393224 | tf_op jit(solution)/shard_map/ppermute | solution.py:21
  308.5 39.9 %copy-start.19 = (bf16[2,64,512]{2,1,0:T(8,128)(2,1)}, bf16[2,64,512]{2,1,0:T(8,128)(2,1)S(1)}, u32[]{:S(2)}) copy-start(bf16[2,64,512]{2,1,0:T(8,128)(2,1)S(1)} %collective-permute-done.5) | copy-start | bytes 393220
  308.5 31.8 %collective-permute-start.11 = (bf16[2,64,512]{2,1,0:T(8,128)(2,1)S(1)}, bf16[2,64,512]{2,1,0:T(8,128)(2,1)S(1)}, u32[]{:S(2)}, u32[]{:S(2)}) collective-permute-start(bf16[2,64,512]{2,1,0:T(8,128)(2,1)S(1)} %copy-done.1), channel_id=1, source_target_pairs={{0,5},{1,6},{2,7},{3,8},{4,9},{5,10},{6,11},{7,12},{8,13},{9,14},{... | collective-permute-start | bytes 393224 | tf_op jit(solution)/shard_map/ppermute | solution.py:21
  319.7 28.7 %copy-start.13 = (bf16[2,64,512]{2,1,0:T(8,128)(2,1)}, bf16[2,64,512]{2,1,0:T(8,128)(2,1)S(1)}, u32[]{:S(2)}) copy-start(bf16[2,64,512]{2,1,0:T(8,128)(2,1)S(1)} %collective-permute-done.6) | copy-start | bytes 393220
  319.7 29.7 %collective-permute-start.12 = (bf16[2,64,512]{2,1,0:T(8,128)(2,1)S(1)}, bf16[2,64,512]{2,1,0:T(8,128)(2,1)}, u32[]{:S(2)}, u32[]{:S(2)}) collective-permute-start(bf16[2,64,512]{2,1,0:T(8,128)(2,1)S(1)} %copy-done.1), channel_id=1, source_target_pairs={{0,4},{1,5},{2,6},{3,7},{4,8},{5,9},{6,10},{7,11},{8,12},{9,13},{1... | collective-permute-start | bytes 393224 | tf_op jit(solution)/shard_map/ppermute | solution.py:21
  322.8 28.4 %collective-permute-start.13 = (bf16[2,64,512]{2,1,0:T(8,128)(2,1)S(1)}, bf16[2,64,512]{2,1,0:T(8,128)(2,1)S(1)}, u32[]{:S(2)}, u32[]{:S(2)}) collective-permute-start(bf16[2,64,512]{2,1,0:T(8,128)(2,1)S(1)} %copy-done.1), channel_id=1, source_target_pairs={{0,3},{1,4},{2,5},{3,6},{4,7},{5,8},{6,9},{7,10},{8,11},{9,12},{10... | collective-permute-start | bytes 393224 | tf_op jit(solution)/shard_map/ppermute | solution.py:21
  328.9 31.6 %collective-permute-start.14 = (bf16[2,64,512]{2,1,0:T(8,128)(2,1)S(1)}, bf16[2,64,512]{2,1,0:T(8,128)(2,1)S(1)}, u32[]{:S(2)}, u32[]{:S(2)}) collective-permute-start(bf16[2,64,512]{2,1,0:T(8,128)(2,1)S(1)} %copy-done.1), channel_id=1, source_target_pairs={{0,2},{1,3},{2,4},{3,5},{4,6},{5,7},{6,8},{7,9},{8,10},{9,11},{10,... | collective-permute-start | bytes 393224 | tf_op jit(solution)/shard_map/ppermute | solution.py:21
  336.1 24.4 %collective-permute-start.15 = (bf16[2,64,512]{2,1,0:T(8,128)(2,1)S(1)}, bf16[2,64,512]{2,1,0:T(8,128)(2,1)}, u32[]{:S(2)}, u32[]{:S(2)}) collective-permute-start(bf16[2,64,512]{2,1,0:T(8,128)(2,1)S(1)} %copy-done.1), channel_id=1, source_target_pairs={{0,1},{1,2},{2,3},{3,4},{4,5},{5,6},{6,7},{7,8},{8,9},{9,10},{10,1... | collective-permute-start | bytes 393224 | tf_op jit(solution)/shard_map/ppermute | solution.py:21
  340.3 21.1 %collective-permute-start.7 = (bf16[2,64,512]{2,1,0:T(8,128)(2,1)}, bf16[2,64,512]{2,1,0:T(8,128)(2,1)}, u32[]{:S(2)}, u32[]{:S(2)}) collective-permute-start(bf16[2,64,512]{2,1,0:T(8,128)(2,1)} %param.11), channel_id=1, source_target_pairs={{0,1},{1,2},{2,3},{3,4},{4,5},{5,6},{6,7},{7,8},{8,9},{9,10},{10,1... | collective-permute-start | bytes 393224 | tf_op jit(solution)/shard_map/ppermute | solution.py:21
  348.4 15.3 %copy-start.8 = (bf16[2,64,512]{2,1,0:T(8,128)(2,1)S(1)}, bf16[2,64,512]{2,1,0:T(8,128)(2,1)}, u32[]{:S(2)}) copy-start(bf16[2,64,512]{2,1,0:T(8,128)(2,1)} %copy-done.7) | copy-start | bytes 393220
  348.4 15.3 %slice-start.2 = ((bf16[2,64,512]{2,1,0:T(8,128)(2,1)}), bf16[1,64,512]{2,1,0:T(8,128)(2,1)S(1)}, s32[]{:S(2)}) async-start(bf16[2,64,512]{2,1,0:T(8,128)(2,1)} %copy-done.7), calls=%async_computation.5 | async-start | bytes 131072 | tf_op jit(solution)/shard_map/slice | solution.py:79
  349.4 15.0 %slice-start.10 = ((bf16[2,64,512]{2,1,0:T(8,128)(2,1)}), bf16[1,64,512]{2,1,0:T(8,128)(2,1)S(1)}, s32[]{:S(2)}) async-start(bf16[2,64,512]{2,1,0:T(8,128)(2,1)} %copy-done.23), calls=%async_computation.13 | async-start | bytes 131072 | tf_op jit(solution)/shard_map/slice | solution.py:79
  (39 other events, 234.9 us)
Sparse Core Ops, SparseCore 0:
  292.3 578.9 all-reduce.19
  885.9 563.1 all-reduce.21
where the time goes:
time: 1480 us
  waiting for transfers between devices  1080 us (73%)
  blocking collectives  256 us (17%)
  starting transfers between devices  71 us (5%)
  matrix products  22.4 us (2%)
  local copies, waits for them, and re-layouts  15.9 us (1%)
  between operations  15.2 us (1%)
    psum x1, waiting for transfers between devices, spread(): return lax.psum(block, axis)  555 us
    psum x1, waiting for transfers between devices, body(): summed = lax.psum(stacked, 'seq')  504 us
    all_gather x1, blocking collectives, body(): lax.all_gather(w_gate, 'seq', axis=1, tiled=True)  88.6 us
    all_gather x1, blocking collectives, body(): lax.all_gather(w_up, 'seq', axis=1, tiled=True)  80.5 us
    all_gather x1, blocking collectives, body(): lax.all_gather(w_down, 'seq', axis=1, tiled=True)  77.9 us
    ppermute x16, starting transfers between devices, shifted(): lax.ppermute(array, axis, [(i, (i + by) % count) for i in range(count)])  70.9 us
  transfers between devices with their start and end apart: 18, of which 7 were waited for; matrix products, arithmetic and copies ran while one was open for 2% of the time, Pallas kernels for 0%

commit v1 on v0

v1 whole, which is shorter than its diff:
```python
import math

import jax
import jax.numpy as jnp
from jax import lax
from jax.experimental import pallas as pl
from jax.experimental.pallas import tpu as pltpu
from jax.sharding import Mesh
from jax.sharding import PartitionSpec as P

DH = 256
DF = 512
NS_STEPS = 5
CHIPS = 32
TOK = 128
REACH = 4
RING = ("y_hi", "z")
F32 = jnp.float32
BF = jnp.bfloat16


def matmul(left, right):
    return lax.dot_general(left, right, (((1,), (0,)), ((), ())), preferred_element_type=F32)


def matmul_nt(left, right):
    return lax.dot_general(left, right, (((1,), (1,)), ((), ())), preferred_element_type=F32)


def matmul_tn(left, right):
    return lax.dot_general(left, right, (((0,), (0,)), ((), ())), preferred_element_type=F32)


def halves(wide):
    high = wide.astype(BF)
    return high, (wide - high.astype(F32)).astype(BF)


def rms_norm(values_in):
    wide = values_in.astype(F32)
    mean_square = jnp.mean(wide * wide, axis=-1, keepdims=True)
    return (wide * lax.rsqrt(mean_square + 1e-06)).astype(BF)


def sigmoid(value):
    return 1.0 / (1.0 + jnp.exp(-value))


def rows_of(ref, first, count, width):
    piece = ref[:, first : first + 8, :].astype(F32)
    return piece.reshape(count * 8, width).astype(BF)


def fast_forward(query, gate_fast, up_fast, down_fast):
    query_norm = rms_norm(query)
    gate_query = matmul(query_norm, gate_fast)
    up_query = matmul(query_norm, up_fast)
    hidden = (gate_query * sigmoid(gate_query) * up_query).astype(BF)
    return matmul(hidden, down_fast)


def grad_kernel(kv_ref, rate_ref, raw_ref, grad_ref, gate_ref, up_ref, down_ref):
    out_row = lax.broadcasted_iota(jnp.int32, (DH, 2 * DH), 0)
    in_row = lax.broadcasted_iota(jnp.int32, (DH, 2 * DH), 1)
    for first, target in ((0, gate_ref), (8, up_ref)):
        mixed = rows_of(raw_ref, first, 64, DH)
        for half in range(2):
            pick = (out_row // 4) * 8 + half * 4 + out_row % 4
            chosen = jnp.where(in_row == pick, 1.0, 0.0).astype(BF)
            target[:, half * DH : (half + 1) * DH] = matmul(chosen, mixed).astype(BF)
    down_ref[...] = rows_of(raw_ref, 16, 64, DH)
    keys_now = rms_norm(kv_ref[0, 0])
    vals_now = kv_ref[1, 0]
    row = lax.broadcasted_iota(jnp.int32, (TOK, TOK), 0)
    column = lax.broadcasted_iota(jnp.int32, (TOK, TOK), 1)
    spread = jnp.where(row == column, jnp.broadcast_to(rate_ref[...], (TOK, TOK)), 0.0)
    rate_col = jnp.sum(spread, axis=1, keepdims=True)
    gate_pre = matmul(keys_now, gate_ref[...])
    up_pre = matmul(keys_now, up_ref[...])
    back = matmul_nt(vals_now, down_ref[...])
    sigmoid_val = sigmoid(gate_pre)
    act_val = gate_pre * sigmoid_val
    rate_back = rate_col * back
    d_gate = (rate_back * up_pre * sigmoid_val * (1.0 + gate_pre * (1.0 - sigmoid_val))).astype(BF)
    d_up = (rate_back * act_val).astype(BF)
    h_rate = (rate_col * act_val * up_pre).astype(BF)
    for index, (left, right) in enumerate(
        ((keys_now, d_gate), (keys_now, d_up), (vals_now, h_rate))
    ):
        grad = matmul_tn(left, right).reshape(CHIPS, 8, DF)
        grad_ref[:, index * 8 : index * 8 + 8, :] = grad.astype(BF)


def sum_kernel(parts_ref, total_ref):
    total = jnp.sum(parts_ref[...].astype(F32), axis=0, keepdims=True)
    total_ref[...] = jnp.broadcast_to(total, (CHIPS, 24, DF)).astype(BF)


def attention_kernel(
    chip_ref, q_ref, own_ref, c1_ref, c2_ref, c3_ref, c4_ref, gate_ref, up_ref, down_ref, out_ref
):
    chip = chip_ref[0]
    row = lax.broadcasted_iota(jnp.int32, (TOK, TOK), 0)
    column = lax.broadcasted_iota(jnp.int32, (TOK, TOK), 1)
    scale = 1.0 / math.sqrt(DH)
    chunks = (own_ref, c1_ref, c2_ref, c3_ref, c4_ref)
    for block in range(2):
        query = q_ref[block]
        scores = []
        for distance, chunk in enumerate(chunks):
            behind = (chip < distance).astype(jnp.int32)
            slot = jnp.maximum(block - behind, 0)
            score = matmul_nt(query, chunk[0, slot]) * scale
            if distance == 0:
                score = jnp.where(row >= column, score, -1e30)
            elif distance == REACH:
                score = jnp.where(row < column, score, -1e30)
            if block == 0 and distance > 0:
                score = jnp.where(behind + jnp.zeros_like(row) > 0, -1e30, score)
            scores.append(score)
        top = scores[0]
        for score in scores[1:]:
            top = jnp.maximum(top, score)
        row_top = jnp.max(top, axis=-1, keepdims=True)
        exps = [jnp.exp(score - row_top) for score in scores]
        total = exps[0]
        for exp_score in exps[1:]:
            total = total + exp_score
        row_sum = jnp.sum(total, axis=-1, keepdims=True)
        result = None
        for distance, chunk in enumerate(chunks):
            behind = (chip < distance).astype(jnp.int32)
            slot = jnp.maximum(block - behind, 0)
            weights = (exps[distance] / row_sum).astype(BF)
            part = matmul(weights, chunk[1, slot])
            result = part if result is None else result + part
        if block == 0:
            result = result + fast_forward(query, gate_ref[...], up_ref[...], down_ref[...])
        out_ref[block] = result


def newton_kernel(
    step_ref, total_ref, gate_ref, up_ref, down_ref, q_ref, base_ref, out_ref, iterate_ref
):
    for index in range(3):
        piece = total_ref[:, index * 8 : index * 8 + 8, :].astype(F32)
        grad = piece.reshape(DH, DF)
        square = jnp.sum(jnp.sum(grad * grad, axis=0, keepdims=True), axis=1, keepdims=True)
        iterate_ref[index] = grad / (jnp.sqrt(square) + 1e-07)

    def one_step(_, carry):
        for index in range(3):
            iterate = iterate_ref[index]
            high, low = halves(iterate)
            gram = matmul_nt(high, high) + (matmul_nt(high, low) + matmul_nt(low, high))
            gram_high, gram_low = halves(gram)
            square = matmul(gram_high, gram_high) + (
                matmul(gram_high, gram_low) + matmul(gram_low, gram_high)
            )
            poly_high, poly_low = halves(-4.775 * gram + 2.0315 * square)
            iterate_ref[index] = 3.4445 * iterate + (
                matmul(poly_high, high) + (matmul(poly_high, low) + matmul(poly_low, high))
            )
        return carry

    lax.fori_loop(0, NS_STEPS, one_step, 0)
    step = step_ref[0]
    gate_fast = (gate_ref[...].astype(F32) + step * iterate_ref[0]).astype(BF)
    up_fast = (up_ref[...].astype(F32) + step * iterate_ref[1]).astype(BF)
    down_fast = (down_ref[...].astype(F32) + step * iterate_ref[2].T).astype(BF)
    fast = fast_forward(q_ref[1], gate_fast, up_fast, down_fast)
    out_ref[:, 0] = base_ref[0].reshape(16, 8, DH).astype(BF)
    out_ref[:, 1] = (fast + base_ref[1]).reshape(16, 8, DH).astype(BF)


def norm_kernel(parts_ref, gain_ref, out_ref):
    square = None
    for source in range(16):
        wide = parts_ref[source].astype(F32)
        part = jnp.sum(wide * wide, axis=-1, keepdims=True)
        square = part if square is None else square + part
    scale = lax.rsqrt(square * (1.0 / (16 * DH)) + 1e-06)
    for source in range(16):
        head = 2 * (source % 8) + source // 8
        columns = slice(head * DH, (head + 1) * DH)
        wide = parts_ref[source].astype(F32) * scale * gain_ref[:, columns][None]
        out_ref[:, :, columns] = wide.astype(BF)


PARAMS = pltpu.CompilerParams(vmem_limit_bytes=16 * 1024 * 1024)
VMEM = pl.BlockSpec(memory_space=pltpu.VMEM)
SMEM = pl.BlockSpec(memory_space=pltpu.SMEM)


def body(queries, keys, values, token_rates, step_size, w_gate, w_up, w_down, norm_gain):
    core = lax.axis_index("core")
    chip = lax.axis_index(RING)
    raw = jnp.concatenate(
        [
            w_gate.reshape(2, 4, 2, DH).transpose(0, 2, 1, 3).reshape(2, 8, DH),
            w_up.reshape(2, 4, 2, DH).transpose(0, 2, 1, 3).reshape(2, 8, DH),
            w_down,
        ],
        1,
    )
    raw = jnp.broadcast_to(raw[None], (CHIPS, 2, 24, DH)).reshape(64, 24, DH)
    raw = lax.all_to_all(raw, RING + ("core",), 0, 0, tiled=True)

    tokens = jnp.stack([queries, keys, values]).reshape(3, 2, 64, 2, DH)
    tokens = tokens.transpose(3, 0, 1, 2, 4).reshape(2, 384, DH)
    first = token_rates[0].astype(BF)
    rest = token_rates[0] - first.astype(F32)
    second = rest.astype(BF)
    third = (rest - second.astype(F32)).astype(BF)
    rates = jnp.concatenate([first, second, third, jnp.zeros_like(first)], 1)
    rates = jnp.pad(rates[:, None, :], ((0, 0), (0, 7), (0, 0)))
    mine = lax.all_to_all(jnp.concatenate([tokens, rates], 1), "core", 0, 0, tiled=True)
    tokens = mine[:, :384].reshape(2, 3, 2, 64, DH).transpose(1, 2, 0, 3, 4)
    tokens = tokens.reshape(3, 2, TOK, DH)
    query, own = tokens[0], tokens[1:]
    rates = mine[:, 384, :192].astype(F32).reshape(2, 3, 64)
    rates = (rates[:, 0] + (rates[:, 1] + rates[:, 2])).reshape(1, TOK)

    grad, gate_fast, up_fast, down_fast = pl.pallas_call(
        grad_kernel,
        out_shape=(
            jax.ShapeDtypeStruct((CHIPS, 24, DF), BF),
            jax.ShapeDtypeStruct((DH, DF), BF),
            jax.ShapeDtypeStruct((DH, DF), BF),
            jax.ShapeDtypeStruct((DF, DH), BF),
        ),
        in_specs=[VMEM] * 3,
        out_specs=(VMEM,) * 4,
        compiler_params=PARAMS,
        name="grad",
    )(own, rates, raw)
    parts = lax.all_to_all(grad, RING, 0, 0, tiled=True)
    total = pl.pallas_call(
        sum_kernel,
        out_shape=jax.ShapeDtypeStruct((CHIPS, 24, DF), BF),
        in_specs=[VMEM],
        out_specs=VMEM,
        compiler_params=PARAMS,
        name="sum",
    )(parts)
    total = lax.all_to_all(total, RING, 0, 0, tiled=True)

    chunks = [own]
    for _ in range(REACH):
        ring = [(i, (i + 1) % CHIPS) for i in range(CHIPS)]
        chunks.append(lax.ppermute(chunks[-1], RING, ring))
    base = pl.pallas_call(
        attention_kernel,
        out_shape=jax.ShapeDtypeStruct((2, TOK, DH), F32),
        in_specs=[SMEM] + [VMEM] * 9,
        out_specs=VMEM,
        compiler_params=PARAMS,
        name="window",
    )(chip.astype(jnp.int32).reshape(1), query, *chunks, gate_fast, up_fast, down_fast)

    step = lax.dynamic_slice_in_dim(step_size, core, 1, 0)
    combined = pl.pallas_call(
        newton_kernel,
        out_shape=jax.ShapeDtypeStruct((16, 2, 8, DH), BF),
        in_specs=[SMEM] + [VMEM] * 6,
        out_specs=VMEM,
        scratch_shapes=[pltpu.VMEM((3, DH, DF), F32)],
        compiler_params=PARAMS,
        name="newton",
    )(step, total, gate_fast, up_fast, down_fast, query, base)
    gathered = lax.all_to_all(combined, ("core", "y_lo", "x"), 0, 0, tiled=True)
    return pl.pallas_call(
        norm_kernel,
        out_shape=jax.ShapeDtypeStruct((2, 8, 16 * DH), BF),
        in_specs=[VMEM] * 2,
        out_specs=VMEM,
        compiler_params=PARAMS,
        name="norm",
    )(gathered, norm_gain.reshape(1, 16 * DH))


def solution(mesh):
    fine = Mesh(mesh.devices.reshape(2, 4, 4, 8, 2), ("y_lo", "x", "y_hi", "z", "core"))
    seq = RING + ("core",)
    head = ("y_lo", "x")
    placed = (
        P(None, seq, head),
        P(None, seq, head),
        P(None, seq, head),
        P(None, head, seq),
        P(head),
        P(head, seq, None),
        P(head, seq, None),
        P(head, seq, None),
        P(),
    )
    return jax.shard_map(
        body, mesh=fine, in_specs=placed, out_specs=P(None, seq + head, None), check_vma=False
    )
```

time: 1480 us -> 207 us (0.14)
  waiting for transfers between devices: 1080 us -> 87 us
  blocking collectives: 256 us -> 54 us
  starting transfers between devices: 71 us -> 35.1 us
  matrix products: 22.4 us -> 0 us
  Pallas kernels: 0 us -> 21.4 us
  between operations: 15.2 us -> 0.22 us
    psum x2 -> x0, waiting for transfers between devices: 1060 us -> none  [the longest x1 555 us: spread(): return lax.psum(block, axis)]
    all_gather x3 -> x0, blocking collectives: 247 us -> none  [the longest x1 88.6 us: body(): lax.all_gather(w_gate, 'seq', axis=1, tiled=True)]
    ppermute x16 -> x4, starting transfers between devices: 70.9 us -> 8.86 us  [body(): chunks.append(lax.ppermute(chunks[-1], RING, ring))]
    all_to_all x1 -> x2, blocking collectives: 9.33 us -> 54 us  [the longest x1 32.7 us: body(): parts = lax.all_to_all(grad, RING, 0, 0, tiled=True)]
    ppermute x16 -> x4, waiting for transfers between devices: 21.2 us -> 62.4 us  [body(): chunks.append(lax.ppermute(chunks[-1], RING, ring))]
    all_to_all x0 -> x3, starting transfers between devices: none -> 26.2 us  [the longest x1 11 us: body(): raw = lax.all_to_all(raw, RING + ('core',), 0, 0, tiled=True)]
    all_to_all x0 -> x3, waiting for transfers between devices: none -> 24.6 us  [the longest x1 24.6 us: body(): raw = lax.all_to_all(raw, RING + ('core',), 0, 0, tiled=True)]
    dot_general x27 -> x0, matrix products: 22.4 us -> none  [the longest x5 5.67 us: newton(): jnp.dot(poly, iterate, precision=lax.Precision.HIGHEST, preferred_element...]
  transfers between devices with their start and end apart: 18 -> 7, of which waited for: 7 -> 5; matrix products, arithmetic and copies ran while one was open for 2% -> 0% of each run, Pallas kernels for 0% -> 1%
where the time goes in v1:
time: 207 us; the launch traced here: 206 us
  waiting for transfers between devices  87 us (42%)
  blocking collectives  54 us (26%)
  starting transfers between devices  35.1 us (17%)
  Pallas kernels  21.4 us (10%)
  local copies, waits for them, and re-layouts  6.75 us (3%)
    ppermute x4, waiting for transfers between devices, body(): chunks.append(lax.ppermute(chunks[-1], RING, ring))  62.4 us
    all_to_all x1, blocking collectives, body(): parts = lax.all_to_all(grad, RING, 0, 0, tiled=True)  32.7 us
    all_to_all x1, waiting for transfers between devices, body(): raw = lax.all_to_all(raw, RING + ('core',), 0, 0, tiled=True)  24.6 us
    all_to_all x1, blocking collectives, body(): gathered = lax.all_to_all(combined, ('core', 'y_lo', 'x'), 0, 0, tiled=True)  21.3 us
    pallas_call x1, Pallas kernels, body(): pl.pallas_call(newton_kernel, out_shape=jax.ShapeDtypeStruct((16, 2, 8, D...  17.2 us
    all_to_all x1, starting transfers between devices, body(): raw = lax.all_to_all(raw, RING + ('core',), 0, 0, tiled=True)  11 us
    all_to_all x1, starting transfers between devices, body(): lax.all_to_all(jnp.concatenate([tokens, rates], 1), 'core', 0, 0, tiled=T...  10.4 us
    ppermute x4, starting transfers between devices, body(): chunks.append(lax.ppermute(chunks[-1], RING, ring))  8.86 us
  transfers between devices with their start and end apart: 7, of which 5 were waited for; matrix products, arithmetic and copies ran while one was open for 0% of the time, Pallas kernels for 1%

profile of v1, /device:TPU:1, one launch (start us, length us, event | category | flops | bytes accessed | tf_op | source)
XLA Modules:
  0.0 206.1 jit_solution(11381770824314775913)
XLA Ops:
  0.0 0.8 fusion.5
  0.8 0.1 maximum_bitcast_fusion
  0.9 0.9 stack.14
  1.9 0.9 copy-done.1
  2.9 0.9 copy-done.2
  3.8 0.8 fusion.1
  4.6 10.4 %all-to-all-start = ((bf16[2,392,256]{2,1,0:T(8,128)(2,1)}), bf16[2,392,256]{2,1,0:T(8,128)(2,1)S(1)}, u32[]{:S(2)}, u32[]{:S(2)}) async-start(bf16[2,392,256]{2,1,0:T(8,128)(2,1)} %fusion.1), calls=%async_computation | async-start | bytes 802816 | tf_op jit(solution)/shard_map/all_to_all | solution.py:217
  15.1 0.7 copy-done.4
  15.8 0.7 copy-done.5
  16.5 1.0 broadcast_in_dim.14
  17.4 11.0 %all-to-all-start.1 = ((bf16[64,24,256]{2,1,0:T(8,128)(2,1)}), bf16[64,24,256]{2,1,0:T(8,128)(2,1)S(1)}, u32[]{:S(2)}, u32[]{:S(2)}) async-start(bf16[64,24,256]{2,1,0:T(8,128)(2,1)} %bitcast.11), calls=%async_computation.1 | async-start | bytes 1572864 | tf_op jit(solution)/shard_map/all_to_all | solution.py:207
  28.6 0.1 reshape.82
  28.7 0.1 add.35.rate_ref
  28.8 24.6 %all-to-all-done.1.raw_ref = bf16[64,24,256]{2,1,0:T(8,128)(2,1)S(1)} async-done(((bf16[64,24,256]{2,1,0:T(8,128)(2,1)}), bf16[64,24,256]{2,1,0:T(8,128)(2,1)S(1)}, u32[]{:S(2)}, u32[]{:S(2)}) %all-to-all-start.1) | async-done | bytes 786464 | tf_op jit(solution)/shard_map/all_to_all | solution.py:207
  53.4 1.1 grad.1
  54.4 32.7 %all_to_all.25.parts_ref = bf16[32,24,512]{2,1,0:T(8,128)(2,1)S(1)} all-to-all(bf16[32,24,512]{2,1,0:T(8,128)(2,1)S(1)} %get-tuple-element.9), channel_id=1, replica_groups=mesh['y_lo'=2,'x'=4,'y_hi'=4,'z'=8,'core'=2] {'y_hi','z'}, dimensions={0} | all-to-all | bytes 1572864 | tf_op jit(solution)/shard_map/all_to_all | solution.py:237
  87.1 1.0 sum.1
  88.2 4.7 %all-to-all-start.3 = ((bf16[32,24,512]{2,1,0:T(8,128)(2,1)}), bf16[32,24,512]{2,1,0:T(8,128)(2,1)S(1)}, u32[]{:S(2)}, u32[]{:S(2)}) async-start(bf16[32,24,512]{2,1,0:T(8,128)(2,1)} %sum.1), calls=%async_computation.3 | async-start | bytes 1572864 | tf_op jit(solution)/shard_map/all_to_all | solution.py:246
  92.9 3.1 %collective-permute-start = (bf16[2,2,128,256]{3,2,1,0:T(8,128)(2,1)S(1)}, bf16[2,2,128,256]{3,2,1,0:T(8,128)(2,1)S(1)}, u32[]{:S(2)}, u32[]{:S(2)}) collective-permute-start(bf16[2,2,128,256]{3,2,1,0:T(8,128)(2,1)S(1)} %bitcast.33), channel_id=1, source_target_pairs={{0,2},{2,4},{4,6},{6,8},{8,10},{10,12},{12,14},{14,16},{16,18},{18... | collective-permute-start | bytes 786440 | tf_op jit(solution)/shard_map/ppermute | solution.py:251
  96.1 31.2 %collective-permute-done.c1_ref = bf16[2,2,128,256]{3,2,1,0:T(8,128)(2,1)S(1)} collective-permute-done((bf16[2,2,128,256]{3,2,1,0:T(8,128)(2,1)S(1)}, bf16[2,2,128,256]{3,2,1,0:T(8,128)(2,1)S(1)}, u32[]{:S(2)}, u32[]{:S(2)}) %collective-permute-start) | collective-permute-done | bytes 262176 | tf_op jit(solution)/shard_map/ppermute | solution.py:251
  127.3 1.9 collective-permute-start.1
  129.2 11.5 %collective-permute-done.1.c2_ref = bf16[2,2,128,256]{3,2,1,0:T(8,128)(2,1)S(1)} collective-permute-done((bf16[2,2,128,256]{3,2,1,0:T(8,128)(2,1)S(1)}, bf16[2,2,128,256]{3,2,1,0:T(8,128)(2,1)S(1)}, u32[]{:S(2)}, u32[]{:S(2)}) %collective-permute-start.1) | collective-permute-done | bytes 262176 | tf_op jit(solution)/shard_map/ppermute | solution.py:251
  140.7 1.9 collective-permute-start.2
  142.6 9.4 %collective-permute-done.2.c3_ref = bf16[2,2,128,256]{3,2,1,0:T(8,128)(2,1)S(1)} collective-permute-done((bf16[2,2,128,256]{3,2,1,0:T(8,128)(2,1)S(1)}, bf16[2,2,128,256]{3,2,1,0:T(8,128)(2,1)S(1)}, u32[]{:S(2)}, u32[]{:S(2)}) %collective-permute-start.2) | collective-permute-done | bytes 262176 | tf_op jit(solution)/shard_map/ppermute | solution.py:251
  152.0 1.9 collective-permute-start.3
  154.0 0.6 copy-done.7
  154.7 0.6 dynamic_slice.3.step_ref
  155.2 10.3 %collective-permute-done.3.c4_ref = bf16[2,2,128,256]{3,2,1,0:T(8,128)(2,1)S(1)} collective-permute-done((bf16[2,2,128,256]{3,2,1,0:T(8,128)(2,1)S(1)}, bf16[2,2,128,256]{3,2,1,0:T(8,128)(2,1)S(1)}, u32[]{:S(2)}, u32[]{:S(2)}) %collective-permute-start.3) | collective-permute-done | bytes 262176 | tf_op jit(solution)/shard_map/ppermute | solution.py:251
  165.5 1.3 window.1.base_ref
  166.8 17.2 %newton.1 = bf16[16,2,8,256]{3,2,1,0:T(8,128)(2,1)S(1)} custom-call(f32[1]{0:T(128)} %dynamic_slice.3.step_ref, bf16[32,24,512]{2,1,0:T(8,128)(2,1)S(1)} %all-to-all-done.3.total_ref, bf16[256,512]{1,0:T(8,128)(2,1)S(1)} %get-tuple-element.10.gate_ref, bf16[256,512]{1,0:T(8,128)(2,1)S(1)} %get-tuple-element.11.up_ref, ...), custom_call_target="tpu_custom_call" | custom-call | tf_op jit(solution)/shard_map/newton/pallas_call | solution.py:262
  184.0 21.3 %all_to_all.26.parts_ref = bf16[16,2,8,256]{3,2,1,0:T(8,128)(2,1)S(1)} all-to-all(bf16[16,2,8,256]{3,2,1,0:T(8,128)(2,1)S(1)} %newton.1), channel_id=1, replica_groups=mesh['y_lo'=2,'x'=4,'y_hi'=4,'z'=8,'core'=2] {'core','y_lo','x'}, dimensions={0} | all-to-all | bytes 262144 | tf_op jit(solution)/shard_map/all_to_all | solution.py:271
  205.3 0.8 norm.1
  (33 shorter events, 0.4 us)
Async XLA Ops:
  0.0 0.8 copy-start.6
  1.9 0.9 copy-start.1
  2.8 0.9 copy-start.2
  4.6 10.4 %copy-start.3 = (bf16[2,4,512]{2,1,0:T(4,128)(2,1)S(1)}, bf16[2,4,512]{2,1,0:T(4,128)(2,1)}, u32[]{:S(2)}) copy-start(bf16[2,4,512]{2,1,0:T(4,128)(2,1)} %param.15) | copy-start | bytes 24580
  4.6 11.8 %all-to-all-start = ((bf16[2,392,256]{2,1,0:T(8,128)(2,1)}), bf16[2,392,256]{2,1,0:T(8,128)(2,1)S(1)}, u32[]{:S(2)}, u32[]{:S(2)}) async-start(bf16[2,392,256]{2,1,0:T(8,128)(2,1)} %fusion.1), calls=%async_computation | async-start | bytes 802816 | tf_op jit(solution)/shard_map/all_to_all | solution.py:217
  15.1 0.7 copy-start.4
  15.8 0.7 copy-start.5
  17.4 35.9 %all-to-all-start.1 = ((bf16[64,24,256]{2,1,0:T(8,128)(2,1)}), bf16[64,24,256]{2,1,0:T(8,128)(2,1)S(1)}, u32[]{:S(2)}, u32[]{:S(2)}) async-start(bf16[64,24,256]{2,1,0:T(8,128)(2,1)} %bitcast.11), calls=%async_computation.1 | async-start | bytes 1572864 | tf_op jit(solution)/shard_map/all_to_all | solution.py:207
  88.2 78.7 %all-to-all-start.3 = ((bf16[32,24,512]{2,1,0:T(8,128)(2,1)}), bf16[32,24,512]{2,1,0:T(8,128)(2,1)S(1)}, u32[]{:S(2)}, u32[]{:S(2)}) async-start(bf16[32,24,512]{2,1,0:T(8,128)(2,1)} %sum.1), calls=%async_computation.3 | async-start | bytes 1572864 | tf_op jit(solution)/shard_map/all_to_all | solution.py:246
  92.9 34.3 %collective-permute-start = (bf16[2,2,128,256]{3,2,1,0:T(8,128)(2,1)S(1)}, bf16[2,2,128,256]{3,2,1,0:T(8,128)(2,1)S(1)}, u32[]{:S(2)}, u32[]{:S(2)}) collective-permute-start(bf16[2,2,128,256]{3,2,1,0:T(8,128)(2,1)S(1)} %bitcast.33), channel_id=1, source_target_pairs={{0,2},{2,4},{4,6},{6,8},{8,10},{10,12},{12,14},{14,16},{16,18},{18... | collective-permute-start | bytes 786440 | tf_op jit(solution)/shard_map/ppermute | solution.py:251
  127.3 13.5 %collective-permute-start.1 = (bf16[2,2,128,256]{3,2,1,0:T(8,128)(2,1)S(1)}, bf16[2,2,128,256]{3,2,1,0:T(8,128)(2,1)S(1)}, u32[]{:S(2)}, u32[]{:S(2)}) collective-permute-start(bf16[2,2,128,256]{3,2,1,0:T(8,128)(2,1)S(1)} %collective-permute-done.c1_ref), channel_id=1, source_target_pairs={{0,2},{2,4},{4,6},{6,8},{8,10},{10,12},{12,14},{14,16},{16,18},{18... | collective-permute-start | bytes 786440 | tf_op jit(solution)/shard_map/ppermute | solution.py:251
  140.7 11.3 %collective-permute-start.2 = (bf16[2,2,128,256]{3,2,1,0:T(8,128)(2,1)S(1)}, bf16[2,2,128,256]{3,2,1,0:T(8,128)(2,1)S(1)}, u32[]{:S(2)}, u32[]{:S(2)}) collective-permute-start(bf16[2,2,128,256]{3,2,1,0:T(8,128)(2,1)S(1)} %collective-permute-done.1.c2_ref), channel_id=1, source_target_pairs={{0,2},{2,4},{4,6},{6,8},{8,10},{10,12},{12,14},{14,16},{16,18},{18... | collective-permute-start | bytes 786440 | tf_op jit(solution)/shard_map/ppermute | solution.py:251
  152.0 13.5 %collective-permute-start.3 = (bf16[2,2,128,256]{3,2,1,0:T(8,128)(2,1)S(1)}, bf16[2,2,128,256]{3,2,1,0:T(8,128)(2,1)S(1)}, u32[]{:S(2)}, u32[]{:S(2)}) collective-permute-start(bf16[2,2,128,256]{3,2,1,0:T(8,128)(2,1)S(1)} %collective-permute-done.2.c3_ref), channel_id=1, source_target_pairs={{0,2},{2,4},{4,6},{6,8},{8,10},{10,12},{12,14},{14,16},{16,18},{18... | collective-permute-start | bytes 786440 | tf_op jit(solution)/shard_map/ppermute | solution.py:251
  154.0 0.7 copy-start.7
  184.0 21.3 %copy-start = (f32[4096]{0:T(1024)S(1)}, f32[4096]{0:T(1024)}, u32[]{:S(2)}) copy-start(f32[4096]{0:T(1024)} %param.17) | copy-start | bytes 49156

commit v2 on v1

v2 whole, which is shorter than its diff:
```python
import math

import jax
import jax.numpy as jnp
from jax import lax
from jax.experimental import pallas as pl
from jax.experimental.pallas import tpu as pltpu
from jax.sharding import Mesh
from jax.sharding import PartitionSpec as P

DH = 256
DF = 512
PART = 128
NS_STEPS = 5
CHIPS = 32
TOK = 128
REACH = 4
RING = ("y_hi", "z")
F32 = jnp.float32
BF = jnp.bfloat16


def matmul(left, right):
    return lax.dot_general(left, right, (((1,), (0,)), ((), ())), preferred_element_type=F32)


def matmul_nt(left, right):
    return lax.dot_general(left, right, (((1,), (1,)), ((), ())), preferred_element_type=F32)


def matmul_tn(left, right):
    return lax.dot_general(left, right, (((0,), (0,)), ((), ())), preferred_element_type=F32)


def halves(wide):
    high = wide.astype(BF)
    return high, (wide - high.astype(F32)).astype(BF)


def rms_norm(values_in):
    wide = values_in.astype(F32)
    mean_square = jnp.mean(wide * wide, axis=-1, keepdims=True)
    return (wide * lax.rsqrt(mean_square + 1e-06)).astype(BF)


def sigmoid(value):
    return 1.0 / (1.0 + jnp.exp(-value))


def fast_forward(query, gate_fast, up_fast, down_fast):
    query_norm = rms_norm(query)
    gate_query = matmul(query_norm, gate_fast)
    up_query = matmul(query_norm, up_fast)
    hidden = (gate_query * sigmoid(gate_query) * up_query).astype(BF)
    return matmul(hidden, down_fast)


def pack_kernel(
    q_ref, k_ref, v_ref, rate_ref, gate_ref, up_ref, down_ref, swap_ref, pool_ref, weight_ref
):
    for head in range(2):
        columns = slice(head * DH, (head + 1) * DH)
        for index, ref in enumerate((q_ref, k_ref, v_ref)):
            for block in range(2):
                first = (index * 2 + block) * 64
                swap_ref[head, first : first + 64, :] = ref[block, :, columns]
        rate = rate_ref[0, head : head + 1, :]
        high = rate.astype(BF).astype(F32)
        middle = (rate - high).astype(BF).astype(F32)
        low = (rate - high) - middle
        terms = jnp.concatenate([high, middle, low, jnp.zeros_like(rate)], 1)
        terms = jnp.broadcast_to(terms, (8, DH)).astype(BF)
        low_half = down_ref[head, :, :128]
        high_half = down_ref[head, :, 128:]
        for row in range(4):
            target = row * 2 + head
            pool_ref[target, 0:64, :] = k_ref[0, :, columns]
            pool_ref[target, 64:128, :] = v_ref[0, :, columns]
            pool_ref[target, 128:136, :] = terms
            part = slice(row * PART, (row + 1) * PART)
            pair = [gate_ref[head, :, part].astype(F32), up_ref[head, :, part].astype(F32)]
            pair = jnp.concatenate(pair, 0).astype(BF)
            for depth in range(8):
                target = (row * 8 + depth) * 2 + head
                weight_ref[target, 0:8, :] = pair
                weight_ref[target, 8:16, :] = low_half
                weight_ref[target, 16:24, :] = high_half


def grad_kernel(row_ref, pool_ref, raw_ref, _, grad_ref, slice_ref, down_ref):
    out_row = lax.broadcasted_iota(jnp.int32, (DH, 2 * DH), 0)
    in_row = lax.broadcasted_iota(jnp.int32, (DH, 2 * DH), 1)
    mixed = raw_ref[:, 0:8, :].astype(F32).reshape(2 * DH, PART).astype(BF)
    weights = []
    for index in range(2):
        pick = (out_row // 4) * 8 + index * 4 + out_row % 4
        chosen = jnp.where(in_row == pick, 1.0, 0.0).astype(BF)
        weights.append(matmul(chosen, mixed).astype(BF))
        for row in range(4):
            slice_ref[row, index * DH : (index + 1) * DH, :] = weights[index]
    for index in range(2):
        half = raw_ref[:, 8 + 8 * index : 16 + 8 * index, :].astype(F32)
        down_ref[:, index * 128 : (index + 1) * 128] = half.reshape(DF, 128).astype(BF)
    gate_part, up_part = weights
    down_part = down_ref[pl.ds(pl.multiple_of(row_ref[0] * PART, PART), PART), :]
    equal = lax.broadcasted_iota(jnp.int32, (64, 64), 0) == lax.broadcasted_iota(
        jnp.int32, (64, 64), 1
    )
    columns = []
    for source in range(8):
        terms = pool_ref[source, 128:136, :].astype(F32)[0:1]
        rate = terms[:, 0:64] + (terms[:, 64:128] + terms[:, 128:192])
        spread = jnp.where(equal, jnp.broadcast_to(rate, (64, 64)), 0.0)
        columns.append(jnp.sum(spread, axis=1, keepdims=True))
    rate_col = jnp.concatenate(columns, 0)
    keys_now = rms_norm(pool_ref[:, 0:64, :].reshape(4 * TOK, DH))
    vals_now = pool_ref[:, 64:128, :].reshape(4 * TOK, DH)
    gate_pre = matmul(keys_now, gate_part)
    up_pre = matmul(keys_now, up_part)
    back = matmul_nt(vals_now, down_part)
    sigmoid_val = sigmoid(gate_pre)
    act_val = gate_pre * sigmoid_val
    rate_back = rate_col * back
    d_gate = (rate_back * up_pre * sigmoid_val * (1.0 + gate_pre * (1.0 - sigmoid_val))).astype(BF)
    d_up = (rate_back * act_val).astype(BF)
    h_rate = (rate_col * act_val * up_pre).astype(BF)
    for index, (left, right) in enumerate(
        ((keys_now, d_gate), (keys_now, d_up), (vals_now, h_rate))
    ):
        grad = matmul_tn(left, right).reshape(8, 32, PART)
        grad_ref[:, index * 32 : index * 32 + 32, :] = grad.astype(BF)


def sum_kernel(parts_ref, _, __, total_ref):
    total = jnp.sum(parts_ref[...].astype(F32), axis=0, keepdims=True)
    total_ref[...] = jnp.broadcast_to(total, (8, 96, PART)).astype(BF)


def widen_kernel(piece_ref, _, total_ref):
    for row in range(4):
        total_ref[row] = piece_ref[...]


def whole_weights(slices_ref, index):
    rows = slice(index * DH, (index + 1) * DH)
    return jnp.concatenate([slices_ref[row, rows, :] for row in range(4)], 1)


def attention_kernel(
    chip_ref, own_ref, c1_ref, c2_ref, c3_ref, c4_ref, slices_ref, down_ref, out_ref
):
    chip = chip_ref[0]
    row = lax.broadcasted_iota(jnp.int32, (TOK, TOK), 0)
    column = lax.broadcasted_iota(jnp.int32, (TOK, TOK), 1)
    scale = 1.0 / math.sqrt(DH)
    chunks = (c1_ref, c2_ref, c3_ref, c4_ref)

    def rows_of(distance, index, block):
        if distance == 0:
            place = 2 + 2 * index + block
            return jnp.concatenate([own_ref[0, place], own_ref[1, place]], 0)
        behind = (chip < distance).astype(jnp.int32)
        place = 2 * index + jnp.maximum(block - behind, 0)
        chunk = chunks[distance - 1]
        return jnp.concatenate([chunk[0, place], chunk[1, place]], 0)

    for block in range(2):
        query = jnp.concatenate([own_ref[0, block], own_ref[1, block]], 0)
        scores = []
        for distance in range(REACH + 1):
            score = matmul_nt(query, rows_of(distance, 0, block)) * scale
            if distance == 0:
                score = jnp.where(row >= column, score, -1e30)
            elif distance == REACH:
                score = jnp.where(row < column, score, -1e30)
            if block == 0 and distance > 0:
                behind = (chip < distance).astype(jnp.int32)
                score = jnp.where(behind + jnp.zeros_like(row) > 0, -1e30, score)
            scores.append(score)
        top = scores[0]
        for score in scores[1:]:
            top = jnp.maximum(top, score)
        row_top = jnp.max(top, axis=-1, keepdims=True)
        exps = [jnp.exp(score - row_top) for score in scores]
        total = exps[0]
        for exp_score in exps[1:]:
            total = total + exp_score
        row_sum = jnp.sum(total, axis=-1, keepdims=True)
        result = None
        for distance in range(REACH + 1):
            weights = (exps[distance] / row_sum).astype(BF)
            part = matmul(weights, rows_of(distance, 1, block))
            result = part if result is None else result + part
        if block == 0:
            gate_fast, up_fast = whole_weights(slices_ref, 0), whole_weights(slices_ref, 1)
            result = result + fast_forward(query, gate_fast, up_fast, down_ref[...])
        out_ref[block] = result


def newton_kernel(
    step_ref, total_ref, slices_ref, down_ref, own_ref, base_ref, out_ref, iterate_ref
):
    for index in range(3):
        rows = slice(index * 32, index * 32 + 32)
        pieces = [total_ref[row, :, rows, :].astype(F32).reshape(DH, PART) for row in range(4)]
        grad = jnp.concatenate(pieces, 1)
        square = jnp.sum(jnp.sum(grad * grad, axis=0, keepdims=True), axis=1, keepdims=True)
        iterate_ref[index] = grad / (jnp.sqrt(square) + 1e-07)

    def one_step(_, carry):
        for index in range(3):
            iterate = iterate_ref[index]
            high, low = halves(iterate)
            gram = matmul_nt(high, high) + (matmul_nt(high, low) + matmul_nt(low, high))
            gram_high, gram_low = halves(gram)
            square = matmul(gram_high, gram_high) + (
                matmul(gram_high, gram_low) + matmul(gram_low, gram_high)
            )
            poly_high, poly_low = halves(-4.775 * gram + 2.0315 * square)
            iterate_ref[index] = 3.4445 * iterate + (
                matmul(poly_high, high) + (matmul(poly_high, low) + matmul(poly_low, high))
            )
        return carry

    lax.fori_loop(0, NS_STEPS, one_step, 0)
    step = step_ref[0]
    gate_fast = (whole_weights(slices_ref, 0).astype(F32) + step * iterate_ref[0]).astype(BF)
    up_fast = (whole_weights(slices_ref, 1).astype(F32) + step * iterate_ref[1]).astype(BF)
    down_fast = (down_ref[...].astype(F32) + step * iterate_ref[2].T).astype(BF)
    query = jnp.concatenate([own_ref[0, 1], own_ref[1, 1]], 0)
    fast = fast_forward(query, gate_fast, up_fast, down_fast)
    out_ref[:, 0] = base_ref[0].reshape(16, 8, DH).astype(BF)
    out_ref[:, 1] = (fast + base_ref[1]).reshape(16, 8, DH).astype(BF)


def norm_kernel(parts_ref, gain_ref, out_ref):
    square = None
    for source in range(16):
        wide = parts_ref[source].astype(F32)
        part = jnp.sum(wide * wide, axis=-1, keepdims=True)
        square = part if square is None else square + part
    scale = lax.rsqrt(square * (1.0 / (16 * DH)) + 1e-06)
    for source in range(16):
        head = 2 * (source % 8) + source // 8
        columns = slice(head * DH, (head + 1) * DH)
        wide = parts_ref[source].astype(F32) * scale * gain_ref[:, columns][None]
        out_ref[:, :, columns] = wide.astype(BF)


PARAMS = pltpu.CompilerParams(vmem_limit_bytes=16 * 1024 * 1024)
VMEM = pl.BlockSpec(memory_space=pltpu.VMEM)
ANY = pl.BlockSpec(memory_space=pl.ANY)
SMEM = pl.BlockSpec(memory_space=pltpu.SMEM)


def shape_of(shape, dtype=BF):
    return jax.ShapeDtypeStruct(shape, dtype)


def body(queries, keys, values, token_rates, step_size, w_gate, w_up, w_down, norm_gain):
    core = lax.axis_index("core")
    chip = lax.axis_index(RING).astype(jnp.int32).reshape(1)
    line = lax.axis_index("y_hi").astype(jnp.int32).reshape(1)
    swap, pool, raw = pl.pallas_call(
        pack_kernel,
        out_shape=(shape_of((2, 384, DH)), shape_of((8, 136, DH)), shape_of((64, 24, 128))),
        in_specs=[VMEM] * 7,
        out_specs=(VMEM,) * 3,
        compiler_params=PARAMS,
        name="pack",
    )(queries, keys, values, token_rates, w_gate, w_up, w_down)
    raw = lax.all_to_all(raw, RING + ("core",), 0, 0, tiled=True)
    pool = lax.all_to_all(pool, ("y_hi", "core"), 0, 0, tiled=True)
    own = lax.all_to_all(swap, "core", 0, 0, tiled=True)

    ring = [(i, (i + 1) % CHIPS) for i in range(CHIPS)]
    chunks = [lax.ppermute(own[:, 128:], RING, ring)]

    grad, slices, down_fast = pl.pallas_call(
        grad_kernel,
        out_shape=(shape_of((8, 96, PART)), shape_of((4, 2 * DH, PART)), shape_of((DF, DH))),
        in_specs=[SMEM] + [VMEM] * 2 + [ANY],
        out_specs=(VMEM,) * 3,
        compiler_params=PARAMS,
        name="grad",
    )(line, pool, raw, chunks[0])
    chunks.append(lax.ppermute(chunks[-1], RING, ring))
    parts = lax.all_to_all(grad, "z", 0, 0, tiled=True)
    slices = lax.all_to_all(slices, "y_hi", 0, 0, tiled=True)
    total = pl.pallas_call(
        sum_kernel,
        out_shape=shape_of((8, 96, PART)),
        in_specs=[VMEM, ANY, ANY],
        out_specs=VMEM,
        compiler_params=PARAMS,
        name="sum",
    )(parts, chunks[1], slices)
    chunks.append(lax.ppermute(chunks[-1], RING, ring))
    total = lax.all_to_all(total, "z", 0, 0, tiled=True)
    total = pl.pallas_call(
        widen_kernel,
        out_shape=shape_of((4, 8, 96, PART)),
        in_specs=[VMEM, ANY],
        out_specs=VMEM,
        compiler_params=PARAMS,
        name="widen",
    )(total, chunks[2])
    chunks.append(lax.ppermute(chunks[-1], RING, ring))
    total = lax.all_to_all(total, "y_hi", 0, 0, tiled=True)

    own = own.reshape(2, 6, 64, DH)
    chunks = [chunk.reshape(2, 4, 64, DH) for chunk in chunks]
    base = pl.pallas_call(
        attention_kernel,
        out_shape=shape_of((2, TOK, DH), F32),
        in_specs=[SMEM] + [VMEM] * 7,
        out_specs=VMEM,
        compiler_params=PARAMS,
        name="window",
    )(chip, own, *chunks, slices, down_fast)

    step = lax.dynamic_slice_in_dim(step_size, core, 1, 0)
    combined = pl.pallas_call(
        newton_kernel,
        out_shape=shape_of((16, 2, 8, DH)),
        in_specs=[SMEM] + [VMEM] * 5,
        out_specs=VMEM,
        scratch_shapes=[pltpu.VMEM((3, DH, DF), F32)],
        compiler_params=PARAMS,
        name="newton",
    )(step, total, slices, down_fast, own, base)
    gathered = lax.all_to_all(combined, ("core", "y_lo", "x"), 0, 0, tiled=True)
    return pl.pallas_call(
        norm_kernel,
        out_shape=jax.ShapeDtypeStruct((2, 8, 16 * DH), BF),
        in_specs=[VMEM] * 2,
        out_specs=VMEM,
        compiler_params=PARAMS,
        name="norm",
    )(gathered, norm_gain.reshape(1, 16 * DH))


def solution(mesh):
    fine = Mesh(mesh.devices.reshape(2, 4, 4, 8, 2), ("y_lo", "x", "y_hi", "z", "core"))
    seq = RING + ("core",)
    head = ("y_lo", "x")
    placed = (
        P(None, seq, head),
        P(None, seq, head),
        P(None, seq, head),
        P(None, head, seq),
        P(head),
        P(head, seq, None),
        P(head, seq, None),
        P(head, seq, None),
        P(),
    )
    return jax.shard_map(
        body, mesh=fine, in_specs=placed, out_specs=P(None, seq + head, None), check_vma=False
    )
```

time: 207 us -> 201 us (0.971)
  blocking collectives: 54 us -> 80.9 us
  waiting for transfers between devices: 87 us -> 63.7 us
  starting transfers between devices: 35.1 us -> 25.9 us
    ppermute x0 -> x1, waiting for transfers between devices: none -> 24.9 us  [body(): chunks = [lax.ppermute(own[:, 128:], RING, ring)]]
    all_to_all x3 -> x4, waiting for transfers between devices: 24.6 us -> 0.01 us  [the longest x1 0.01 us: body(): slices = lax.all_to_all(slices, 'y_hi', 0, 0, tiled=True)]
    ppermute x4 -> x3, waiting for transfers between devices: 62.4 us -> 38.8 us  [body(): chunks.append(lax.ppermute(chunks[-1], RING, ring))]
    all_to_all x1 -> x3, blocking collectives: 32.7 us -> 49.1 us  [the longest x1 26.9 us: body(): raw = lax.all_to_all(raw, RING + ('core',), 0, 0, tiled=True)]
    all_to_all x1, blocking collectives: 21.3 us -> 31.8 us  [body(): gathered = lax.all_to_all(combined, ('core', 'y_lo', 'x'), 0, 0, tiled=True)]
    all_to_all x3 -> x4, starting transfers between devices: 26.2 us -> 16 us  [the longest x1 5.66 us: body(): pool = lax.all_to_all(pool, ('y_hi', 'core'), 0, 0, tiled=True)]
    ppermute x0 -> x1, starting transfers between devices: none -> 2.64 us  [body(): chunks = [lax.ppermute(own[:, 128:], RING, ring)]]
    unnamed x17 -> x18, local copies, waits for them, and re-layouts: 3.79 us -> 6.14 us
  transfers between devices with their start and end apart: 7 -> 8, of which waited for: 5 -> 4; matrix products, arithmetic and copies ran while one was open for 0% -> 0% of each run, Pallas kernels for 1% -> 1%
where the time goes in v2:
time: 201 us
  blocking collectives  80.9 us (40%)
  waiting for transfers between devices  63.7 us (32%)
  starting transfers between devices  25.9 us (13%)
  Pallas kernels  23.2 us (12%)
  local copies, waits for them, and re-layouts  6.74 us (3%)
    ppermute x3, waiting for transfers between devices, body(): chunks.append(lax.ppermute(chunks[-1], RING, ring))  38.8 us
    all_to_all x1, blocking collectives, body(): gathered = lax.all_to_all(combined, ('core', 'y_lo', 'x'), 0, 0, tiled=True)  31.8 us
    all_to_all x1, blocking collectives, body(): raw = lax.all_to_all(raw, RING + ('core',), 0, 0, tiled=True)  26.9 us
    ppermute x1, waiting for transfers between devices, body(): chunks = [lax.ppermute(own[:, 128:], RING, ring)]  24.9 us
    pallas_call x1, Pallas kernels, body(): pl.pallas_call(newton_kernel, out_shape=shape_of((16, 2, 8, DH)), in_spec...  17.3 us
    all_to_all x1, blocking collectives, body(): parts = lax.all_to_all(grad, 'z', 0, 0, tiled=True)  11.6 us
    all_to_all x1, blocking collectives, body(): own = lax.all_to_all(swap, 'core', 0, 0, tiled=True)  10.5 us
    ppermute x3, starting transfers between devices, body(): chunks.append(lax.ppermute(chunks[-1], RING, ring))  7.25 us
  transfers between devices with their start and end apart: 8, of which 4 were waited for; matrix products, arithmetic and copies ran while one was open for 0% of the time, Pallas kernels for 1%

profile of v2, /device:TPU:1, one launch (start us, length us, event | category | flops | bytes accessed | tf_op | source)
XLA Modules:
  0.0 200.5 jit_solution(14836163578732673773)
XLA Ops:
  0.0 0.9 copy-done
  0.9 0.9 copy-done.1
  1.8 0.9 copy-done.2
  2.7 0.7 copy-done.4
  3.4 0.7 copy-done.5
  4.1 0.7 copy-done.6
  4.8 0.7 copy-done.7
  5.5 0.9 pack.1
  6.4 10.5 %all_to_all.40 = bf16[2,384,256]{2,1,0:T(8,128)(2,1)S(1)} all-to-all(bf16[2,384,256]{2,1,0:T(8,128)(2,1)S(1)} %get-tuple-element.13), channel_id=1, replica_groups=mesh['y_lo'=2,'x'=4,'y_hi'=4,'z'=8,'core'=2] {'core'}, dimensions={0} | all-to-all | bytes 786432 | tf_op jit(solution)/shard_map/all_to_all | solution.py:274
  16.9 26.9 %all_to_all.41.raw_ref = bf16[64,24,128]{2,1,0:T(8,128)(2,1)S(1)} all-to-all(bf16[64,24,128]{2,1,0:T(8,128)(2,1)S(1)} %get-tuple-element.12), channel_id=1, replica_groups=mesh['y_lo'=2,'x'=4,'y_hi'=4,'z'=8,'core'=2] {'y_hi','z','core'}, dimensions={0} | all-to-all | bytes 786432 | tf_op jit(solution)/shard_map/all_to_all | solution.py:272
  43.8 5.7 %all-to-all-start = ((bf16[8,136,256]{2,1,0:T(8,128)(2,1)}), bf16[8,136,256]{2,1,0:T(8,128)(2,1)S(1)}, u32[]{:S(2)}, u32[]{:S(2)}) async-start(bf16[8,136,256]{2,1,0:T(8,128)(2,1)} %get-tuple-element.11), calls=%async_computation | async-start | bytes 1114112 | tf_op jit(solution)/shard_map/all_to_all | solution.py:273
  49.5 2.6 %collective-permute-start = (bf16[2,256,256]{2,1,0:T(8,128)(2,1)S(1)}, bf16[2,256,256]{2,1,0:T(8,128)(2,1)S(1)}, u32[]{:S(2)}, u32[]{:S(2)}) collective-permute-start(bf16[2,256,256]{2,1,0:T(8,128)(2,1)S(1)} %slice.4), channel_id=1, source_target_pairs={{0,2},{2,4},{4,6},{6,8},{8,10},{10,12},{12,14},{14,16},{16,18},{18... | collective-permute-start | bytes 786440 | tf_op jit(solution)/shard_map/ppermute | solution.py:277
  52.2 24.9 %collective-permute-done._ = bf16[2,256,256]{2,1,0:T(8,128)(2,1)S(1)} collective-permute-done((bf16[2,256,256]{2,1,0:T(8,128)(2,1)S(1)}, bf16[2,256,256]{2,1,0:T(8,128)(2,1)S(1)}, u32[]{:S(2)}, u32[]{:S(2)}) %collective-permute-start) | collective-permute-done | bytes 262176 | tf_op jit(solution)/shard_map/ppermute | solution.py:277
  77.1 1.2 grad.1
  78.3 11.6 %all_to_all.42.parts_ref = bf16[8,96,128]{2,1,0:T(8,128)(2,1)S(1)} all-to-all(bf16[8,96,128]{2,1,0:T(8,128)(2,1)S(1)} %get-tuple-element.14), channel_id=1, replica_groups=mesh['y_lo'=2,'x'=4,'y_hi'=4,'z'=8,'core'=2] {'z'}, dimensions={0} | all-to-all | bytes 393216 | tf_op jit(solution)/shard_map/all_to_all | solution.py:288
  89.9 3.5 %all-to-all-start.4 = ((bf16[4,512,128]{2,1,0:T(8,128)(2,1)}), bf16[4,512,128]{2,1,0:T(8,128)(2,1)S(1)}, u32[]{:S(2)}, u32[]{:S(2)}) async-start(bf16[4,512,128]{2,1,0:T(8,128)(2,1)} %get-tuple-element.15), calls=%async_computation.4 | async-start | bytes 1048576 | tf_op jit(solution)/shard_map/all_to_all | solution.py:289
  93.4 1.9 collective-permute-start.1
  95.4 14.6 %collective-permute-done.1._ = bf16[2,256,256]{2,1,0:T(8,128)(2,1)S(1)} collective-permute-done((bf16[2,256,256]{2,1,0:T(8,128)(2,1)S(1)}, bf16[2,256,256]{2,1,0:T(8,128)(2,1)S(1)}, u32[]{:S(2)}, u32[]{:S(2)}) %collective-permute-start.1) | collective-permute-done | bytes 262176 | tf_op jit(solution)/shard_map/ppermute | solution.py:287
  109.9 0.7 sum.1
  110.7 3.4 %all-to-all-start.5 = ((bf16[8,96,128]{2,1,0:T(8,128)(2,1)}), bf16[8,96,128]{2,1,0:T(8,128)(2,1)S(1)}, u32[]{:S(2)}, u32[]{:S(2)}) async-start(bf16[8,96,128]{2,1,0:T(8,128)(2,1)} %sum.1), calls=%async_computation.5 | async-start | bytes 393216 | tf_op jit(solution)/shard_map/all_to_all | solution.py:299
  114.1 3.3 %collective-permute-start.2 = (bf16[2,256,256]{2,1,0:T(8,128)(2,1)S(1)}, bf16[2,256,256]{2,1,0:T(8,128)(2,1)S(1)}, u32[]{:S(2)}, u32[]{:S(2)}) collective-permute-start(bf16[2,256,256]{2,1,0:T(8,128)(2,1)S(1)} %collective-permute-done.1._), channel_id=1, source_target_pairs={{0,2},{2,4},{4,6},{6,8},{8,10},{10,12},{12,14},{14,16},{16,18},{18... | collective-permute-start | bytes 786440 | tf_op jit(solution)/shard_map/ppermute | solution.py:298
  117.3 9.0 %collective-permute-done.2._ = bf16[2,256,256]{2,1,0:T(8,128)(2,1)S(1)} collective-permute-done((bf16[2,256,256]{2,1,0:T(8,128)(2,1)S(1)}, bf16[2,256,256]{2,1,0:T(8,128)(2,1)S(1)}, u32[]{:S(2)}, u32[]{:S(2)}) %collective-permute-start.2) | collective-permute-done | bytes 262176 | tf_op jit(solution)/shard_map/ppermute | solution.py:298
  126.3 1.0 widen.1
  127.3 3.5 %all-to-all-start.6 = ((bf16[4,8,96,128]{3,2,1,0:T(8,128)(2,1)}), bf16[4,8,96,128]{3,2,1,0:T(8,128)(2,1)S(1)}, u32[]{:S(2)}, u32[]{:S(2)}) async-start(bf16[4,8,96,128]{3,2,1,0:T(8,128)(2,1)} %widen.1), calls=%async_computation.6 | async-start | bytes 1572864 | tf_op jit(solution)/shard_map/all_to_all | solution.py:309
  130.8 2.1 %collective-permute-start.3 = (bf16[2,256,256]{2,1,0:T(8,128)(2,1)S(1)}, bf16[2,256,256]{2,1,0:T(8,128)(2,1)S(1)}, u32[]{:S(2)}, u32[]{:S(2)}) collective-permute-start(bf16[2,256,256]{2,1,0:T(8,128)(2,1)S(1)} %collective-permute-done.2._), channel_id=1, source_target_pairs={{0,2},{2,4},{4,6},{6,8},{8,10},{10,12},{12,14},{14,16},{16,18},{18... | collective-permute-start | bytes 786440 | tf_op jit(solution)/shard_map/ppermute | solution.py:308
  132.9 0.6 copy-done.8
  133.5 0.6 dynamic_slice.3.step_ref
  134.1 15.2 %collective-permute-done.3 = bf16[2,256,256]{2,1,0:T(8,128)(2,1)S(1)} collective-permute-done((bf16[2,256,256]{2,1,0:T(8,128)(2,1)S(1)}, bf16[2,256,256]{2,1,0:T(8,128)(2,1)S(1)}, u32[]{:S(2)}, u32[]{:S(2)}) %collective-permute-start.3) | collective-permute-done | bytes 262176 | tf_op jit(solution)/shard_map/ppermute | solution.py:308
  149.3 1.3 window.1.base_ref
  150.6 17.3 %newton.1 = bf16[16,2,8,256]{3,2,1,0:T(8,128)(2,1)S(1)} custom-call(f32[1]{0:T(128)} %dynamic_slice.3.step_ref, bf16[4,8,96,128]{3,2,1,0:T(8,128)(2,1)S(1)} %all-to-all-done.6.total_ref, bf16[4,512,128]{2,1,0:T(8,128)(2,1)S(1)} %all-to-all-done.4.__.slices_ref, bf16[512,256]{1,0:T(8,128)(2,1)S(1)} %get-tuple-element.16.down_ref, ...), custom_call_target="tpu_custom_call" | custom-call | tf_op jit(solution)/shard_map/newton/pallas_call | solution.py:323
  167.9 31.8 %all_to_all.43.parts_ref = bf16[16,2,8,256]{3,2,1,0:T(8,128)(2,1)S(1)} all-to-all(bf16[16,2,8,256]{3,2,1,0:T(8,128)(2,1)S(1)} %newton.1), channel_id=1, replica_groups=mesh['y_lo'=2,'x'=4,'y_hi'=4,'z'=8,'core'=2] {'core','y_lo','x'}, dimensions={0} | all-to-all | bytes 262144 | tf_op jit(solution)/shard_map/all_to_all | solution.py:332
  199.8 0.8 norm.1
  (15 shorter events, 0.0 us)
Async XLA Ops:
  0.0 0.9 copy-start
  0.9 0.9 copy-start.1
  1.8 0.9 copy-start.2
  2.7 0.7 copy-start.4
  3.4 0.7 copy-start.5
  4.1 0.7 copy-start.6
  4.8 0.7 copy-start.7
  43.8 33.3 %all-to-all-start = ((bf16[8,136,256]{2,1,0:T(8,128)(2,1)}), bf16[8,136,256]{2,1,0:T(8,128)(2,1)S(1)}, u32[]{:S(2)}, u32[]{:S(2)}) async-start(bf16[8,136,256]{2,1,0:T(8,128)(2,1)} %get-tuple-element.11), calls=%async_computation | async-start | bytes 1114112 | tf_op jit(solution)/shard_map/all_to_all | solution.py:273
  49.5 27.6 %collective-permute-start = (bf16[2,256,256]{2,1,0:T(8,128)(2,1)S(1)}, bf16[2,256,256]{2,1,0:T(8,128)(2,1)S(1)}, u32[]{:S(2)}, u32[]{:S(2)}) collective-permute-start(bf16[2,256,256]{2,1,0:T(8,128)(2,1)S(1)} %slice.4), channel_id=1, source_target_pairs={{0,2},{2,4},{4,6},{6,8},{8,10},{10,12},{12,14},{14,16},{16,18},{18... | collective-permute-start | bytes 786440 | tf_op jit(solution)/shard_map/ppermute | solution.py:277
  89.9 20.0 %all-to-all-start.4 = ((bf16[4,512,128]{2,1,0:T(8,128)(2,1)}), bf16[4,512,128]{2,1,0:T(8,128)(2,1)S(1)}, u32[]{:S(2)}, u32[]{:S(2)}) async-start(bf16[4,512,128]{2,1,0:T(8,128)(2,1)} %get-tuple-element.15), calls=%async_computation.4 | async-start | bytes 1048576 | tf_op jit(solution)/shard_map/all_to_all | solution.py:289
  93.4 16.5 %collective-permute-start.1 = (bf16[2,256,256]{2,1,0:T(8,128)(2,1)S(1)}, bf16[2,256,256]{2,1,0:T(8,128)(2,1)S(1)}, u32[]{:S(2)}, u32[]{:S(2)}) collective-permute-start(bf16[2,256,256]{2,1,0:T(8,128)(2,1)S(1)} %collective-permute-done._), channel_id=1, source_target_pairs={{0,2},{2,4},{4,6},{6,8},{8,10},{10,12},{12,14},{14,16},{16,18},{18... | collective-permute-start | bytes 786440 | tf_op jit(solution)/shard_map/ppermute | solution.py:287
  110.7 15.7 %all-to-all-start.5 = ((bf16[8,96,128]{2,1,0:T(8,128)(2,1)}), bf16[8,96,128]{2,1,0:T(8,128)(2,1)S(1)}, u32[]{:S(2)}, u32[]{:S(2)}) async-start(bf16[8,96,128]{2,1,0:T(8,128)(2,1)} %sum.1), calls=%async_computation.5 | async-start | bytes 393216 | tf_op jit(solution)/shard_map/all_to_all | solution.py:299
  114.1 12.3 %collective-permute-start.2 = (bf16[2,256,256]{2,1,0:T(8,128)(2,1)S(1)}, bf16[2,256,256]{2,1,0:T(8,128)(2,1)S(1)}, u32[]{:S(2)}, u32[]{:S(2)}) collective-permute-start(bf16[2,256,256]{2,1,0:T(8,128)(2,1)S(1)} %collective-permute-done.1._), channel_id=1, source_target_pairs={{0,2},{2,4},{4,6},{6,8},{8,10},{10,12},{12,14},{14,16},{16,18},{18... | collective-permute-start | bytes 786440 | tf_op jit(solution)/shard_map/ppermute | solution.py:298
  127.3 23.3 %all-to-all-start.6 = ((bf16[4,8,96,128]{3,2,1,0:T(8,128)(2,1)}), bf16[4,8,96,128]{3,2,1,0:T(8,128)(2,1)S(1)}, u32[]{:S(2)}, u32[]{:S(2)}) async-start(bf16[4,8,96,128]{3,2,1,0:T(8,128)(2,1)} %widen.1), calls=%async_computation.6 | async-start | bytes 1572864 | tf_op jit(solution)/shard_map/all_to_all | solution.py:309
  130.8 18.5 %collective-permute-start.3 = (bf16[2,256,256]{2,1,0:T(8,128)(2,1)S(1)}, bf16[2,256,256]{2,1,0:T(8,128)(2,1)S(1)}, u32[]{:S(2)}, u32[]{:S(2)}) collective-permute-start(bf16[2,256,256]{2,1,0:T(8,128)(2,1)S(1)} %collective-permute-done.2._), channel_id=1, source_target_pairs={{0,2},{2,4},{4,6},{6,8},{8,10},{10,12},{12,14},{14,16},{16,18},{18... | collective-permute-start | bytes 786440 | tf_op jit(solution)/shard_map/ppermute | solution.py:308
  132.9 0.7 copy-start.8
  167.9 31.9 %copy-start.3 = (f32[4096]{0:T(1024)S(1)}, f32[4096]{0:T(1024)}, u32[]{:S(2)}) copy-start(f32[4096]{0:T(1024)} %param.17) | copy-start | bytes 49156

commit v3 on v2

v3 whole, which is shorter than its diff:
```python
import math

import jax
import jax.numpy as jnp
from jax import lax
from jax.experimental import pallas as pl
from jax.experimental.pallas import tpu as pltpu
from jax.sharding import Mesh
from jax.sharding import PartitionSpec as P

DH = 256
DF = 512
PART = 128
NS_STEPS = 5
CHIPS = 32
TOK = 128
REACH = 4
RING = ("y_hi", "z")
F32 = jnp.float32
BF = jnp.bfloat16


def matmul(left, right):
    return lax.dot_general(left, right, (((1,), (0,)), ((), ())), preferred_element_type=F32)


def matmul_nt(left, right):
    return lax.dot_general(left, right, (((1,), (1,)), ((), ())), preferred_element_type=F32)


def matmul_tn(left, right):
    return lax.dot_general(left, right, (((0,), (0,)), ((), ())), preferred_element_type=F32)


def halves(wide):
    high = wide.astype(BF)
    return high, (wide - high.astype(F32)).astype(BF)


def rms_norm(values_in):
    wide = values_in.astype(F32)
    mean_square = jnp.mean(wide * wide, axis=-1, keepdims=True)
    return (wide * lax.rsqrt(mean_square + 1e-06)).astype(BF)


def sigmoid(value):
    return 1.0 / (1.0 + jnp.exp(-value))


def fast_forward(query, gate_fast, up_fast, down_fast):
    query_norm = rms_norm(query)
    gate_query = matmul(query_norm, gate_fast)
    up_query = matmul(query_norm, up_fast)
    hidden = (gate_query * sigmoid(gate_query) * up_query).astype(BF)
    return matmul(hidden, down_fast)


def pack_kernel(
    core_ref, q_in, k_in, v_in, rate_in, gate_in, up_in, down_in, mine_ref, other_ref, *scratch
):
    sources = (q_in, k_in, v_in, rate_in, gate_in, up_in, down_in)
    q_ref, k_ref, v_ref, rate_ref, gate_ref, up_ref, down_ref = scratch[:7]
    semaphores = scratch[7]
    copies = [
        pltpu.make_async_copy(source, target, semaphores.at[index])
        for index, (source, target) in enumerate(zip(sources, scratch[:7]))
    ]
    for copy in copies:
        copy.start()
    for copy in copies:
        copy.wait()

    def fill(target, head):
        columns = slice(head * DH, (head + 1) * DH)
        for index, ref in enumerate((q_ref, k_ref, v_ref)):
            for block in range(2):
                first = (index * 2 + block) * 64
                target[first : first + 64, :] = ref[block, :, columns]
        for index, ref in enumerate((gate_ref, up_ref)):
            wide = ref[head].astype(F32)
            pair = jnp.concatenate([wide[:, :DH], wide[:, DH:]], 0)
            target[384 + 8 * index : 392 + 8 * index, :] = pair.astype(BF)
        target[400:408, :] = down_ref[head]
        rate = rate_ref[0, head : head + 1, :]
        high = rate.astype(BF).astype(F32)
        middle = (rate - high).astype(BF).astype(F32)
        low = (rate - high) - middle
        terms = jnp.concatenate([high, middle, low, jnp.zeros_like(rate)], 1)
        target[408:416, :] = jnp.broadcast_to(terms, (8, DH)).astype(BF)

    for head in range(2):

        @pl.when(core_ref[0] == head)
        def _():
            fill(mine_ref, head)
            fill(other_ref, 1 - head)


def arrange_kernel(core_ref, mine_ref, arrived_ref, own_ref, context_ref, pool_ref, weight_ref):
    own_ref[core_ref[0]] = mine_ref[...]
    own_ref[1 - core_ref[0]] = arrived_ref[...]
    for source in range(2):
        context_ref[source] = own_ref[source, 128:384, :]
        for index in range(2):
            first = 128 * index + 64 * source
            rows = slice(128 * (index + 1), 128 * (index + 1) + 64)
            pool_ref[first : first + 64, :] = own_ref[source, rows, :]
        pool_ref[256 + 8 * source : 264 + 8 * source, :] = own_ref[source, 408:416, :]
    for row in range(4):
        lanes = slice(row % 2 * PART, (row % 2 + 1) * PART)
        pieces = []
        for index in range(2):
            first = 384 + 8 * index
            both = [own_ref[src, first : first + 8, lanes].astype(F32) for src in range(2)]
            rows = slice(row // 2 * 4, row // 2 * 4 + 4)
            pieces += [one[rows] for one in both]
        piece = jnp.concatenate(pieces, 0).astype(BF)
        down = jnp.concatenate([own_ref[src, 400:408, :].astype(F32) for src in range(2)], 0)
        down = down.astype(BF)
        for depth in range(8):
            weight_ref[row * 8 + depth, 0:16, :] = piece
            weight_ref[row * 8 + depth, 16:32, :] = down[:, :128]
            weight_ref[row * 8 + depth, 32:48, :] = down[:, 128:]


def grad_kernel(row_ref, p0_ref, p1_ref, p2_ref, p3_ref, raw_ref, grad_ref, slice_ref, down_ref):
    pools = (p0_ref, p1_ref, p2_ref, p3_ref)
    weights = []
    for index in range(2):
        piece = raw_ref[:, 8 * index : 8 * index + 8, :].astype(F32)
        weights.append(piece.reshape(DH, PART).astype(BF))
        slice_ref[index * DH : (index + 1) * DH, :] = weights[index]
        half = raw_ref[:, 16 + 16 * index : 32 + 16 * index, :]
        down_ref[:, index * 128 : (index + 1) * 128] = half.reshape(DF, 128)
    gate_part, up_part = weights
    down_part = down_ref[pl.ds(pl.multiple_of(row_ref[0] * PART, PART), PART), :]
    equal = lax.broadcasted_iota(jnp.int32, (64, 64), 0) == lax.broadcasted_iota(
        jnp.int32, (64, 64), 1
    )
    columns = []
    for pool in pools:
        for source in range(2):
            terms = pool[256 + 8 * source : 264 + 8 * source, :].astype(F32)[0:1]
            rate = terms[:, 0:64] + (terms[:, 64:128] + terms[:, 128:192])
            spread = jnp.where(equal, jnp.broadcast_to(rate, (64, 64)), 0.0)
            columns.append(jnp.sum(spread, axis=1, keepdims=True))
    rate_col = jnp.concatenate(columns, 0)
    keys_now = rms_norm(jnp.concatenate([pool[0:128, :] for pool in pools], 0))
    vals_now = jnp.concatenate([pool[128:256, :] for pool in pools], 0)
    gate_pre = matmul(keys_now, gate_part)
    up_pre = matmul(keys_now, up_part)
    back = matmul_nt(vals_now, down_part)
    sigmoid_val = sigmoid(gate_pre)
    act_val = gate_pre * sigmoid_val
    rate_back = rate_col * back
    d_gate = (rate_back * up_pre * sigmoid_val * (1.0 + gate_pre * (1.0 - sigmoid_val))).astype(BF)
    d_up = (rate_back * act_val).astype(BF)
    h_rate = (rate_col * act_val * up_pre).astype(BF)
    for index, (left, right) in enumerate(
        ((keys_now, d_gate), (keys_now, d_up), (vals_now, h_rate))
    ):
        grad = matmul_tn(left, right).reshape(8, 32, PART)
        grad_ref[:, index * 32 : index * 32 + 32, :] = grad.astype(BF)


def sum_kernel(parts_ref, _, total_ref):
    total = jnp.sum(parts_ref[...].astype(F32), axis=0, keepdims=True)
    total_ref[...] = jnp.broadcast_to(total, (8, 96, PART)).astype(BF)


def widen_kernel(row_ref, piece_ref, f0_ref, f1_ref, f2_ref, f3_ref, _, total_ref, slices_ref):
    for row in range(4):
        total_ref[row] = piece_ref[...]
    for distance, ref in enumerate((f0_ref, f1_ref, f2_ref, f3_ref)):
        slices_ref[lax.rem(row_ref[0] + 4 - distance, 4)] = ref[...]


def whole_weights(slices_ref, index):
    rows = slice(index * DH, (index + 1) * DH)
    return jnp.concatenate([slices_ref[row, rows, :] for row in range(4)], 1)


def attention_kernel(
    chip_ref, own_ref, c1_ref, c2_ref, c3_ref, c4_ref, slices_ref, down_ref, fast_ref, out_ref
):
    chip = chip_ref[0]
    row = lax.broadcasted_iota(jnp.int32, (TOK, TOK), 0)
    column = lax.broadcasted_iota(jnp.int32, (TOK, TOK), 1)
    scale = 1.0 / math.sqrt(DH)
    chunks = (c1_ref, c2_ref, c3_ref, c4_ref)

    def rows_of(distance, index, block):
        if distance == 0:
            first = (2 + 2 * index + block) * 64
            return jnp.concatenate([own_ref[src, first : first + 64, :] for src in range(2)], 0)
        behind = (chip < distance).astype(jnp.int32)
        place = 2 * index + jnp.maximum(block - behind, 0)
        chunk = chunks[distance - 1]
        return jnp.concatenate([chunk[0, place], chunk[1, place]], 0)

    for block in range(2):
        rows = slice(block * 64, block * 64 + 64)
        query = jnp.concatenate([own_ref[0, rows, :], own_ref[1, rows, :]], 0)
        scores = []
        for distance in range(REACH + 1):
            score = matmul_nt(query, rows_of(distance, 0, block)) * scale
            if distance == 0:
                score = jnp.where(row >= column, score, -1e30)
            elif distance == REACH:
                score = jnp.where(row < column, score, -1e30)
            if block == 0 and distance > 0:
                behind = (chip < distance).astype(jnp.int32)
                score = jnp.where(behind + jnp.zeros_like(row) > 0, -1e30, score)
            scores.append(score)
        top = scores[0]
        for score in scores[1:]:
            top = jnp.maximum(top, score)
        row_top = jnp.max(top, axis=-1, keepdims=True)
        exps = [jnp.exp(score - row_top) for score in scores]
        total = exps[0]
        for exp_score in exps[1:]:
            total = total + exp_score
        row_sum = jnp.sum(total, axis=-1, keepdims=True)
        result = None
        for distance in range(REACH + 1):
            weights = (exps[distance] / row_sum).astype(BF)
            part = matmul(weights, rows_of(distance, 1, block))
            result = part if result is None else result + part
        if block == 0:
            gate_fast, up_fast = whole_weights(slices_ref, 0), whole_weights(slices_ref, 1)
            result = result + fast_forward(query, gate_fast, up_fast, down_ref[...])
        else:
            result = result + fast_ref[...]
        out_ref[:, block] = result.reshape(16, 8, DH).astype(BF)


def newton_kernel(step_ref, total_ref, slices_ref, down_ref, own_ref, _, fast_ref, iterate_ref):
    for index in range(3):
        rows = slice(index * 32, index * 32 + 32)
        pieces = [total_ref[row, :, rows, :].astype(F32).reshape(DH, PART) for row in range(4)]
        grad = jnp.concatenate(pieces, 1)
        square = jnp.sum(jnp.sum(grad * grad, axis=0, keepdims=True), axis=1, keepdims=True)
        iterate_ref[index] = grad / (jnp.sqrt(square) + 1e-07)

    def coarse_step(_, carry):
        for index in range(3):
            iterate = iterate_ref[index]
            high = iterate.astype(BF)
            gram = matmul_nt(high, high)
            gram_high = gram.astype(BF)
            poly = -4.775 * gram + 2.0315 * matmul(gram_high, gram_high)
            iterate_ref[index] = 3.4445 * iterate + matmul(poly.astype(BF), high)
        return carry

    def fine_step(_, carry):
        for index in range(3):
            iterate = iterate_ref[index]
            high, low = halves(iterate)
            left = jnp.concatenate([high, high, low], 1)
            gram = matmul_nt(left, jnp.concatenate([high, low, high], 1))
            gram_high, gram_low = halves(gram)
            left = jnp.concatenate([gram_high, gram_high, gram_low], 1)
            square = matmul(left, jnp.concatenate([gram_high, gram_low, gram_high], 0))
            poly_high, poly_low = halves(-4.775 * gram + 2.0315 * square)
            left = jnp.concatenate([poly_high, poly_high, poly_low], 1)
            change = matmul(left, jnp.concatenate([high, low, high], 0))
            iterate_ref[index] = 3.4445 * iterate + change
        return carry

    lax.fori_loop(0, 2, coarse_step, 0)
    lax.fori_loop(0, NS_STEPS - 2, fine_step, 0)
    step = step_ref[0]
    gate_fast = (whole_weights(slices_ref, 0).astype(F32) + step * iterate_ref[0]).astype(BF)
    up_fast = (whole_weights(slices_ref, 1).astype(F32) + step * iterate_ref[1]).astype(BF)
    down_fast = (down_ref[...].astype(F32) + step * iterate_ref[2].T).astype(BF)
    query = jnp.concatenate([own_ref[0, 64:128, :], own_ref[1, 64:128, :]], 0)
    fast_ref[...] = fast_forward(query, gate_fast, up_fast, down_fast)


def norm_kernel(parts_ref, gain_ref, out_ref):
    square = None
    for source in range(16):
        wide = parts_ref[source].astype(F32)
        part = jnp.sum(wide * wide, axis=-1, keepdims=True)
        square = part if square is None else square + part
    scale = lax.rsqrt(square * (1.0 / (16 * DH)) + 1e-06)
    for source in range(16):
        head = 2 * (source % 8) + source // 8
        columns = slice(head * DH, (head + 1) * DH)
        wide = parts_ref[source].astype(F32) * scale * gain_ref[:, columns][None]
        out_ref[:, :, columns] = wide.astype(BF)


PARAMS = pltpu.CompilerParams(vmem_limit_bytes=16 * 1024 * 1024)
VMEM = pl.BlockSpec(memory_space=pltpu.VMEM)
ANY = pl.BlockSpec(memory_space=pl.ANY)
HBM = pl.BlockSpec(memory_space=pltpu.HBM)
SMEM = pl.BlockSpec(memory_space=pltpu.SMEM)


def shape_of(shape, dtype=BF):
    return jax.ShapeDtypeStruct(shape, dtype)


def body(queries, keys, values, token_rates, step_size, w_gate, w_up, w_down, norm_gain):
    core = lax.axis_index("core")
    chip = lax.axis_index(RING).astype(jnp.int32).reshape(1)
    line = lax.axis_index("y_hi").astype(jnp.int32).reshape(1)
    pieces = (queries, keys, values, token_rates, w_gate, w_up, w_down)
    place = core.astype(jnp.int32).reshape(1)
    mine, other = pl.pallas_call(
        pack_kernel,
        out_shape=(shape_of((416, DH)),) * 2,
        in_specs=[SMEM] + [HBM] * 7,
        out_specs=(VMEM,) * 2,
        scratch_shapes=[pltpu.VMEM(piece.shape, piece.dtype) for piece in pieces]
        + [pltpu.SemaphoreType.DMA((7,))],
        compiler_params=pltpu.CompilerParams(vmem_limit_bytes=61500 * 1024),
        name="pack",
    )(place, *pieces)
    arrived = lax.ppermute(other, "core", [(0, 1), (1, 0)])
    own, context, pool, raw = pl.pallas_call(
        arrange_kernel,
        out_shape=(
            shape_of((2, 416, DH)),
            shape_of((2, 256, DH)),
            shape_of((272, DH)),
            shape_of((CHIPS, 48, 128)),
        ),
        in_specs=[SMEM, VMEM, VMEM],
        out_specs=(VMEM,) * 4,
        compiler_params=PARAMS,
        name="arrange",
    )(place, mine, arrived)
    raw = lax.all_to_all(raw, RING, 0, 0, tiled=True)
    pools = [pool]
    for distance in range(1, 4):
        pools.append(lax.ppermute(pool, "y_hi", [(i, (i + distance) % 4) for i in range(4)]))
    ring = [(i, (i + 1) % CHIPS) for i in range(CHIPS)]
    chunks = [lax.ppermute(context, RING, ring)]

    grad, slices, down_fast = pl.pallas_call(
        grad_kernel,
        out_shape=(shape_of((8, 96, PART)), shape_of((2 * DH, PART)), shape_of((DF, DH))),
        in_specs=[SMEM] + [VMEM] * 5,
        out_specs=(VMEM,) * 3,
        compiler_params=PARAMS,
        name="grad",
    )(line, *pools, raw)
    parts = lax.all_to_all(grad, "z", 0, 0, tiled=True)
    fills = [slices]
    for distance in range(1, 4):
        fills.append(lax.ppermute(slices, "y_hi", [(i, (i + distance) % 4) for i in range(4)]))
    total = pl.pallas_call(
        sum_kernel,
        out_shape=shape_of((8, 96, PART)),
        in_specs=[VMEM, ANY],
        out_specs=VMEM,
        compiler_params=PARAMS,
        name="sum",
    )(parts, chunks[0])
    chunks.append(lax.ppermute(chunks[-1], RING, ring))
    total = lax.all_to_all(total, "z", 0, 0, tiled=True)
    total, slices = pl.pallas_call(
        widen_kernel,
        out_shape=(shape_of((4, 8, 96, PART)), shape_of((4, 2 * DH, PART))),
        in_specs=[SMEM] + [VMEM] * 5 + [ANY],
        out_specs=(VMEM,) * 2,
        compiler_params=PARAMS,
        name="widen",
    )(line, total, *fills, chunks[1])
    chunks.append(lax.ppermute(chunks[-1], RING, ring))
    total = lax.all_to_all(total, "y_hi", 0, 0, tiled=True)

    step = lax.dynamic_slice_in_dim(step_size, core, 1, 0)
    fast = pl.pallas_call(
        newton_kernel,
        out_shape=shape_of((TOK, DH), F32),
        in_specs=[SMEM] + [VMEM] * 4 + [ANY],
        out_specs=VMEM,
        scratch_shapes=[pltpu.VMEM((3, DH, DF), F32)],
        compiler_params=PARAMS,
        cost_estimate=pl.CostEstimate(
            flops=8_000_000_000, transcendentals=100_000, bytes_accessed=4_000_000
        ),
        name="newton",
    )(step, total, slices, down_fast, own, chunks[2])
    chunks.append(lax.ppermute(chunks[-1], RING, ring))
    chunks = [chunk.reshape(2, 4, 64, DH) for chunk in chunks]
    combined = pl.pallas_call(
        attention_kernel,
        out_shape=shape_of((16, 2, 8, DH)),
        in_specs=[SMEM] + [VMEM] * 8,
        out_specs=VMEM,
        compiler_params=PARAMS,
        name="window",
    )(chip, own, *chunks, slices, down_fast, fast)
    gathered = lax.all_to_all(combined, ("core", "y_lo", "x"), 0, 0, tiled=True)
    return pl.pallas_call(
        norm_kernel,
        out_shape=jax.ShapeDtypeStruct((2, 8, 16 * DH), BF),
        in_specs=[VMEM] * 2,
        out_specs=VMEM,
        compiler_params=PARAMS,
        name="norm",
    )(gathered, norm_gain.reshape(1, 16 * DH))


def solution(mesh):
    fine = Mesh(mesh.devices.reshape(2, 4, 4, 8, 2), ("y_lo", "x", "y_hi", "z", "core"))
    seq = RING + ("core",)
    head = ("y_lo", "x")
    placed = (
        P(None, seq, head),
        P(None, seq, head),
        P(None, seq, head),
        P(None, head, seq),
        P(head),
        P(head, seq, None),
        P(head, seq, None),
        P(head, seq, None),
        P(),
    )
    return jax.shard_map(
        body, mesh=fine, in_specs=placed, out_specs=P(None, seq + head, None), check_vma=False
    )
```

time: 201 us -> 170 us (0.85)
  blocking collectives: 80.9 us -> 11.7 us
  starting transfers between devices: 25.9 us -> 73.7 us
  local copies, waits for them, and re-layouts: 6.74 us -> 2.2 us
  waiting for transfers between devices: 63.7 us -> 60.3 us
  Pallas kernels: 23.2 us -> 21 us
    all_to_all x3 -> x0, blocking collectives: 49.1 us -> none  [the longest x1 26.9 us: body(): raw = lax.all_to_all(raw, RING + ('core',), 0, 0, tiled=True)]
    ppermute x1 -> x8, starting transfers between devices: 2.64 us -> 38.6 us  [the longest x3 14.4 us: body(): lax.ppermute(pool, 'y_hi', [(i, (i + distance) % 4) for i in range(4)])]
    all_to_all x1, blocking collectives: 31.8 us -> 11.7 us  [body(): gathered = lax.all_to_all(combined, ('core', 'y_lo', 'x'), 0, 0, tiled=True)]
    all_to_all x2, starting transfers between devices: 9.13 us -> 16.4 us  [the longest x1 10.3 us: body(): raw = lax.all_to_all(raw, RING, 0, 0, tiled=True)]
    ppermute x3, waiting for transfers between devices: 38.8 us -> 32.9 us  [body(): chunks.append(lax.ppermute(chunks[-1], RING, ring))]
    unnamed x18 -> x6, local copies, waits for them, and re-layouts: 6.14 us -> 1.59 us
    all_to_all x1, starting transfers between devices: 3.49 us -> 7.04 us  [body(): total = lax.all_to_all(total, 'y_hi', 0, 0, tiled=True)]
    pallas_call x4 -> x5, Pallas kernels: 20.5 us -> 17.7 us  [the longest x1 12.7 us: body(): pl.pallas_call(newton_kernel, out_shape=shape_of((TOK, DH), F32), in_spec...]
  transfers between devices with their start and end apart: 8 -> 15, of which waited for: 4 -> 9; matrix products, arithmetic and copies ran while one was open for 0% -> 0% of each run, Pallas kernels for 1% -> 7%
where the time goes in v3:
time: 170 us; the launch traced here: 169 us
  starting transfers between devices  73.7 us (43%)
  waiting for transfers between devices  60.3 us (35%)
  Pallas kernels  21 us (12%)
  blocking collectives  11.7 us (7%)
  local copies, waits for them, and re-layouts  2.2 us (1%)
    ppermute x3, waiting for transfers between devices, body(): chunks.append(lax.ppermute(chunks[-1], RING, ring))  32.9 us
    ppermute x3, starting transfers between devices, body(): lax.ppermute(pool, 'y_hi', [(i, (i + distance) % 4) for i in range(4)])  14.4 us
    ppermute x1, waiting for transfers between devices, body(): chunks = [lax.ppermute(context, RING, ring)]  12.8 us
    pallas_call x1, Pallas kernels, body(): pl.pallas_call(newton_kernel, out_shape=shape_of((TOK, DH), F32), in_spec...  12.7 us
    ppermute x3, starting transfers between devices, body(): lax.ppermute(slices, 'y_hi', [(i, (i + distance) % 4) for i in range(4)])  12.1 us
    all_to_all x1, blocking collectives, body(): gathered = lax.all_to_all(combined, ('core', 'y_lo', 'x'), 0, 0, tiled=True)  11.7 us
    ppermute x3, waiting for transfers between devices, body(): lax.ppermute(pool, 'y_hi', [(i, (i + distance) % 4) for i in range(4)])  10.9 us
    all_to_all x1, starting transfers between devices, body(): raw = lax.all_to_all(raw, RING, 0, 0, tiled=True)  10.3 us
  transfers between devices with their start and end apart: 15, of which 9 were waited for; matrix products, arithmetic and copies ran while one was open for 0% of the time, Pallas kernels for 7%

profile of v3, /device:TPU:1, one launch (start us, length us, event | category | flops | bytes accessed | tf_op | source)
XLA Modules:
  0.0 169.1 jit_solution(9167078583400474857)
XLA Ops:
  0.0 1.9 %pack.1 = (bf16[416,256]{1,0:T(8,128)(2,1)}, bf16[416,256]{1,0:T(8,128)(2,1)}) custom-call(s32[1]{0:T(128)} %bitcast.1.core_ref, bf16[2,64,512]{2,1,0:T(8,128)(2,1)} %q_in.1, bf16[2,64,512]{2,1,0:T(8,128)(2,1)} %k_in.1, bf16[2,64,512]{2,1,0:T(8,128)(2,1)} %v_in.1, f32[1,2,64]{2,1,0:T(2,128)} %rate_in.1, bf16[2,4,512]{2,1,0:T(4,128)(2,1)} %gate_in.1, ...), custom_call_target="tpu_custom_call" | custom-call | tf_op jit(solution)/shard_map/pack/pallas_call | solution.py:311
  1.9 8.7 %collective-permute-start = (bf16[416,256]{1,0:T(8,128)(2,1)}, bf16[416,256]{1,0:T(8,128)(2,1)S(1)}, u32[]{:S(2)}, u32[]{:S(2)}) collective-permute-start(bf16[416,256]{1,0:T(8,128)(2,1)} %get-tuple-element.17), channel_id=1, source_target_pairs={{0,1},{1,0},{2,3},{3,2},{4,5},{5,4},{6,7},{7,6},{8,9},{9,8},{10,11... | collective-permute-start | bytes 638984 | tf_op jit(solution)/shard_map/ppermute | solution.py:321
  10.7 1.3 collective-permute-done.arrived_ref
  12.0 0.9 copy-done
  12.9 0.8 arrange.1
  13.7 10.3 %all-to-all-start = ((bf16[32,48,128]{2,1,0:T(8,128)(2,1)}), bf16[32,48,128]{2,1,0:T(8,128)(2,1)S(1)}, u32[]{:S(2)}, u32[]{:S(2)}) async-start(bf16[32,48,128]{2,1,0:T(8,128)(2,1)} %get-tuple-element.21), calls=%async_computation | async-start | bytes 786432 | tf_op jit(solution)/shard_map/all_to_all | solution.py:335
  24.1 4.0 %collective-permute-start.5 = (bf16[272,256]{1,0:T(8,128)(2,1)S(1)}, bf16[272,256]{1,0:T(8,128)(2,1)S(1)}, u32[]{:S(2)}, u32[]{:S(2)}) collective-permute-start(bf16[272,256]{1,0:T(8,128)(2,1)S(1)} %get-tuple-element.20.p0_ref), channel_id=1, source_target_pairs={{0,16},{16,32},{32,48},{48,0},{1,17},{17,33},{33,49},{49,1},{2,18}... | collective-permute-start | bytes 417800 | tf_op jit(solution)/shard_map/ppermute | solution.py:338
  28.1 5.2 %collective-permute-start.6 = (bf16[272,256]{1,0:T(8,128)(2,1)S(1)}, bf16[272,256]{1,0:T(8,128)(2,1)S(1)}, u32[]{:S(2)}, u32[]{:S(2)}) collective-permute-start(bf16[272,256]{1,0:T(8,128)(2,1)S(1)} %get-tuple-element.20.p0_ref), channel_id=1, source_target_pairs={{0,32},{16,48},{32,0},{48,16},{1,33},{17,49},{33,1},{49,17},{2,34}... | collective-permute-start | bytes 417800 | tf_op jit(solution)/shard_map/ppermute | solution.py:338
  33.4 5.2 %collective-permute-start.7 = (bf16[272,256]{1,0:T(8,128)(2,1)S(1)}, bf16[272,256]{1,0:T(8,128)(2,1)S(1)}, u32[]{:S(2)}, u32[]{:S(2)}) collective-permute-start(bf16[272,256]{1,0:T(8,128)(2,1)S(1)} %get-tuple-element.20.p0_ref), channel_id=1, source_target_pairs={{0,48},{16,0},{32,16},{48,32},{1,49},{17,1},{33,17},{49,33},{2,50}... | collective-permute-start | bytes 417800 | tf_op jit(solution)/shard_map/ppermute | solution.py:338
  38.6 2.8 %collective-permute-done.5.p1_ref = bf16[272,256]{1,0:T(8,128)(2,1)S(1)} collective-permute-done((bf16[272,256]{1,0:T(8,128)(2,1)S(1)}, bf16[272,256]{1,0:T(8,128)(2,1)S(1)}, u32[]{:S(2)}, u32[]{:S(2)}) %collective-permute-start.5) | collective-permute-done | bytes 139296 | tf_op jit(solution)/shard_map/ppermute | solution.py:338
  41.3 6.4 %collective-permute-done.6.p2_ref = bf16[272,256]{1,0:T(8,128)(2,1)S(1)} collective-permute-done((bf16[272,256]{1,0:T(8,128)(2,1)S(1)}, bf16[272,256]{1,0:T(8,128)(2,1)S(1)}, u32[]{:S(2)}, u32[]{:S(2)}) %collective-permute-start.6) | collective-permute-done | bytes 139296 | tf_op jit(solution)/shard_map/ppermute | solution.py:338
  47.7 1.7 %collective-permute-done.7.p3_ref = bf16[272,256]{1,0:T(8,128)(2,1)S(1)} collective-permute-done((bf16[272,256]{1,0:T(8,128)(2,1)S(1)}, bf16[272,256]{1,0:T(8,128)(2,1)S(1)}, u32[]{:S(2)}, u32[]{:S(2)}) %collective-permute-start.7) | collective-permute-done | bytes 139296 | tf_op jit(solution)/shard_map/ppermute | solution.py:338
  49.4 1.7 %grad.1 = (bf16[8,96,128]{2,1,0:T(8,128)(2,1)}, bf16[512,128]{1,0:T(8,128)(2,1)S(1)}, bf16[512,256]{1,0:T(8,128)(2,1)S(1)}) custom-call(s32[1]{0:T(128)} %bitcast.6.row_ref, bf16[272,256]{1,0:T(8,128)(2,1)S(1)} %get-tuple-element.20.p0_ref, bf16[272,256]{1,0:T(8,128)(2,1)S(1)} %collective-permute-done.5.p1_ref, ...), custom_call_target="tpu_custom_call" | custom-call | tf_op jit(solution)/shard_map/grad/pallas_call | solution.py:342
  51.2 6.0 %all-to-all-start.1 = ((bf16[8,96,128]{2,1,0:T(8,128)(2,1)}), bf16[8,96,128]{2,1,0:T(8,128)(2,1)S(1)}, u32[]{:S(2)}, u32[]{:S(2)}) async-start(bf16[8,96,128]{2,1,0:T(8,128)(2,1)} %get-tuple-element.22), calls=%async_computation.1 | async-start | bytes 393216 | tf_op jit(solution)/shard_map/all_to_all | solution.py:350
  57.2 3.4 %collective-permute-start.1 = (bf16[2,256,256]{2,1,0:T(8,128)(2,1)S(1)}, bf16[2,256,256]{2,1,0:T(8,128)(2,1)S(1)}, u32[]{:S(2)}, u32[]{:S(2)}) collective-permute-start(bf16[2,256,256]{2,1,0:T(8,128)(2,1)S(1)} %get-tuple-element.19), channel_id=1, source_target_pairs={{0,2},{2,4},{4,6},{6,8},{8,10},{10,12},{12,14},{14,16},{16,18},{18... | collective-permute-start | bytes 786440 | tf_op jit(solution)/shard_map/ppermute | solution.py:340
  60.6 12.8 %collective-permute-done.1._ = bf16[2,256,256]{2,1,0:T(8,128)(2,1)S(1)} collective-permute-done((bf16[2,256,256]{2,1,0:T(8,128)(2,1)S(1)}, bf16[2,256,256]{2,1,0:T(8,128)(2,1)S(1)}, u32[]{:S(2)}, u32[]{:S(2)}) %collective-permute-start.1) | collective-permute-done | bytes 262176 | tf_op jit(solution)/shard_map/ppermute | solution.py:340
  74.1 3.4 %all-to-all-start.2 = ((bf16[8,96,128]{2,1,0:T(8,128)(2,1)}), bf16[8,96,128]{2,1,0:T(8,128)(2,1)S(1)}, u32[]{:S(2)}, u32[]{:S(2)}) async-start(bf16[8,96,128]{2,1,0:T(8,128)(2,1)} %sum.1), calls=%async_computation.2 | async-start | bytes 393216 | tf_op jit(solution)/shard_map/all_to_all | solution.py:363
  77.5 3.3 %collective-permute-start.2 = (bf16[2,256,256]{2,1,0:T(8,128)(2,1)S(1)}, bf16[2,256,256]{2,1,0:T(8,128)(2,1)S(1)}, u32[]{:S(2)}, u32[]{:S(2)}) collective-permute-start(bf16[2,256,256]{2,1,0:T(8,128)(2,1)S(1)} %collective-permute-done.1._), channel_id=1, source_target_pairs={{0,2},{2,4},{4,6},{6,8},{8,10},{10,12},{12,14},{14,16},{16,18},{18... | collective-permute-start | bytes 786440 | tf_op jit(solution)/shard_map/ppermute | solution.py:362
  80.8 3.9 %collective-permute-start.10 = (bf16[512,128]{1,0:T(8,128)(2,1)S(1)}, bf16[512,128]{1,0:T(8,128)(2,1)S(1)}, u32[]{:S(2)}, u32[]{:S(2)}) collective-permute-start(bf16[512,128]{1,0:T(8,128)(2,1)S(1)} %get-tuple-element.23.f0_ref), channel_id=1, source_target_pairs={{0,48},{16,0},{32,16},{48,32},{1,49},{17,1},{33,17},{49,33},{2,50}... | collective-permute-start | bytes 393224 | tf_op jit(solution)/shard_map/ppermute | solution.py:353
  84.7 2.3 %collective-permute-start.8 = (bf16[512,128]{1,0:T(8,128)(2,1)S(1)}, bf16[512,128]{1,0:T(8,128)(2,1)S(1)}, u32[]{:S(2)}, u32[]{:S(2)}) collective-permute-start(bf16[512,128]{1,0:T(8,128)(2,1)S(1)} %get-tuple-element.23.f0_ref), channel_id=1, source_target_pairs={{0,16},{16,32},{32,48},{48,0},{1,17},{17,33},{33,49},{49,1},{2,18}... | collective-permute-start | bytes 393224 | tf_op jit(solution)/shard_map/ppermute | solution.py:353
  87.0 5.9 %collective-permute-start.9 = (bf16[512,128]{1,0:T(8,128)(2,1)S(1)}, bf16[512,128]{1,0:T(8,128)(2,1)S(1)}, u32[]{:S(2)}, u32[]{:S(2)}) collective-permute-start(bf16[512,128]{1,0:T(8,128)(2,1)S(1)} %get-tuple-element.23.f0_ref), channel_id=1, source_target_pairs={{0,32},{16,48},{32,0},{48,16},{1,33},{17,49},{33,1},{49,17},{2,34}... | collective-permute-start | bytes 393224 | tf_op jit(solution)/shard_map/ppermute | solution.py:353
  92.9 1.4 collective-permute-done.2._
  94.2 2.4 %collective-permute-done.9.f2_ref = bf16[512,128]{1,0:T(8,128)(2,1)S(1)} collective-permute-done((bf16[512,128]{1,0:T(8,128)(2,1)S(1)}, bf16[512,128]{1,0:T(8,128)(2,1)S(1)}, u32[]{:S(2)}, u32[]{:S(2)}) %collective-permute-start.9) | collective-permute-done | bytes 131104 | tf_op jit(solution)/shard_map/ppermute | solution.py:353
  96.7 1.0 widen.1
  97.7 7.0 %all-to-all-start.3 = ((bf16[4,8,96,128]{3,2,1,0:T(8,128)(2,1)}), bf16[4,8,96,128]{3,2,1,0:T(8,128)(2,1)S(1)}, u32[]{:S(2)}, u32[]{:S(2)}) async-start(bf16[4,8,96,128]{3,2,1,0:T(8,128)(2,1)} %get-tuple-element.26), calls=%async_computation.3 | async-start | bytes 1572864 | tf_op jit(solution)/shard_map/all_to_all | solution.py:373
  104.7 3.1 %collective-permute-start.3 = (bf16[2,256,256]{2,1,0:T(8,128)(2,1)S(1)}, bf16[2,256,256]{2,1,0:T(8,128)(2,1)S(1)}, u32[]{:S(2)}, u32[]{:S(2)}) collective-permute-start(bf16[2,256,256]{2,1,0:T(8,128)(2,1)S(1)} %collective-permute-done.2._), channel_id=1, source_target_pairs={{0,2},{2,4},{4,6},{6,8},{8,10},{10,12},{12,14},{14,16},{16,18},{18... | collective-permute-start | bytes 786440 | tf_op jit(solution)/shard_map/ppermute | solution.py:372
  109.1 29.8 %collective-permute-done.3._ = bf16[2,256,256]{2,1,0:T(8,128)(2,1)S(1)} collective-permute-done((bf16[2,256,256]{2,1,0:T(8,128)(2,1)S(1)}, bf16[2,256,256]{2,1,0:T(8,128)(2,1)S(1)}, u32[]{:S(2)}, u32[]{:S(2)}) %collective-permute-start.3) | collective-permute-done | bytes 262176 | tf_op jit(solution)/shard_map/ppermute | solution.py:372
  138.9 1.9 %collective-permute-start.4 = (bf16[2,256,256]{2,1,0:T(8,128)(2,1)S(1)}, bf16[2,256,256]{2,1,0:T(8,128)(2,1)S(1)}, u32[]{:S(2)}, u32[]{:S(2)}) collective-permute-start(bf16[2,256,256]{2,1,0:T(8,128)(2,1)S(1)} %collective-permute-done.3._), channel_id=1, source_target_pairs={{0,2},{2,4},{4,6},{6,8},{8,10},{10,12},{12,14},{14,16},{16,18},{18... | collective-permute-start | bytes 786440 | tf_op jit(solution)/shard_map/ppermute | solution.py:388
  140.8 12.7 %newton.1.fast_ref = f32[128,256]{1,0:T(8,128)S(1)} custom-call(f32[1]{0:T(128)} %dynamic_slice.3.step_ref, bf16[4,8,96,128]{3,2,1,0:T(8,128)(2,1)S(1)} %all-to-all-done.3.total_ref, bf16[4,512,128]{2,1,0:T(8,128)(2,1)S(1)} %get-tuple-element.24.slices_ref, bf16[512,256]{1,0:T(8,128)(2,1)S(1)} %get-tuple-element.25.down_ref, ...), custom_call_target="tpu_custom_call" | custom-call | flops 8000000000 | bytes 4000000 | tf_op jit(solution)/shard_map/newton/pallas_call | solution.py:376
  153.5 1.7 %collective-permute-done.4 = bf16[2,256,256]{2,1,0:T(8,128)(2,1)S(1)} collective-permute-done((bf16[2,256,256]{2,1,0:T(8,128)(2,1)S(1)}, bf16[2,256,256]{2,1,0:T(8,128)(2,1)S(1)}, u32[]{:S(2)}, u32[]{:S(2)}) %collective-permute-start.4) | collective-permute-done | bytes 262176 | tf_op jit(solution)/shard_map/ppermute | solution.py:388
  155.2 1.3 window.1
  156.6 11.7 %all_to_all.25.parts_ref = bf16[16,2,8,256]{3,2,1,0:T(8,128)(2,1)S(1)} all-to-all(bf16[16,2,8,256]{3,2,1,0:T(8,128)(2,1)S(1)} %window.1), channel_id=1, replica_groups=mesh['y_lo'=2,'x'=4,'y_hi'=4,'z'=8,'core'=2] {'core','y_lo','x'}, dimensions={0} | all-to-all | bytes 262144 | tf_op jit(solution)/shard_map/all_to_all | solution.py:398
  (14 shorter events, 2.8 us)
Async XLA Ops:
  1.9 10.0 %collective-permute-start = (bf16[416,256]{1,0:T(8,128)(2,1)}, bf16[416,256]{1,0:T(8,128)(2,1)S(1)}, u32[]{:S(2)}, u32[]{:S(2)}) collective-permute-start(bf16[416,256]{1,0:T(8,128)(2,1)} %get-tuple-element.17), channel_id=1, source_target_pairs={{0,1},{1,0},{2,3},{3,2},{4,5},{5,4},{6,7},{7,6},{8,9},{9,8},{10,11... | collective-permute-start | bytes 638984 | tf_op jit(solution)/shard_map/ppermute | solution.py:321
  12.0 0.9 copy-start
  13.7 35.7 %all-to-all-start = ((bf16[32,48,128]{2,1,0:T(8,128)(2,1)}), bf16[32,48,128]{2,1,0:T(8,128)(2,1)S(1)}, u32[]{:S(2)}, u32[]{:S(2)}) async-start(bf16[32,48,128]{2,1,0:T(8,128)(2,1)} %get-tuple-element.21), calls=%async_computation | async-start | bytes 786432 | tf_op jit(solution)/shard_map/all_to_all | solution.py:335
  24.1 17.3 %collective-permute-start.5 = (bf16[272,256]{1,0:T(8,128)(2,1)S(1)}, bf16[272,256]{1,0:T(8,128)(2,1)S(1)}, u32[]{:S(2)}, u32[]{:S(2)}) collective-permute-start(bf16[272,256]{1,0:T(8,128)(2,1)S(1)} %get-tuple-element.20.p0_ref), channel_id=1, source_target_pairs={{0,16},{16,32},{32,48},{48,0},{1,17},{17,33},{33,49},{49,1},{2,18}... | collective-permute-start | bytes 417800 | tf_op jit(solution)/shard_map/ppermute | solution.py:338
  28.1 19.6 %collective-permute-start.6 = (bf16[272,256]{1,0:T(8,128)(2,1)S(1)}, bf16[272,256]{1,0:T(8,128)(2,1)S(1)}, u32[]{:S(2)}, u32[]{:S(2)}) collective-permute-start(bf16[272,256]{1,0:T(8,128)(2,1)S(1)} %get-tuple-element.20.p0_ref), channel_id=1, source_target_pairs={{0,32},{16,48},{32,0},{48,16},{1,33},{17,49},{33,1},{49,17},{2,34}... | collective-permute-start | bytes 417800 | tf_op jit(solution)/shard_map/ppermute | solution.py:338
  33.4 16.0 %collective-permute-start.7 = (bf16[272,256]{1,0:T(8,128)(2,1)S(1)}, bf16[272,256]{1,0:T(8,128)(2,1)S(1)}, u32[]{:S(2)}, u32[]{:S(2)}) collective-permute-start(bf16[272,256]{1,0:T(8,128)(2,1)S(1)} %get-tuple-element.20.p0_ref), channel_id=1, source_target_pairs={{0,48},{16,0},{32,16},{48,32},{1,49},{17,1},{33,17},{49,33},{2,50}... | collective-permute-start | bytes 417800 | tf_op jit(solution)/shard_map/ppermute | solution.py:338
  51.2 22.2 %all-to-all-start.1 = ((bf16[8,96,128]{2,1,0:T(8,128)(2,1)}), bf16[8,96,128]{2,1,0:T(8,128)(2,1)S(1)}, u32[]{:S(2)}, u32[]{:S(2)}) async-start(bf16[8,96,128]{2,1,0:T(8,128)(2,1)} %get-tuple-element.22), calls=%async_computation.1 | async-start | bytes 393216 | tf_op jit(solution)/shard_map/all_to_all | solution.py:350
  57.2 16.2 %collective-permute-start.1 = (bf16[2,256,256]{2,1,0:T(8,128)(2,1)S(1)}, bf16[2,256,256]{2,1,0:T(8,128)(2,1)S(1)}, u32[]{:S(2)}, u32[]{:S(2)}) collective-permute-start(bf16[2,256,256]{2,1,0:T(8,128)(2,1)S(1)} %get-tuple-element.19), channel_id=1, source_target_pairs={{0,2},{2,4},{4,6},{6,8},{8,10},{10,12},{12,14},{14,16},{16,18},{18... | collective-permute-start | bytes 786440 | tf_op jit(solution)/shard_map/ppermute | solution.py:340
  74.1 22.5 %all-to-all-start.2 = ((bf16[8,96,128]{2,1,0:T(8,128)(2,1)}), bf16[8,96,128]{2,1,0:T(8,128)(2,1)S(1)}, u32[]{:S(2)}, u32[]{:S(2)}) async-start(bf16[8,96,128]{2,1,0:T(8,128)(2,1)} %sum.1), calls=%async_computation.2 | async-start | bytes 393216 | tf_op jit(solution)/shard_map/all_to_all | solution.py:363
  77.5 16.7 %collective-permute-start.2 = (bf16[2,256,256]{2,1,0:T(8,128)(2,1)S(1)}, bf16[2,256,256]{2,1,0:T(8,128)(2,1)S(1)}, u32[]{:S(2)}, u32[]{:S(2)}) collective-permute-start(bf16[2,256,256]{2,1,0:T(8,128)(2,1)S(1)} %collective-permute-done.1._), channel_id=1, source_target_pairs={{0,2},{2,4},{4,6},{6,8},{8,10},{10,12},{12,14},{14,16},{16,18},{18... | collective-permute-start | bytes 786440 | tf_op jit(solution)/shard_map/ppermute | solution.py:362
  80.8 13.5 %collective-permute-start.10 = (bf16[512,128]{1,0:T(8,128)(2,1)S(1)}, bf16[512,128]{1,0:T(8,128)(2,1)S(1)}, u32[]{:S(2)}, u32[]{:S(2)}) collective-permute-start(bf16[512,128]{1,0:T(8,128)(2,1)S(1)} %get-tuple-element.23.f0_ref), channel_id=1, source_target_pairs={{0,48},{16,0},{32,16},{48,32},{1,49},{17,1},{33,17},{49,33},{2,50}... | collective-permute-start | bytes 393224 | tf_op jit(solution)/shard_map/ppermute | solution.py:353
  84.7 9.6 %collective-permute-start.8 = (bf16[512,128]{1,0:T(8,128)(2,1)S(1)}, bf16[512,128]{1,0:T(8,128)(2,1)S(1)}, u32[]{:S(2)}, u32[]{:S(2)}) collective-permute-start(bf16[512,128]{1,0:T(8,128)(2,1)S(1)} %get-tuple-element.23.f0_ref), channel_id=1, source_target_pairs={{0,16},{16,32},{32,48},{48,0},{1,17},{17,33},{33,49},{49,1},{2,18}... | collective-permute-start | bytes 393224 | tf_op jit(solution)/shard_map/ppermute | solution.py:353
  87.0 9.7 %collective-permute-start.9 = (bf16[512,128]{1,0:T(8,128)(2,1)S(1)}, bf16[512,128]{1,0:T(8,128)(2,1)S(1)}, u32[]{:S(2)}, u32[]{:S(2)}) collective-permute-start(bf16[512,128]{1,0:T(8,128)(2,1)S(1)} %get-tuple-element.23.f0_ref), channel_id=1, source_target_pairs={{0,32},{16,48},{32,0},{48,16},{1,33},{17,49},{33,1},{49,17},{2,34}... | collective-permute-start | bytes 393224 | tf_op jit(solution)/shard_map/ppermute | solution.py:353
  97.7 43.2 %all-to-all-start.3 = ((bf16[4,8,96,128]{3,2,1,0:T(8,128)(2,1)}), bf16[4,8,96,128]{3,2,1,0:T(8,128)(2,1)S(1)}, u32[]{:S(2)}, u32[]{:S(2)}) async-start(bf16[4,8,96,128]{3,2,1,0:T(8,128)(2,1)} %get-tuple-element.26), calls=%async_computation.3 | async-start | bytes 1572864 | tf_op jit(solution)/shard_map/all_to_all | solution.py:373
  104.7 34.2 %collective-permute-start.3 = (bf16[2,256,256]{2,1,0:T(8,128)(2,1)S(1)}, bf16[2,256,256]{2,1,0:T(8,128)(2,1)S(1)}, u32[]{:S(2)}, u32[]{:S(2)}) collective-permute-start(bf16[2,256,256]{2,1,0:T(8,128)(2,1)S(1)} %collective-permute-done.2._), channel_id=1, source_target_pairs={{0,2},{2,4},{4,6},{6,8},{8,10},{10,12},{12,14},{14,16},{16,18},{18... | collective-permute-start | bytes 786440 | tf_op jit(solution)/shard_map/ppermute | solution.py:372
  107.8 0.7 copy-start.2
  138.9 16.3 %collective-permute-start.4 = (bf16[2,256,256]{2,1,0:T(8,128)(2,1)S(1)}, bf16[2,256,256]{2,1,0:T(8,128)(2,1)S(1)}, u32[]{:S(2)}, u32[]{:S(2)}) collective-permute-start(bf16[2,256,256]{2,1,0:T(8,128)(2,1)S(1)} %collective-permute-done.3._), channel_id=1, source_target_pairs={{0,2},{2,4},{4,6},{6,8},{8,10},{10,12},{12,14},{14,16},{16,18},{18... | collective-permute-start | bytes 786440 | tf_op jit(solution)/shard_map/ppermute | solution.py:388
  156.5 11.8 %copy-start.1 = (f32[4096]{0:T(1024)S(1)}, f32[4096]{0:T(1024)}, u32[]{:S(2)}) copy-start(f32[4096]{0:T(1024)} %param.17) | copy-start | bytes 49156

commit v4 on v3

--- a/solution.py
+++ b/solution.py
@@ -56,7 +56,7 @@
 
 
 def pack_kernel(
-    core_ref, q_in, k_in, v_in, rate_in, gate_in, up_in, down_in, mine_ref, other_ref, *scratch
+    core_ref, q_in, k_in, v_in, rate_in, gate_in, up_in, down_in, mine_ref, other_ref, deal_ref, *scratch
 ):
     sources = (q_in, k_in, v_in, rate_in, gate_in, up_in, down_in)
     q_ref, k_ref, v_ref, rate_ref, gate_ref, up_ref, down_ref = scratch[:7]
@@ -76,17 +76,12 @@
             for block in range(2):
                 first = (index * 2 + block) * 64
                 target[first : first + 64, :] = ref[block, :, columns]
-        for index, ref in enumerate((gate_ref, up_ref)):
-            wide = ref[head].astype(F32)
-            pair = jnp.concatenate([wide[:, :DH], wide[:, DH:]], 0)
-            target[384 + 8 * index : 392 + 8 * index, :] = pair.astype(BF)
-        target[400:408, :] = down_ref[head]
         rate = rate_ref[0, head : head + 1, :]
         high = rate.astype(BF).astype(F32)
         middle = (rate - high).astype(BF).astype(F32)
         low = (rate - high) - middle
         terms = jnp.concatenate([high, middle, low, jnp.zeros_like(rate)], 1)
-        target[408:416, :] = jnp.broadcast_to(terms, (8, DH)).astype(BF)
+        target[384:392, :] = jnp.broadcast_to(terms, (8, DH)).astype(BF)
 
     for head in range(2):
 
@@ -95,58 +90,66 @@
             fill(mine_ref, head)
             fill(other_ref, 1 - head)
 
-
-def arrange_kernel(core_ref, mine_ref, arrived_ref, own_ref, context_ref, pool_ref, weight_ref):
+        tiles = []
+        for row in range(4):
+            part = slice(row * PART, (row + 1) * PART)
+            pair = [gate_ref[head, :, part].astype(F32), up_ref[head, :, part].astype(F32)]
+            tiles.append(jnp.concatenate(pair, 0))
+        tiles += [down_ref[head, :, :128].astype(F32), down_ref[head, :, 128:].astype(F32)]
+        piece = jnp.concatenate(tiles, 0).astype(BF)
+        for depth in range(8):
+            deal_ref[2 * depth + head] = piece
+
+
+def arrange_kernel(core_ref, mine_ref, arrived_ref, own_ref, context_ref):
     own_ref[core_ref[0]] = mine_ref[...]
     own_ref[1 - core_ref[0]] = arrived_ref[...]
     for source in range(2):
         context_ref[source] = own_ref[source, 128:384, :]
-        for index in range(2):
-            first = 128 * index + 64 * source
-            rows = slice(128 * (index + 1), 128 * (index + 1) + 64)
-            pool_ref[first : first + 64, :] = own_ref[source, rows, :]
-        pool_ref[256 + 8 * source : 264 + 8 * source, :] = own_ref[source, 408:416, :]
+
+
+def merge_kernel(own_ref, dealt_ref, pool_ref, down_ref):
+    out_row = lax.broadcasted_iota(jnp.int32, (128, 128), 0)
+    in_row = lax.broadcasted_iota(jnp.int32, (128, 128), 1)
+    place = out_row % 64
+    pick = (place // 4) * 8 + (out_row // 64) * 4 + place % 4
+    chosen = jnp.where(in_row == pick, 1.0, 0.0).astype(BF)
     for row in range(4):
-        lanes = slice(row % 2 * PART, (row % 2 + 1) * PART)
-        pieces = []
-        for index in range(2):
-            first = 384 + 8 * index
-            both = [own_ref[src, first : first + 8, lanes].astype(F32) for src in range(2)]
-            rows = slice(row // 2 * 4, row // 2 * 4 + 4)
-            pieces += [one[rows] for one in both]
-        piece = jnp.concatenate(pieces, 0).astype(BF)
-        down = jnp.concatenate([own_ref[src, 400:408, :].astype(F32) for src in range(2)], 0)
-        down = down.astype(BF)
-        for depth in range(8):
-            weight_ref[row * 8 + depth, 0:16, :] = piece
-            weight_ref[row * 8 + depth, 16:32, :] = down[:, :128]
-            weight_ref[row * 8 + depth, 32:48, :] = down[:, 128:]
-
-
-def grad_kernel(row_ref, p0_ref, p1_ref, p2_ref, p3_ref, raw_ref, grad_ref, slice_ref, down_ref):
-    pools = (p0_ref, p1_ref, p2_ref, p3_ref)
-    weights = []
+        for source in range(2):
+            for index in range(2):
+                first = 128 * index + 64 * source
+                rows = slice(128 * (index + 1), 128 * (index + 1) + 64)
+                pool_ref[row, first : first + 64, :] = own_ref[source, rows, :]
+            first = 256 + 8 * source
+            pool_ref[row, first : first + 8, :] = own_ref[source, 384:392, :]
+        mixed = dealt_ref[:, 8 * row : 8 * row + 8, :].astype(F32).reshape(128, PART).astype(BF)
+        ordered = matmul(chosen, mixed).astype(BF)
+        pool_ref[row, 272:336, :128] = ordered[:64]
+        pool_ref[row, 272:336, 128:] = ordered[64:]
     for index in range(2):
-        piece = raw_ref[:, 8 * index : 8 * index + 8, :].astype(F32)
-        weights.append(piece.reshape(DH, PART).astype(BF))
-        slice_ref[index * DH : (index + 1) * DH, :] = weights[index]
-        half = raw_ref[:, 16 + 16 * index : 32 + 16 * index, :]
-        down_ref[:, index * 128 : (index + 1) * 128] = half.reshape(DF, 128)
+        half = dealt_ref[:, 32 + 8 * index : 40 + 8 * index, :].astype(F32)
+        down_ref[:, index * 128 : (index + 1) * 128] = half.reshape(PART, 128).astype(BF)
+
+
+def grad_kernel(pool_ref, down_ref, grad_ref, slice_ref):
+    slice_ref[0:DH, :] = pool_ref[:, 272:336, :].reshape(DH, DH)
+    slice_ref[DH:, :] = down_ref[...]
+    weights = (slice_ref[0:DH, :PART], slice_ref[0:DH, PART:])
     gate_part, up_part = weights
-    down_part = down_ref[pl.ds(pl.multiple_of(row_ref[0] * PART, PART), PART), :]
+    down_part = down_ref[...]
     equal = lax.broadcasted_iota(jnp.int32, (64, 64), 0) == lax.broadcasted_iota(
         jnp.int32, (64, 64), 1
     )
     columns = []
-    for pool in pools:
+    for row in range(4):
         for source in range(2):
-            terms = pool[256 + 8 * source : 264 + 8 * source, :].astype(F32)[0:1]
+            terms = pool_ref[row, 256 + 8 * source : 264 + 8 * source, :].astype(F32)[0:1]
             rate = terms[:, 0:64] + (terms[:, 64:128] + terms[:, 128:192])
             spread = jnp.where(equal, jnp.broadcast_to(rate, (64, 64)), 0.0)
             columns.append(jnp.sum(spread, axis=1, keepdims=True))
     rate_col = jnp.concatenate(columns, 0)
-    keys_now = rms_norm(jnp.concatenate([pool[0:128, :] for pool in pools], 0))
-    vals_now = jnp.concatenate([pool[128:256, :] for pool in pools], 0)
+    keys_now = rms_norm(pool_ref[:, 0:128, :].reshape(4 * TOK, DH))
+    vals_now = pool_ref[:, 128:256, :].reshape(4 * TOK, DH)
     gate_pre = matmul(keys_now, gate_part)
     up_pre = matmul(keys_now, up_part)
     back = matmul_nt(vals_now, down_part)
@@ -163,25 +166,24 @@
         grad_ref[:, index * 32 : index * 32 + 32, :] = grad.astype(BF)
 
 
-def sum_kernel(parts_ref, _, total_ref):
+def sum_kernel(parts_ref, total_ref):
     total = jnp.sum(parts_ref[...].astype(F32), axis=0, keepdims=True)
     total_ref[...] = jnp.broadcast_to(total, (8, 96, PART)).astype(BF)
 
 
-def widen_kernel(row_ref, piece_ref, f0_ref, f1_ref, f2_ref, f3_ref, _, total_ref, slices_ref):
+def widen_kernel(piece_ref, total_ref):
     for row in range(4):
         total_ref[row] = piece_ref[...]
-    for distance, ref in enumerate((f0_ref, f1_ref, f2_ref, f3_ref)):
-        slices_ref[lax.rem(row_ref[0] + 4 - distance, 4)] = ref[...]
-
-
-def whole_weights(slices_ref, index):
-    rows = slice(index * DH, (index + 1) * DH)
-    return jnp.concatenate([slices_ref[row, rows, :] for row in range(4)], 1)
+
+
+def whole_weights(slices_ref):
+    gate_fast = jnp.concatenate([slices_ref[row, 0:DH, :PART] for row in range(4)], 1)
+    up_fast = jnp.concatenate([slices_ref[row, 0:DH, PART:] for row in range(4)], 1)
+    return gate_fast, up_fast, slices_ref[:, DH:, :].reshape(DF, DH)
 
 
 def attention_kernel(
-    chip_ref, own_ref, c1_ref, c2_ref, c3_ref, c4_ref, slices_ref, down_ref, fast_ref, out_ref
+    chip_ref, own_ref, c1_ref, c2_ref, c3_ref, c4_ref, slices_ref, fast_ref, out_ref
 ):
     chip = chip_ref[0]
     row = lax.broadcasted_iota(jnp.int32, (TOK, TOK), 0)
@@ -227,14 +229,28 @@
             part = matmul(weights, rows_of(distance, 1, block))
             result = part if result is None else result + part
         if block == 0:
-            gate_fast, up_fast = whole_weights(slices_ref, 0), whole_weights(slices_ref, 1)
-            result = result + fast_forward(query, gate_fast, up_fast, down_ref[...])
+            result = result + fast_forward(query, *whole_weights(slices_ref))
         else:
             result = result + fast_ref[...]
         out_ref[:, block] = result.reshape(16, 8, DH).astype(BF)
 
 
-def newton_kernel(step_ref, total_ref, slices_ref, down_ref, own_ref, _, fast_ref, iterate_ref):
+def newton_kernel(
+    step_ref,
+    row_ref,
+    total_ref,
+    f0_ref,
+    f1_ref,
+    f2_ref,
+    f3_ref,
+    own_ref,
+    _,
+    fast_ref,
+    slices_ref,
+    iterate_ref,
+):
+    for distance, ref in enumerate((f0_ref, f1_ref, f2_ref, f3_ref)):
+        slices_ref[lax.rem(row_ref[0] + 4 - distance, 4)] = ref[...]
     for index in range(3):
         rows = slice(index * 32, index * 32 + 32)
         pieces = [total_ref[row, :, rows, :].astype(F32).reshape(DH, PART) for row in range(4)]
@@ -270,9 +286,10 @@
     lax.fori_loop(0, 2, coarse_step, 0)
     lax.fori_loop(0, NS_STEPS - 2, fine_step, 0)
     step = step_ref[0]
-    gate_fast = (whole_weights(slices_ref, 0).astype(F32) + step * iterate_ref[0]).astype(BF)
-    up_fast = (whole_weights(slices_ref, 1).astype(F32) + step * iterate_ref[1]).astype(BF)
-    down_fast = (down_ref[...].astype(F32) + step * iterate_ref[2].T).astype(BF)
+    gate_fast, up_fast, down_fast = whole_weights(slices_ref)
+    gate_fast = (gate_fast.astype(F32) + step * iterate_ref[0]).astype(BF)
+    up_fast = (up_fast.astype(F32) + step * iterate_ref[1]).astype(BF)
+    down_fast = (down_fast.astype(F32) + step * iterate_ref[2].T).astype(BF)
     query = jnp.concatenate([own_ref[0, 64:128, :], own_ref[1, 64:128, :]], 0)
     fast_ref[...] = fast_forward(query, gate_fast, up_fast, down_fast)
 
@@ -308,93 +325,94 @@
     line = lax.axis_index("y_hi").astype(jnp.int32).reshape(1)
     pieces = (queries, keys, values, token_rates, w_gate, w_up, w_down)
     place = core.astype(jnp.int32).reshape(1)
-    mine, other = pl.pallas_call(
+    mine, other, dealt = pl.pallas_call(
         pack_kernel,
-        out_shape=(shape_of((416, DH)),) * 2,
+        out_shape=(shape_of((392, DH)), shape_of((392, DH)), shape_of((16, 48, 128))),
         in_specs=[SMEM] + [HBM] * 7,
-        out_specs=(VMEM,) * 2,
+        out_specs=(VMEM,) * 3,
         scratch_shapes=[pltpu.VMEM(piece.shape, piece.dtype) for piece in pieces]
         + [pltpu.SemaphoreType.DMA((7,))],
         compiler_params=pltpu.CompilerParams(vmem_limit_bytes=61500 * 1024),
         name="pack",
     )(place, *pieces)
+    dealt = lax.all_to_all(dealt, ("z", "core"), 0, 0, tiled=True)
     arrived = lax.ppermute(other, "core", [(0, 1), (1, 0)])
-    own, context, pool, raw = pl.pallas_call(
+    own, context = pl.pallas_call(
         arrange_kernel,
-        out_shape=(
-            shape_of((2, 416, DH)),
-            shape_of((2, 256, DH)),
-            shape_of((272, DH)),
-            shape_of((CHIPS, 48, 128)),
-        ),
+        out_shape=(shape_of((2, 392, DH)), shape_of((2, 256, DH))),
         in_specs=[SMEM, VMEM, VMEM],
-        out_specs=(VMEM,) * 4,
+        out_specs=(VMEM,) * 2,
         compiler_params=PARAMS,
         name="arrange",
     )(place, mine, arrived)
-    raw = lax.all_to_all(raw, RING, 0, 0, tiled=True)
-    pools = [pool]
-    for distance in range(1, 4):
-        pools.append(lax.ppermute(pool, "y_hi", [(i, (i + distance) % 4) for i in range(4)]))
     ring = [(i, (i + 1) % CHIPS) for i in range(CHIPS)]
     chunks = [lax.ppermute(context, RING, ring)]
-
-    grad, slices, down_fast = pl.pallas_call(
+    pool, down = pl.pallas_call(
+        merge_kernel,
+        out_shape=(shape_of((4, 336, DH)), shape_of((PART, DH))),
+        in_specs=[VMEM] * 2,
+        out_specs=(VMEM,) * 2,
+        compiler_params=PARAMS,
+        name="merge",
+    )(own, dealt)
+    pool = lax.all_to_all(pool, "y_hi", 0, 0, tiled=True)
+
+    grad, slices = pl.pallas_call(
         grad_kernel,
-        out_shape=(shape_of((8, 96, PART)), shape_of((2 * DH, PART)), shape_of((DF, DH))),
-        in_specs=[SMEM] + [VMEM] * 5,
-        out_specs=(VMEM,) * 3,
+        out_shape=(shape_of((8, 96, PART)), shape_of((384, DH))),
+        in_specs=[VMEM] * 2,
+        out_specs=(VMEM,) * 2,
         compiler_params=PARAMS,
         name="grad",
-    )(line, *pools, raw)
+    )(pool, down)
     parts = lax.all_to_all(grad, "z", 0, 0, tiled=True)
     fills = [slices]
     for distance in range(1, 4):
         fills.append(lax.ppermute(slices, "y_hi", [(i, (i + distance) % 4) for i in range(4)]))
+    chunks.append(lax.ppermute(chunks[-1], RING, ring))
     total = pl.pallas_call(
         sum_kernel,
         out_shape=shape_of((8, 96, PART)),
-        in_specs=[VMEM, ANY],
+        in_specs=[VMEM],
         out_specs=VMEM,
         compiler_params=PARAMS,
         name="sum",
-    )(parts, chunks[0])
+    )(parts)
+    total = lax.all_to_all(total, "z", 0, 0, tiled=True)
     chunks.append(lax.ppermute(chunks[-1], RING, ring))
-    total = lax.all_to_all(total, "z", 0, 0, tiled=True)
-    total, slices = pl.pallas_call(
+    total = pl.pallas_call(
         widen_kernel,
-        out_shape=(shape_of((4, 8, 96, PART)), shape_of((4, 2 * DH, PART))),
-        in_specs=[SMEM] + [VMEM] * 5 + [ANY],
+        out_shape=shape_of((4, 8, 96, PART)),
+        in_specs=[VMEM],
+        out_specs=VMEM,
+        compiler_params=PARAMS,
+        name="widen",
+    )(total)
+    total = lax.all_to_all(total, "y_hi", 0, 0, tiled=True)
+
+    step = lax.dynamic_slice_in_dim(step_size, core, 1, 0)
+    fast, slices = pl.pallas_call(
+        newton_kernel,
+        out_shape=(shape_of((TOK, DH), F32), shape_of((4, 384, DH))),
+        in_specs=[SMEM] * 2 + [VMEM] * 6 + [ANY],
         out_specs=(VMEM,) * 2,
-        compiler_params=PARAMS,
-        name="widen",
-    )(line, total, *fills, chunks[1])
-    chunks.append(lax.ppermute(chunks[-1], RING, ring))
-    total = lax.all_to_all(total, "y_hi", 0, 0, tiled=True)
-
-    step = lax.dynamic_slice_in_dim(step_size, core, 1, 0)
-    fast = pl.pallas_call(
-        newton_kernel,
-        out_shape=shape_of((TOK, DH), F32),
-        in_specs=[SMEM] + [VMEM] * 4 + [ANY],
-        out_specs=VMEM,
         scratch_shapes=[pltpu.VMEM((3, DH, DF), F32)],
         compiler_params=PARAMS,
         cost_estimate=pl.CostEstimate(
             flops=8_000_000_000, transcendentals=100_000, bytes_accessed=4_000_000
         ),
         name="newton",
-    )(step, total, slices, down_fast, own, chunks[2])
+    )(step, line, total, *fills, own, chunks[2])
     chunks.append(lax.ppermute(chunks[-1], RING, ring))
     chunks = [chunk.reshape(2, 4, 64, DH) for chunk in chunks]
     combined = pl.pallas_call(
         attention_kernel,
         out_shape=shape_of((16, 2, 8, DH)),
-        in_specs=[SMEM] + [VMEM] * 8,
+        in_specs=[SMEM] + [VMEM] * 7,
         out_specs=VMEM,
         compiler_params=PARAMS,
         name="window",
-    )(chip, own, *chunks, slices, down_fast, fast)
+    )(chip, own, *chunks, slices, fast)
     gathered = lax.all_to_all(combined, ("core", "y_lo", "x"), 0, 0, tiled=True)
     return pl.pallas_call(
         norm_kernel,

time: 170 us -> 183 us (1.076)
  blocking collectives: 11.7 us -> 79.7 us
  starting transfers between devices: 73.7 us -> 37.6 us
  waiting for transfers between devices: 60.3 us -> 43.9 us
    all_to_all x0 -> x3, blocking collectives: none -> 48.5 us  [the longest x1 26.4 us: body(): pool = lax.all_to_all(pool, 'y_hi', 0, 0, tiled=True)]
    all_to_all x1, blocking collectives: 11.7 us -> 31.2 us  [body(): gathered = lax.all_to_all(combined, ('core', 'y_lo', 'x'), 0, 0, tiled=True)]
    ppermute x3 -> x0, starting transfers between devices: 14.4 us -> none  [body(): lax.ppermute(pool, 'y_hi', [(i, (i + distance) % 4) for i in range(4)])]
    ppermute x3, waiting for transfers between devices: 32.9 us -> 18.9 us  [body(): chunks.append(lax.ppermute(chunks[-1], RING, ring))]
    ppermute x3 -> x0, waiting for transfers between devices: 10.9 us -> none  [body(): lax.ppermute(pool, 'y_hi', [(i, (i + distance) % 4) for i in range(4)])]
    all_to_all x3 -> x1, starting transfers between devices: 19.8 us -> 12 us  [body(): dealt = lax.all_to_all(dealt, ('z', 'core'), 0, 0, tiled=True)]
    ppermute x1, starting transfers between devices: 8.75 us -> 2.01 us  [body(): arrived = lax.ppermute(other, 'core', [(0, 1), (1, 0)])]
    all_to_all x3 -> x1, waiting for transfers between devices: 0.01 us -> 6.61 us  [body(): dealt = lax.all_to_all(dealt, ('z', 'core'), 0, 0, tiled=True)]
  transfers between devices with their start and end apart: 15 -> 10, of which waited for: 9 -> 6; matrix products, arithmetic and copies ran while one was open for 0% -> 0% of each run, Pallas kernels for 7% -> 7%
where the time goes in v4:
time: 183 us; the launch traced here: 182 us
  blocking collectives  79.7 us (44%)
  waiting for transfers between devices  43.9 us (24%)
  starting transfers between devices  37.6 us (21%)
  Pallas kernels  19.2 us (10%)
    all_to_all x1, blocking collectives, body(): gathered = lax.all_to_all(combined, ('core', 'y_lo', 'x'), 0, 0, tiled=True)  31.2 us
    all_to_all x1, blocking collectives, body(): pool = lax.all_to_all(pool, 'y_hi', 0, 0, tiled=True)  26.4 us
    ppermute x3, waiting for transfers between devices, body(): chunks.append(lax.ppermute(chunks[-1], RING, ring))  18.9 us
    ppermute x1, waiting for transfers between devices, body(): chunks = [lax.ppermute(context, RING, ring)]  14.6 us
    pallas_call x1, Pallas kernels, body(): pl.pallas_call(newton_kernel, out_shape=(shape_of((TOK, DH), F32), shape_...  12.8 us
    all_to_all x1, starting transfers between devices, body(): dealt = lax.all_to_all(dealt, ('z', 'core'), 0, 0, tiled=True)  12 us
    ppermute x3, starting transfers between devices, body(): lax.ppermute(slices, 'y_hi', [(i, (i + distance) % 4) for i in range(4)])  12 us
    all_to_all x1, blocking collectives, body(): total = lax.all_to_all(total, 'z', 0, 0, tiled=True)  11.4 us
  transfers between devices with their start and end apart: 10, of which 6 were waited for; matrix products, arithmetic and copies ran while one was open for 0% of the time, Pallas kernels for 7%

profile of v4, /device:TPU:1, one launch (start us, length us, event | category | flops | bytes accessed | tf_op | source)
XLA Modules:
  0.0 181.9 jit_solution(3977193380065580402)
XLA Ops:
  0.0 2.0 %pack.1 = (bf16[392,256]{1,0:T(8,128)(2,1)}, bf16[392,256]{1,0:T(8,128)(2,1)}, bf16[16,48,128]{2,1,0:T(8,128)(2,1)}) custom-call(s32[1]{0:T(128)} %bitcast.1.core_ref, bf16[2,64,512]{2,1,0:T(8,128)(2,1)} %q_in.1, bf16[2,64,512]{2,1,0:T(8,128)(2,1)} %k_in.1, bf16[2,64,512]{2,1,0:T(8,128)(2,1)} %v_in.1, f32[1,2,64]{2,1,0:T(2,128)} %rate_in.1, ...), custom_call_target="tpu_custom_call" | custom-call | tf_op jit(solution)/shard_map/pack/pallas_call | solution.py:328
  2.0 12.0 %all-to-all-start = ((bf16[16,48,128]{2,1,0:T(8,128)(2,1)}), bf16[16,48,128]{2,1,0:T(8,128)(2,1)S(1)}, u32[]{:S(2)}, u32[]{:S(2)}) async-start(bf16[16,48,128]{2,1,0:T(8,128)(2,1)} %get-tuple-element.20), calls=%async_computation | async-start | bytes 393216 | tf_op jit(solution)/shard_map/all_to_all | solution.py:338
  14.0 2.0 %collective-permute-start = (bf16[392,256]{1,0:T(8,128)(2,1)}, bf16[392,256]{1,0:T(8,128)(2,1)S(1)}, u32[]{:S(2)}, u32[]{:S(2)}) collective-permute-start(bf16[392,256]{1,0:T(8,128)(2,1)} %get-tuple-element.17), channel_id=1, source_target_pairs={{0,1},{1,0},{2,3},{3,2},{4,5},{5,4},{6,7},{7,6},{8,9},{9,8},{10,11... | collective-permute-start | bytes 602120 | tf_op jit(solution)/shard_map/ppermute | solution.py:339
  16.0 1.5 collective-permute-done.arrived_ref
  17.6 6.6 %all-to-all-done.dealt_ref = bf16[16,48,128]{2,1,0:T(8,128)(2,1)S(1)} async-done(((bf16[16,48,128]{2,1,0:T(8,128)(2,1)}), bf16[16,48,128]{2,1,0:T(8,128)(2,1)S(1)}, u32[]{:S(2)}, u32[]{:S(2)}) %all-to-all-start) | async-done | bytes 196640 | tf_op jit(solution)/shard_map/all_to_all | solution.py:338
  24.2 0.2 merge.1
  24.4 26.4 %all_to_all.30.pool_ref = bf16[4,336,256]{2,1,0:T(8,128)(2,1)S(1)} all-to-all(bf16[4,336,256]{2,1,0:T(8,128)(2,1)S(1)} %get-tuple-element.21), channel_id=1, replica_groups=mesh['y_lo'=2,'x'=4,'y_hi'=4,'z'=8,'core'=2] {'y_hi'}, dimensions={0} | all-to-all | bytes 1376256 | tf_op jit(solution)/shard_map/all_to_all | solution.py:358
  50.8 1.1 grad.1
  51.8 10.8 %all_to_all.31.parts_ref = bf16[8,96,128]{2,1,0:T(8,128)(2,1)S(1)} all-to-all(bf16[8,96,128]{2,1,0:T(8,128)(2,1)S(1)} %get-tuple-element.23), channel_id=1, replica_groups=mesh['y_lo'=2,'x'=4,'y_hi'=4,'z'=8,'core'=2] {'z'}, dimensions={0} | all-to-all | bytes 393216 | tf_op jit(solution)/shard_map/all_to_all | solution.py:368
  62.6 11.4 %all_to_all.32.piece_ref = bf16[8,96,128]{2,1,0:T(8,128)(2,1)S(1)} all-to-all(bf16[8,96,128]{2,1,0:T(8,128)(2,1)S(1)} %sum.1), channel_id=1, replica_groups=mesh['y_lo'=2,'x'=4,'y_hi'=4,'z'=8,'core'=2] {'z'}, dimensions={0} | all-to-all | bytes 393216 | tf_op jit(solution)/shard_map/all_to_all | solution.py:381
  74.0 1.0 widen.1
  75.0 3.8 %all-to-all-start.4 = ((bf16[4,8,96,128]{3,2,1,0:T(8,128)(2,1)}), bf16[4,8,96,128]{3,2,1,0:T(8,128)(2,1)S(1)}, u32[]{:S(2)}, u32[]{:S(2)}) async-start(bf16[4,8,96,128]{3,2,1,0:T(8,128)(2,1)} %widen.1), calls=%async_computation.4 | async-start | bytes 1572864 | tf_op jit(solution)/shard_map/all_to_all | solution.py:391
  78.8 2.1 %collective-permute-start.1 = (bf16[2,256,256]{2,1,0:T(8,128)(2,1)S(1)}, bf16[2,256,256]{2,1,0:T(8,128)(2,1)S(1)}, u32[]{:S(2)}, u32[]{:S(2)}) collective-permute-start(bf16[2,256,256]{2,1,0:T(8,128)(2,1)S(1)} %get-tuple-element.19), channel_id=1, source_target_pairs={{0,2},{2,4},{4,6},{6,8},{8,10},{10,12},{12,14},{14,16},{16,18},{18... | collective-permute-start | bytes 786440 | tf_op jit(solution)/shard_map/ppermute | solution.py:349
  80.9 14.6 %collective-permute-done.1 = bf16[2,256,256]{2,1,0:T(8,128)(2,1)S(1)} collective-permute-done((bf16[2,256,256]{2,1,0:T(8,128)(2,1)S(1)}, bf16[2,256,256]{2,1,0:T(8,128)(2,1)S(1)}, u32[]{:S(2)}, u32[]{:S(2)}) %collective-permute-start.1) | collective-permute-done | bytes 262176 | tf_op jit(solution)/shard_map/ppermute | solution.py:349
  95.5 1.9 %collective-permute-start.2 = (bf16[2,256,256]{2,1,0:T(8,128)(2,1)S(1)}, bf16[2,256,256]{2,1,0:T(8,128)(2,1)S(1)}, u32[]{:S(2)}, u32[]{:S(2)}) collective-permute-start(bf16[2,256,256]{2,1,0:T(8,128)(2,1)S(1)} %collective-permute-done.1), channel_id=1, source_target_pairs={{0,2},{2,4},{4,6},{6,8},{8,10},{10,12},{12,14},{14,16},{16,18},{18... | collective-permute-start | bytes 786440 | tf_op jit(solution)/shard_map/ppermute | solution.py:372
  97.4 17.9 %collective-permute-done.2 = bf16[2,256,256]{2,1,0:T(8,128)(2,1)S(1)} collective-permute-done((bf16[2,256,256]{2,1,0:T(8,128)(2,1)S(1)}, bf16[2,256,256]{2,1,0:T(8,128)(2,1)S(1)}, u32[]{:S(2)}, u32[]{:S(2)}) %collective-permute-start.2) | collective-permute-done | bytes 262176 | tf_op jit(solution)/shard_map/ppermute | solution.py:372
  115.3 1.9 %collective-permute-start.3 = (bf16[2,256,256]{2,1,0:T(8,128)(2,1)S(1)}, bf16[2,256,256]{2,1,0:T(8,128)(2,1)S(1)}, u32[]{:S(2)}, u32[]{:S(2)}) collective-permute-start(bf16[2,256,256]{2,1,0:T(8,128)(2,1)S(1)} %collective-permute-done.2), channel_id=1, source_target_pairs={{0,2},{2,4},{4,6},{6,8},{8,10},{10,12},{12,14},{14,16},{16,18},{18... | collective-permute-start | bytes 786440 | tf_op jit(solution)/shard_map/ppermute | solution.py:382
  117.2 3.4 %collective-permute-start.5 = (bf16[384,256]{1,0:T(8,128)(2,1)S(1)}, bf16[384,256]{1,0:T(8,128)(2,1)S(1)}, u32[]{:S(2)}, u32[]{:S(2)}) collective-permute-start(bf16[384,256]{1,0:T(8,128)(2,1)S(1)} %get-tuple-element.24.f0_ref), channel_id=1, source_target_pairs={{0,16},{16,32},{32,48},{48,0},{1,17},{17,33},{33,49},{49,1},{2,18}... | collective-permute-start | bytes 589832 | tf_op jit(solution)/shard_map/ppermute | solution.py:371
  120.6 3.0 %collective-permute-start.6 = (bf16[384,256]{1,0:T(8,128)(2,1)S(1)}, bf16[384,256]{1,0:T(8,128)(2,1)S(1)}, u32[]{:S(2)}, u32[]{:S(2)}) collective-permute-start(bf16[384,256]{1,0:T(8,128)(2,1)S(1)} %get-tuple-element.24.f0_ref), channel_id=1, source_target_pairs={{0,32},{16,48},{32,0},{48,16},{1,33},{17,49},{33,1},{49,17},{2,34}... | collective-permute-start | bytes 589832 | tf_op jit(solution)/shard_map/ppermute | solution.py:371
  123.7 5.5 %collective-permute-start.7 = (bf16[384,256]{1,0:T(8,128)(2,1)S(1)}, bf16[384,256]{1,0:T(8,128)(2,1)S(1)}, u32[]{:S(2)}, u32[]{:S(2)}) collective-permute-start(bf16[384,256]{1,0:T(8,128)(2,1)S(1)} %get-tuple-element.24.f0_ref), channel_id=1, source_target_pairs={{0,48},{16,0},{32,16},{48,32},{1,49},{17,1},{33,17},{49,33},{2,50}... | collective-permute-start | bytes 589832 | tf_op jit(solution)/shard_map/ppermute | solution.py:371
  129.2 0.0 copy-start.2
  129.2 0.6 copy-done.2
  129.8 0.7 dynamic_slice.3.step_ref
  130.5 0.0 collective-permute-done.3._
  130.5 1.9 %collective-permute-start.4 = (bf16[2,256,256]{2,1,0:T(8,128)(2,1)S(1)}, bf16[2,256,256]{2,1,0:T(8,128)(2,1)S(1)}, u32[]{:S(2)}, u32[]{:S(2)}) collective-permute-start(bf16[2,256,256]{2,1,0:T(8,128)(2,1)S(1)} %collective-permute-done.3._), channel_id=1, source_target_pairs={{0,2},{2,4},{4,6},{6,8},{8,10},{10,12},{12,14},{14,16},{16,18},{18... | collective-permute-start | bytes 786440 | tf_op jit(solution)/shard_map/ppermute | solution.py:406
  132.4 2.3 %collective-permute-done.6.f2_ref = bf16[384,256]{1,0:T(8,128)(2,1)S(1)} collective-permute-done((bf16[384,256]{1,0:T(8,128)(2,1)S(1)}, bf16[384,256]{1,0:T(8,128)(2,1)S(1)}, u32[]{:S(2)}, u32[]{:S(2)}) %collective-permute-start.6) | collective-permute-done | bytes 196640 | tf_op jit(solution)/shard_map/ppermute | solution.py:371
  134.8 12.8 %newton.1 = (f32[128,256]{1,0:T(8,128)S(1)}, bf16[4,384,256]{2,1,0:T(8,128)(2,1)S(1)}) custom-call(f32[1]{0:T(128)} %dynamic_slice.3.step_ref, s32[1]{0:T(128)} %bitcast.6.row_ref, bf16[4,8,96,128]{3,2,1,0:T(8,128)(2,1)S(1)} %all-to-all-done.4.total_ref, bf16[384,256]{1,0:T(8,128)(2,1)S(1)} %get-tuple-element.24.f0_ref, ...), custom_call_target="tpu_custom_call" | custom-call | flops 8000000000 | bytes 4000000 | tf_op jit(solution)/shard_map/newton/pallas_call | solution.py:394
  147.6 1.0 collective-permute-done.4
  148.6 1.3 window.1
  149.9 0.0 copy-start.1
  149.9 31.2 %all_to_all.33.parts_ref = bf16[16,2,8,256]{3,2,1,0:T(8,128)(2,1)S(1)} all-to-all(bf16[16,2,8,256]{3,2,1,0:T(8,128)(2,1)S(1)} %window.1), channel_id=1, replica_groups=mesh['y_lo'=2,'x'=4,'y_hi'=4,'z'=8,'core'=2] {'core','y_lo','x'}, dimensions={0} | all-to-all | bytes 262144 | tf_op jit(solution)/shard_map/all_to_all | solution.py:416
  181.1 0.8 norm.1
  (8 shorter events, 0.1 us)
Async XLA Ops:
  2.0 15.5 %copy-start = (bf16[392,256]{1,0:T(8,128)(2,1)S(1)}, bf16[392,256]{1,0:T(8,128)(2,1)}, u32[]{:S(2)}) copy-start(bf16[392,256]{1,0:T(8,128)(2,1)} %get-tuple-element.16.mine_ref) | copy-start | bytes 602116
  2.0 22.2 %all-to-all-start = ((bf16[16,48,128]{2,1,0:T(8,128)(2,1)}), bf16[16,48,128]{2,1,0:T(8,128)(2,1)S(1)}, u32[]{:S(2)}, u32[]{:S(2)}) async-start(bf16[16,48,128]{2,1,0:T(8,128)(2,1)} %get-tuple-element.20), calls=%async_computation | async-start | bytes 393216 | tf_op jit(solution)/shard_map/all_to_all | solution.py:338
  14.0 3.5 %collective-permute-start = (bf16[392,256]{1,0:T(8,128)(2,1)}, bf16[392,256]{1,0:T(8,128)(2,1)S(1)}, u32[]{:S(2)}, u32[]{:S(2)}) collective-permute-start(bf16[392,256]{1,0:T(8,128)(2,1)} %get-tuple-element.17), channel_id=1, source_target_pairs={{0,1},{1,0},{2,3},{3,2},{4,5},{5,4},{6,7},{7,6},{8,9},{9,8},{10,11... | collective-permute-start | bytes 602120 | tf_op jit(solution)/shard_map/ppermute | solution.py:339
  75.0 59.8 %all-to-all-start.4 = ((bf16[4,8,96,128]{3,2,1,0:T(8,128)(2,1)}), bf16[4,8,96,128]{3,2,1,0:T(8,128)(2,1)S(1)}, u32[]{:S(2)}, u32[]{:S(2)}) async-start(bf16[4,8,96,128]{3,2,1,0:T(8,128)(2,1)} %widen.1), calls=%async_computation.4 | async-start | bytes 1572864 | tf_op jit(solution)/shard_map/all_to_all | solution.py:391
  78.8 16.7 %collective-permute-start.1 = (bf16[2,256,256]{2,1,0:T(8,128)(2,1)S(1)}, bf16[2,256,256]{2,1,0:T(8,128)(2,1)S(1)}, u32[]{:S(2)}, u32[]{:S(2)}) collective-permute-start(bf16[2,256,256]{2,1,0:T(8,128)(2,1)S(1)} %get-tuple-element.19), channel_id=1, source_target_pairs={{0,2},{2,4},{4,6},{6,8},{8,10},{10,12},{12,14},{14,16},{16,18},{18... | collective-permute-start | bytes 786440 | tf_op jit(solution)/shard_map/ppermute | solution.py:349
  95.5 19.8 %collective-permute-start.2 = (bf16[2,256,256]{2,1,0:T(8,128)(2,1)S(1)}, bf16[2,256,256]{2,1,0:T(8,128)(2,1)S(1)}, u32[]{:S(2)}, u32[]{:S(2)}) collective-permute-start(bf16[2,256,256]{2,1,0:T(8,128)(2,1)S(1)} %collective-permute-done.1), channel_id=1, source_target_pairs={{0,2},{2,4},{4,6},{6,8},{8,10},{10,12},{12,14},{14,16},{16,18},{18... | collective-permute-start | bytes 786440 | tf_op jit(solution)/shard_map/ppermute | solution.py:372
  115.3 15.2 %collective-permute-start.3 = (bf16[2,256,256]{2,1,0:T(8,128)(2,1)S(1)}, bf16[2,256,256]{2,1,0:T(8,128)(2,1)S(1)}, u32[]{:S(2)}, u32[]{:S(2)}) collective-permute-start(bf16[2,256,256]{2,1,0:T(8,128)(2,1)S(1)} %collective-permute-done.2), channel_id=1, source_target_pairs={{0,2},{2,4},{4,6},{6,8},{8,10},{10,12},{12,14},{14,16},{16,18},{18... | collective-permute-start | bytes 786440 | tf_op jit(solution)/shard_map/ppermute | solution.py:382
  117.2 15.2 %collective-permute-start.5 = (bf16[384,256]{1,0:T(8,128)(2,1)S(1)}, bf16[384,256]{1,0:T(8,128)(2,1)S(1)}, u32[]{:S(2)}, u32[]{:S(2)}) collective-permute-start(bf16[384,256]{1,0:T(8,128)(2,1)S(1)} %get-tuple-element.24.f0_ref), channel_id=1, source_target_pairs={{0,16},{16,32},{32,48},{48,0},{1,17},{17,33},{33,49},{49,1},{2,18}... | collective-permute-start | bytes 589832 | tf_op jit(solution)/shard_map/ppermute | solution.py:371
  120.6 14.1 %collective-permute-start.6 = (bf16[384,256]{1,0:T(8,128)(2,1)S(1)}, bf16[384,256]{1,0:T(8,128)(2,1)S(1)}, u32[]{:S(2)}, u32[]{:S(2)}) collective-permute-start(bf16[384,256]{1,0:T(8,128)(2,1)S(1)} %get-tuple-element.24.f0_ref), channel_id=1, source_target_pairs={{0,32},{16,48},{32,0},{48,16},{1,33},{17,49},{33,1},{49,17},{2,34}... | collective-permute-start | bytes 589832 | tf_op jit(solution)/shard_map/ppermute | solution.py:371
  123.7 11.1 %collective-permute-start.7 = (bf16[384,256]{1,0:T(8,128)(2,1)S(1)}, bf16[384,256]{1,0:T(8,128)(2,1)S(1)}, u32[]{:S(2)}, u32[]{:S(2)}) collective-permute-start(bf16[384,256]{1,0:T(8,128)(2,1)S(1)} %get-tuple-element.24.f0_ref), channel_id=1, source_target_pairs={{0,48},{16,0},{32,16},{48,32},{1,49},{17,1},{33,17},{49,33},{2,50}... | collective-permute-start | bytes 589832 | tf_op jit(solution)/shard_map/ppermute | solution.py:371
  129.2 0.7 copy-start.2
  130.5 18.1 %collective-permute-start.4 = (bf16[2,256,256]{2,1,0:T(8,128)(2,1)S(1)}, bf16[2,256,256]{2,1,0:T(8,128)(2,1)S(1)}, u32[]{:S(2)}, u32[]{:S(2)}) collective-permute-start(bf16[2,256,256]{2,1,0:T(8,128)(2,1)S(1)} %collective-permute-done.3._), channel_id=1, source_target_pairs={{0,2},{2,4},{4,6},{6,8},{8,10},{10,12},{12,14},{14,16},{16,18},{18... | collective-permute-start | bytes 786440 | tf_op jit(solution)/shard_map/ppermute | solution.py:406
  149.9 31.2 %copy-start.1 = (f32[4096]{0:T(1024)S(1)}, f32[4096]{0:T(1024)}, u32[]{:S(2)}) copy-start(f32[4096]{0:T(1024)} %param.17) | copy-start | bytes 49156

commit v5 on v3

--- a/solution.py
+++ b/solution.py
@@ -56,7 +56,7 @@
 
 
 def pack_kernel(
-    core_ref, q_in, k_in, v_in, rate_in, gate_in, up_in, down_in, mine_ref, other_ref, *scratch
+    core_ref, q_in, k_in, v_in, rate_in, gate_in, up_in, down_in, mine_ref, other_ref, deal_ref, *scratch
 ):
     sources = (q_in, k_in, v_in, rate_in, gate_in, up_in, down_in)
     q_ref, k_ref, v_ref, rate_ref, gate_ref, up_ref, down_ref = scratch[:7]
@@ -76,17 +76,12 @@
             for block in range(2):
                 first = (index * 2 + block) * 64
                 target[first : first + 64, :] = ref[block, :, columns]
-        for index, ref in enumerate((gate_ref, up_ref)):
-            wide = ref[head].astype(F32)
-            pair = jnp.concatenate([wide[:, :DH], wide[:, DH:]], 0)
-            target[384 + 8 * index : 392 + 8 * index, :] = pair.astype(BF)
-        target[400:408, :] = down_ref[head]
         rate = rate_ref[0, head : head + 1, :]
         high = rate.astype(BF).astype(F32)
         middle = (rate - high).astype(BF).astype(F32)
         low = (rate - high) - middle
         terms = jnp.concatenate([high, middle, low, jnp.zeros_like(rate)], 1)
-        target[408:416, :] = jnp.broadcast_to(terms, (8, DH)).astype(BF)
+        target[384:392, :] = jnp.broadcast_to(terms, (8, DH)).astype(BF)
 
     for head in range(2):
 
@@ -95,8 +90,17 @@
             fill(mine_ref, head)
             fill(other_ref, 1 - head)
 
-
-def arrange_kernel(core_ref, mine_ref, arrived_ref, own_ref, context_ref, pool_ref, weight_ref):
+        tiles = []
+        for ref in (gate_ref, up_ref):
+            wide = ref[head].astype(F32)
+            tiles += [wide[:, :DH], wide[:, DH:]]
+        tiles.append(down_ref[head].astype(F32))
+        piece = jnp.concatenate(tiles, 0).astype(BF)
+        for target in range(CHIPS):
+            deal_ref[2 * target + head] = piece
+
+
+def arrange_kernel(core_ref, mine_ref, arrived_ref, own_ref, context_ref, pool_ref):
     own_ref[core_ref[0]] = mine_ref[...]
     own_ref[1 - core_ref[0]] = arrived_ref[...]
     for source in range(2):
@@ -105,35 +109,27 @@
             first = 128 * index + 64 * source
             rows = slice(128 * (index + 1), 128 * (index + 1) + 64)
             pool_ref[first : first + 64, :] = own_ref[source, rows, :]
-        pool_ref[256 + 8 * source : 264 + 8 * source, :] = own_ref[source, 408:416, :]
-    for row in range(4):
-        lanes = slice(row % 2 * PART, (row % 2 + 1) * PART)
-        pieces = []
-        for index in range(2):
-            first = 384 + 8 * index
-            both = [own_ref[src, first : first + 8, lanes].astype(F32) for src in range(2)]
-            rows = slice(row // 2 * 4, row // 2 * 4 + 4)
-            pieces += [one[rows] for one in both]
-        piece = jnp.concatenate(pieces, 0).astype(BF)
-        down = jnp.concatenate([own_ref[src, 400:408, :].astype(F32) for src in range(2)], 0)
-        down = down.astype(BF)
-        for depth in range(8):
-            weight_ref[row * 8 + depth, 0:16, :] = piece
-            weight_ref[row * 8 + depth, 16:32, :] = down[:, :128]
-            weight_ref[row * 8 + depth, 32:48, :] = down[:, 128:]
-
-
-def grad_kernel(row_ref, p0_ref, p1_ref, p2_ref, p3_ref, raw_ref, grad_ref, slice_ref, down_ref):
+        pool_ref[256 + 8 * source : 264 + 8 * source, :] = own_ref[source, 384:392, :]
+
+
+def grad_kernel(row_ref, p0_ref, p1_ref, p2_ref, p3_ref, raw_ref, grad_ref, slices_ref, down_ref):
     pools = (p0_ref, p1_ref, p2_ref, p3_ref)
-    weights = []
+    out_row = lax.broadcasted_iota(jnp.int32, (DH, 2 * DH), 0)
+    in_row = lax.broadcasted_iota(jnp.int32, (DH, 2 * DH), 1)
     for index in range(2):
-        piece = raw_ref[:, 8 * index : 8 * index + 8, :].astype(F32)
-        weights.append(piece.reshape(DH, PART).astype(BF))
-        slice_ref[index * DH : (index + 1) * DH, :] = weights[index]
-        half = raw_ref[:, 16 + 16 * index : 32 + 16 * index, :]
-        down_ref[:, index * 128 : (index + 1) * 128] = half.reshape(DF, 128)
-    gate_part, up_part = weights
-    down_part = down_ref[pl.ds(pl.multiple_of(row_ref[0] * PART, PART), PART), :]
+        mixed = raw_ref[:, 8 * index : 8 * index + 8, :].astype(F32)
+        mixed = mixed.reshape(2 * DH, DH).astype(BF)
+        rows = slice(index * DH, (index + 1) * DH)
+        for half in range(2):
+            pick = (out_row // 4) * 8 + half * 4 + out_row % 4
+            chosen = jnp.where(in_row == pick, 1.0, 0.0).astype(BF)
+            ordered = matmul(chosen, mixed).astype(BF)
+            slices_ref[2 * half, rows, :] = ordered[:, :PART]
+            slices_ref[2 * half + 1, rows, :] = ordered[:, PART:]
+    down_ref[...] = raw_ref[:, 16:24, :].astype(F32).reshape(DF, DH).astype(BF)
+    row = row_ref[0]
+    weights = (slices_ref[row, :DH, :], slices_ref[row, DH:, :])
+    down_part = down_ref[pl.ds(pl.multiple_of(row * PART, PART), PART), :]
     equal = lax.broadcasted_iota(jnp.int32, (64, 64), 0) == lax.broadcasted_iota(
         jnp.int32, (64, 64), 1
     )
@@ -145,6 +141,7 @@
             spread = jnp.where(equal, jnp.broadcast_to(rate, (64, 64)), 0.0)
             columns.append(jnp.sum(spread, axis=1, keepdims=True))
     rate_col = jnp.concatenate(columns, 0)
+    gate_part, up_part = weights
     keys_now = rms_norm(jnp.concatenate([pool[0:128, :] for pool in pools], 0))
     vals_now = jnp.concatenate([pool[128:256, :] for pool in pools], 0)
     gate_pre = matmul(keys_now, gate_part)
@@ -163,21 +160,20 @@
         grad_ref[:, index * 32 : index * 32 + 32, :] = grad.astype(BF)
 
 
-def sum_kernel(parts_ref, _, total_ref):
+def sum_kernel(parts_ref, total_ref):
     total = jnp.sum(parts_ref[...].astype(F32), axis=0, keepdims=True)
     total_ref[...] = jnp.broadcast_to(total, (8, 96, PART)).astype(BF)
 
 
-def widen_kernel(row_ref, piece_ref, f0_ref, f1_ref, f2_ref, f3_ref, _, total_ref, slices_ref):
+def widen_kernel(piece_ref, total_ref):
     for row in range(4):
         total_ref[row] = piece_ref[...]
-    for distance, ref in enumerate((f0_ref, f1_ref, f2_ref, f3_ref)):
-        slices_ref[lax.rem(row_ref[0] + 4 - distance, 4)] = ref[...]
-
-
-def whole_weights(slices_ref, index):
-    rows = slice(index * DH, (index + 1) * DH)
-    return jnp.concatenate([slices_ref[row, rows, :] for row in range(4)], 1)
+
+
+def whole_weights(slices_ref):
+    gate_fast = jnp.concatenate([slices_ref[row, :DH, :] for row in range(4)], 1)
+    up_fast = jnp.concatenate([slices_ref[row, DH:, :] for row in range(4)], 1)
+    return gate_fast, up_fast
 
 
 def attention_kernel(
@@ -227,14 +223,15 @@
             part = matmul(weights, rows_of(distance, 1, block))
             result = part if result is None else result + part
         if block == 0:
-            gate_fast, up_fast = whole_weights(slices_ref, 0), whole_weights(slices_ref, 1)
-            result = result + fast_forward(query, gate_fast, up_fast, down_ref[...])
+            result = result + fast_forward(query, *whole_weights(slices_ref), down_ref[...])
         else:
             result = result + fast_ref[...]
         out_ref[:, block] = result.reshape(16, 8, DH).astype(BF)
 
 
-def newton_kernel(step_ref, total_ref, slices_ref, down_ref, own_ref, _, fast_ref, iterate_ref):
+def newton_kernel(
+    step_ref, total_ref, slices_ref, down_ref, own_ref, _, fast_ref, iterate_ref
+):
     for index in range(3):
         rows = slice(index * 32, index * 32 + 32)
         pieces = [total_ref[row, :, rows, :].astype(F32).reshape(DH, PART) for row in range(4)]
@@ -270,8 +267,9 @@
     lax.fori_loop(0, 2, coarse_step, 0)
     lax.fori_loop(0, NS_STEPS - 2, fine_step, 0)
     step = step_ref[0]
-    gate_fast = (whole_weights(slices_ref, 0).astype(F32) + step * iterate_ref[0]).astype(BF)
-    up_fast = (whole_weights(slices_ref, 1).astype(F32) + step * iterate_ref[1]).astype(BF)
+    gate_fast, up_fast = whole_weights(slices_ref)
+    gate_fast = (gate_fast.astype(F32) + step * iterate_ref[0]).astype(BF)
+    up_fast = (up_fast.astype(F32) + step * iterate_ref[1]).astype(BF)
     down_fast = (down_ref[...].astype(F32) + step * iterate_ref[2].T).astype(BF)
     query = jnp.concatenate([own_ref[0, 64:128, :], own_ref[1, 64:128, :]], 0)
     fast_ref[...] = fast_forward(query, gate_fast, up_fast, down_fast)
@@ -308,31 +306,26 @@
     line = lax.axis_index("y_hi").astype(jnp.int32).reshape(1)
     pieces = (queries, keys, values, token_rates, w_gate, w_up, w_down)
     place = core.astype(jnp.int32).reshape(1)
-    mine, other = pl.pallas_call(
+    mine, other, dealt = pl.pallas_call(
         pack_kernel,
-        out_shape=(shape_of((416, DH)),) * 2,
+        out_shape=(shape_of((392, DH)), shape_of((392, DH)), shape_of((64, 24, DH))),
         in_specs=[SMEM] + [HBM] * 7,
-        out_specs=(VMEM,) * 2,
+        out_specs=(VMEM,) * 3,
         scratch_shapes=[pltpu.VMEM(piece.shape, piece.dtype) for piece in pieces]
         + [pltpu.SemaphoreType.DMA((7,))],
         compiler_params=pltpu.CompilerParams(vmem_limit_bytes=61500 * 1024),
         name="pack",
     )(place, *pieces)
+    dealt = lax.all_to_all(dealt, RING + ("core",), 0, 0, tiled=True)
     arrived = lax.ppermute(other, "core", [(0, 1), (1, 0)])
-    own, context, pool, raw = pl.pallas_call(
+    own, context, pool = pl.pallas_call(
         arrange_kernel,
-        out_shape=(
-            shape_of((2, 416, DH)),
-            shape_of((2, 256, DH)),
-            shape_of((272, DH)),
-            shape_of((CHIPS, 48, 128)),
-        ),
+        out_shape=(shape_of((2, 392, DH)), shape_of((2, 256, DH)), shape_of((272, DH))),
         in_specs=[SMEM, VMEM, VMEM],
-        out_specs=(VMEM,) * 4,
+        out_specs=(VMEM,) * 3,
         compiler_params=PARAMS,
         name="arrange",
     )(place, mine, arrived)
-    raw = lax.all_to_all(raw, RING, 0, 0, tiled=True)
     pools = [pool]
     for distance in range(1, 4):
         pools.append(lax.ppermute(pool, "y_hi", [(i, (i + distance) % 4) for i in range(4)]))
@@ -341,35 +334,32 @@
 
     grad, slices, down_fast = pl.pallas_call(
         grad_kernel,
-        out_shape=(shape_of((8, 96, PART)), shape_of((2 * DH, PART)), shape_of((DF, DH))),
+        out_shape=(shape_of((8, 96, PART)), shape_of((4, 2 * DH, PART)), shape_of((DF, DH))),
         in_specs=[SMEM] + [VMEM] * 5,
         out_specs=(VMEM,) * 3,
         compiler_params=PARAMS,
         name="grad",
-    )(line, *pools, raw)
+    )(line, *pools, dealt)
     parts = lax.all_to_all(grad, "z", 0, 0, tiled=True)
-    fills = [slices]
-    for distance in range(1, 4):
-        fills.append(lax.ppermute(slices, "y_hi", [(i, (i + distance) % 4) for i in range(4)]))
+    chunks.append(lax.ppermute(chunks[-1], RING, ring))
     total = pl.pallas_call(
         sum_kernel,
         out_shape=shape_of((8, 96, PART)),
-        in_specs=[VMEM, ANY],
+        in_specs=[VMEM],
         out_specs=VMEM,
         compiler_params=PARAMS,
         name="sum",
-    )(parts, chunks[0])
+    )(parts)
+    total = lax.all_to_all(total, "z", 0, 0, tiled=True)
     chunks.append(lax.ppermute(chunks[-1], RING, ring))
-    total = lax.all_to_all(total, "z", 0, 0, tiled=True)
-    total, slices = pl.pallas_call(
+    total = pl.pallas_call(
         widen_kernel,
-        out_shape=(shape_of((4, 8, 96, PART)), shape_of((4, 2 * DH, PART))),
-        in_specs=[SMEM] + [VMEM] * 5 + [ANY],
-        out_specs=(VMEM,) * 2,
+        out_shape=shape_of((4, 8, 96, PART)),
+        in_specs=[VMEM],
+        out_specs=VMEM,
         compiler_params=PARAMS,
         name="widen",
-    )(line, total, *fills, chunks[1])
-    chunks.append(lax.ppermute(chunks[-1], RING, ring))
+    )(total)
     total = lax.all_to_all(total, "y_hi", 0, 0, tiled=True)
 
     step = lax.dynamic_slice_in_dim(step_size, core, 1, 0)

time: 170 us -> 181 us (1.065)
  blocking collectives: 11.7 us -> 44 us
  starting transfers between devices: 73.7 us -> 48.1 us
  waiting for transfers between devices: 60.3 us -> 67.9 us
    all_to_all x0 -> x2, blocking collectives: none -> 24.8 us  [the longest x1 13.6 us: body(): parts = lax.all_to_all(grad, 'z', 0, 0, tiled=True)]
    ppermute x1, waiting for transfers between devices: 12.8 us -> 28.3 us  [body(): chunks = [lax.ppermute(context, RING, ring)]]
    ppermute x3 -> x0, starting transfers between devices: 12.1 us -> none  [body(): lax.ppermute(slices, 'y_hi', [(i, (i + distance) % 4) for i in range(4)])]
    ppermute x3, waiting for transfers between devices: 32.9 us -> 23.5 us  [body(): chunks.append(lax.ppermute(chunks[-1], RING, ring))]
    all_to_all x1, blocking collectives: 11.7 us -> 19.2 us  [body(): gathered = lax.all_to_all(combined, ('core', 'y_lo', 'x'), 0, 0, tiled=True)]
    ppermute x1, starting transfers between devices: 8.75 us -> 2.36 us  [body(): arrived = lax.ppermute(other, 'core', [(0, 1), (1, 0)])]
    ppermute x3, waiting for transfers between devices: 10.9 us -> 13.8 us  [body(): lax.ppermute(pool, 'y_hi', [(i, (i + distance) % 4) for i in range(4)])]
    ppermute x3, starting transfers between devices: 8.25 us -> 5.73 us  [body(): chunks.append(lax.ppermute(chunks[-1], RING, ring))]
  transfers between devices with their start and end apart: 15 -> 10, of which waited for: 9 -> 8; matrix products, arithmetic and copies ran while one was open for 0% -> 0% of each run, Pallas kernels for 7% -> 7%
where the time goes in v5:
time: 181 us
  waiting for transfers between devices  67.9 us (38%)
  starting transfers between devices  48.1 us (27%)
  blocking collectives  44 us (24%)
  Pallas kernels  19.4 us (11%)
    ppermute x1, waiting for transfers between devices, body(): chunks = [lax.ppermute(context, RING, ring)]  28.3 us
    ppermute x3, waiting for transfers between devices, body(): chunks.append(lax.ppermute(chunks[-1], RING, ring))  23.5 us
    all_to_all x1, blocking collectives, body(): gathered = lax.all_to_all(combined, ('core', 'y_lo', 'x'), 0, 0, tiled=True)  19.2 us
    all_to_all x1, starting transfers between devices, body(): dealt = lax.all_to_all(dealt, RING + ('core',), 0, 0, tiled=True)  17.8 us
    ppermute x3, starting transfers between devices, body(): lax.ppermute(pool, 'y_hi', [(i, (i + distance) % 4) for i in range(4)])  14.6 us
    ppermute x3, waiting for transfers between devices, body(): lax.ppermute(pool, 'y_hi', [(i, (i + distance) % 4) for i in range(4)])  13.8 us
    all_to_all x1, blocking collectives, body(): parts = lax.all_to_all(grad, 'z', 0, 0, tiled=True)  13.6 us
    pallas_call x1, Pallas kernels, body(): pl.pallas_call(newton_kernel, out_shape=shape_of((TOK, DH), F32), in_spec...  12.7 us
  transfers between devices with their start and end apart: 10, of which 8 were waited for; matrix products, arithmetic and copies ran while one was open for 0% of the time, Pallas kernels for 7%

profile of v5, /device:TPU:1, one launch (start us, length us, event | category | flops | bytes accessed | tf_op | source)
XLA Modules:
  0.0 180.8 jit_solution(8274354639120321768)
XLA Ops:
  0.0 2.2 %pack.1 = (bf16[392,256]{1,0:T(8,128)(2,1)}, bf16[392,256]{1,0:T(8,128)(2,1)}, bf16[64,24,256]{2,1,0:T(8,128)(2,1)}) custom-call(s32[1]{0:T(128)} %bitcast.1.core_ref, bf16[2,64,512]{2,1,0:T(8,128)(2,1)} %q_in.1, bf16[2,64,512]{2,1,0:T(8,128)(2,1)} %k_in.1, bf16[2,64,512]{2,1,0:T(8,128)(2,1)} %v_in.1, f32[1,2,64]{2,1,0:T(2,128)} %rate_in.1, ...), custom_call_target="tpu_custom_call" | custom-call | tf_op jit(solution)/shard_map/pack/pallas_call | solution.py:309
  2.2 17.8 %all-to-all-start = ((bf16[64,24,256]{2,1,0:T(8,128)(2,1)}), bf16[64,24,256]{2,1,0:T(8,128)(2,1)S(1)}, u32[]{:S(2)}, u32[]{:S(2)}) async-start(bf16[64,24,256]{2,1,0:T(8,128)(2,1)} %get-tuple-element.19), calls=%async_computation | async-start | bytes 1572864 | tf_op jit(solution)/shard_map/all_to_all | solution.py:319
  20.0 2.4 %collective-permute-start = (bf16[392,256]{1,0:T(8,128)(2,1)S(1)}, bf16[392,256]{1,0:T(8,128)(2,1)S(1)}, u32[]{:S(2)}, u32[]{:S(2)}) collective-permute-start(bf16[392,256]{1,0:T(8,128)(2,1)S(1)} %copy-done.2), channel_id=1, source_target_pairs={{0,1},{1,0},{2,3},{3,2},{4,5},{5,4},{6,7},{7,6},{8,9},{9,8},{10,11... | collective-permute-start | bytes 602120 | tf_op jit(solution)/shard_map/ppermute | solution.py:320
  22.4 1.1 collective-permute-done.arrived_ref
  23.5 0.1 arrange.1
  23.5 4.1 %collective-permute-start.5 = (bf16[272,256]{1,0:T(8,128)(2,1)S(1)}, bf16[272,256]{1,0:T(8,128)(2,1)S(1)}, u32[]{:S(2)}, u32[]{:S(2)}) collective-permute-start(bf16[272,256]{1,0:T(8,128)(2,1)S(1)} %get-tuple-element.18.p0_ref), channel_id=1, source_target_pairs={{0,16},{16,32},{32,48},{48,0},{1,17},{17,33},{33,49},{49,1},{2,18}... | collective-permute-start | bytes 417800 | tf_op jit(solution)/shard_map/ppermute | solution.py:331
  27.6 5.4 %collective-permute-start.6 = (bf16[272,256]{1,0:T(8,128)(2,1)S(1)}, bf16[272,256]{1,0:T(8,128)(2,1)S(1)}, u32[]{:S(2)}, u32[]{:S(2)}) collective-permute-start(bf16[272,256]{1,0:T(8,128)(2,1)S(1)} %get-tuple-element.18.p0_ref), channel_id=1, source_target_pairs={{0,32},{16,48},{32,0},{48,16},{1,33},{17,49},{33,1},{49,17},{2,34}... | collective-permute-start | bytes 417800 | tf_op jit(solution)/shard_map/ppermute | solution.py:331
  33.1 5.1 %collective-permute-start.7 = (bf16[272,256]{1,0:T(8,128)(2,1)S(1)}, bf16[272,256]{1,0:T(8,128)(2,1)S(1)}, u32[]{:S(2)}, u32[]{:S(2)}) collective-permute-start(bf16[272,256]{1,0:T(8,128)(2,1)S(1)} %get-tuple-element.18.p0_ref), channel_id=1, source_target_pairs={{0,48},{16,0},{32,16},{48,32},{1,49},{17,1},{33,17},{49,33},{2,50}... | collective-permute-start | bytes 417800 | tf_op jit(solution)/shard_map/ppermute | solution.py:331
  38.2 8.8 %collective-permute-done.5.p1_ref = bf16[272,256]{1,0:T(8,128)(2,1)S(1)} collective-permute-done((bf16[272,256]{1,0:T(8,128)(2,1)S(1)}, bf16[272,256]{1,0:T(8,128)(2,1)S(1)}, u32[]{:S(2)}, u32[]{:S(2)}) %collective-permute-start.5) | collective-permute-done | bytes 139296 | tf_op jit(solution)/shard_map/ppermute | solution.py:331
  47.0 4.9 %collective-permute-done.6.p2_ref = bf16[272,256]{1,0:T(8,128)(2,1)S(1)} collective-permute-done((bf16[272,256]{1,0:T(8,128)(2,1)S(1)}, bf16[272,256]{1,0:T(8,128)(2,1)S(1)}, u32[]{:S(2)}, u32[]{:S(2)}) %collective-permute-start.6) | collective-permute-done | bytes 139296 | tf_op jit(solution)/shard_map/ppermute | solution.py:331
  51.9 0.1 collective-permute-done.7.p3_ref
  52.0 1.2 all-to-all-done.raw_ref
  53.1 1.3 grad.1
  54.4 13.6 %all_to_all.25.parts_ref = bf16[8,96,128]{2,1,0:T(8,128)(2,1)S(1)} all-to-all(bf16[8,96,128]{2,1,0:T(8,128)(2,1)S(1)} %get-tuple-element.22), channel_id=1, replica_groups=mesh['y_lo'=2,'x'=4,'y_hi'=4,'z'=8,'core'=2] {'z'}, dimensions={0} | all-to-all | bytes 393216 | tf_op jit(solution)/shard_map/all_to_all | solution.py:343
  68.0 11.2 %all_to_all.26.piece_ref = bf16[8,96,128]{2,1,0:T(8,128)(2,1)S(1)} all-to-all(bf16[8,96,128]{2,1,0:T(8,128)(2,1)S(1)} %sum.1), channel_id=1, replica_groups=mesh['y_lo'=2,'x'=4,'y_hi'=4,'z'=8,'core'=2] {'z'}, dimensions={0} | all-to-all | bytes 393216 | tf_op jit(solution)/shard_map/all_to_all | solution.py:353
  79.3 1.0 widen.1
  80.2 5.5 %all-to-all-start.3 = ((bf16[4,8,96,128]{3,2,1,0:T(8,128)(2,1)}), bf16[4,8,96,128]{3,2,1,0:T(8,128)(2,1)S(1)}, u32[]{:S(2)}, u32[]{:S(2)}) async-start(bf16[4,8,96,128]{3,2,1,0:T(8,128)(2,1)} %widen.1), calls=%async_computation.3 | async-start | bytes 1572864 | tf_op jit(solution)/shard_map/all_to_all | solution.py:363
  85.8 2.1 %collective-permute-start.1 = (bf16[2,256,256]{2,1,0:T(8,128)(2,1)S(1)}, bf16[2,256,256]{2,1,0:T(8,128)(2,1)S(1)}, u32[]{:S(2)}, u32[]{:S(2)}) collective-permute-start(bf16[2,256,256]{2,1,0:T(8,128)(2,1)S(1)} %get-tuple-element.17), channel_id=1, source_target_pairs={{0,2},{2,4},{4,6},{6,8},{8,10},{10,12},{12,14},{14,16},{16,18},{18... | collective-permute-start | bytes 786440 | tf_op jit(solution)/shard_map/ppermute | solution.py:333
  87.9 28.3 %collective-permute-done.1 = bf16[2,256,256]{2,1,0:T(8,128)(2,1)S(1)} collective-permute-done((bf16[2,256,256]{2,1,0:T(8,128)(2,1)S(1)}, bf16[2,256,256]{2,1,0:T(8,128)(2,1)S(1)}, u32[]{:S(2)}, u32[]{:S(2)}) %collective-permute-start.1) | collective-permute-done | bytes 262176 | tf_op jit(solution)/shard_map/ppermute | solution.py:333
  116.2 1.9 %collective-permute-start.2 = (bf16[2,256,256]{2,1,0:T(8,128)(2,1)S(1)}, bf16[2,256,256]{2,1,0:T(8,128)(2,1)S(1)}, u32[]{:S(2)}, u32[]{:S(2)}) collective-permute-start(bf16[2,256,256]{2,1,0:T(8,128)(2,1)S(1)} %collective-permute-done.1), channel_id=1, source_target_pairs={{0,2},{2,4},{4,6},{6,8},{8,10},{10,12},{12,14},{14,16},{16,18},{18... | collective-permute-start | bytes 786440 | tf_op jit(solution)/shard_map/ppermute | solution.py:344
  118.1 13.5 %collective-permute-done.2 = bf16[2,256,256]{2,1,0:T(8,128)(2,1)S(1)} collective-permute-done((bf16[2,256,256]{2,1,0:T(8,128)(2,1)S(1)}, bf16[2,256,256]{2,1,0:T(8,128)(2,1)S(1)}, u32[]{:S(2)}, u32[]{:S(2)}) %collective-permute-start.2) | collective-permute-done | bytes 262176 | tf_op jit(solution)/shard_map/ppermute | solution.py:344
  131.6 1.9 %collective-permute-start.3 = (bf16[2,256,256]{2,1,0:T(8,128)(2,1)S(1)}, bf16[2,256,256]{2,1,0:T(8,128)(2,1)S(1)}, u32[]{:S(2)}, u32[]{:S(2)}) collective-permute-start(bf16[2,256,256]{2,1,0:T(8,128)(2,1)S(1)} %collective-permute-done.2), channel_id=1, source_target_pairs={{0,2},{2,4},{4,6},{6,8},{8,10},{10,12},{12,14},{14,16},{16,18},{18... | collective-permute-start | bytes 786440 | tf_op jit(solution)/shard_map/ppermute | solution.py:354
  133.6 0.0 copy-start.3
  133.6 0.6 copy-done.3
  134.2 0.6 dynamic_slice.3.step_ref
  134.9 10.0 %collective-permute-done.3._ = bf16[2,256,256]{2,1,0:T(8,128)(2,1)S(1)} collective-permute-done((bf16[2,256,256]{2,1,0:T(8,128)(2,1)S(1)}, bf16[2,256,256]{2,1,0:T(8,128)(2,1)S(1)}, u32[]{:S(2)}, u32[]{:S(2)}) %collective-permute-start.3) | collective-permute-done | bytes 262176 | tf_op jit(solution)/shard_map/ppermute | solution.py:354
  144.8 1.9 %collective-permute-start.4 = (bf16[2,256,256]{2,1,0:T(8,128)(2,1)S(1)}, bf16[2,256,256]{2,1,0:T(8,128)(2,1)S(1)}, u32[]{:S(2)}, u32[]{:S(2)}) collective-permute-start(bf16[2,256,256]{2,1,0:T(8,128)(2,1)S(1)} %collective-permute-done.3._), channel_id=1, source_target_pairs={{0,2},{2,4},{4,6},{6,8},{8,10},{10,12},{12,14},{14,16},{16,18},{18... | collective-permute-start | bytes 786440 | tf_op jit(solution)/shard_map/ppermute | solution.py:378
  146.8 12.7 %newton.1.fast_ref = f32[128,256]{1,0:T(8,128)S(1)} custom-call(f32[1]{0:T(128)} %dynamic_slice.3.step_ref, bf16[4,8,96,128]{3,2,1,0:T(8,128)(2,1)S(1)} %all-to-all-done.3.total_ref, bf16[4,512,128]{2,1,0:T(8,128)(2,1)S(1)} %get-tuple-element.20.slices_ref, bf16[512,256]{1,0:T(8,128)(2,1)S(1)} %get-tuple-element.21.down_ref, ...), custom_call_target="tpu_custom_call" | custom-call | flops 8000000000 | bytes 4000000 | tf_op jit(solution)/shard_map/newton/pallas_call | solution.py:366
  159.5 1.3 window.1
  160.8 0.0 copy-start.1
  160.9 19.2 %all_to_all.27.parts_ref = bf16[16,2,8,256]{3,2,1,0:T(8,128)(2,1)S(1)} all-to-all(bf16[16,2,8,256]{3,2,1,0:T(8,128)(2,1)S(1)} %window.1), channel_id=1, replica_groups=mesh['y_lo'=2,'x'=4,'y_hi'=4,'z'=8,'core'=2] {'core','y_lo','x'}, dimensions={0} | all-to-all | bytes 262144 | tf_op jit(solution)/shard_map/all_to_all | solution.py:388
  180.0 0.8 norm.1
  (8 shorter events, 0.0 us)
Async XLA Ops:
  2.2 17.8 %copy-start.2 = (bf16[392,256]{1,0:T(8,128)(2,1)S(1)}, bf16[392,256]{1,0:T(8,128)(2,1)}, u32[]{:S(2)}) copy-start(bf16[392,256]{1,0:T(8,128)(2,1)} %get-tuple-element.15) | copy-start | bytes 602116
  2.2 21.2 %copy-start = (bf16[392,256]{1,0:T(8,128)(2,1)S(1)}, bf16[392,256]{1,0:T(8,128)(2,1)}, u32[]{:S(2)}) copy-start(bf16[392,256]{1,0:T(8,128)(2,1)} %get-tuple-element.14.mine_ref) | copy-start | bytes 602116
  2.2 50.9 %all-to-all-start = ((bf16[64,24,256]{2,1,0:T(8,128)(2,1)}), bf16[64,24,256]{2,1,0:T(8,128)(2,1)S(1)}, u32[]{:S(2)}, u32[]{:S(2)}) async-start(bf16[64,24,256]{2,1,0:T(8,128)(2,1)} %get-tuple-element.19), calls=%async_computation | async-start | bytes 1572864 | tf_op jit(solution)/shard_map/all_to_all | solution.py:319
  20.0 3.4 %collective-permute-start = (bf16[392,256]{1,0:T(8,128)(2,1)S(1)}, bf16[392,256]{1,0:T(8,128)(2,1)S(1)}, u32[]{:S(2)}, u32[]{:S(2)}) collective-permute-start(bf16[392,256]{1,0:T(8,128)(2,1)S(1)} %copy-done.2), channel_id=1, source_target_pairs={{0,1},{1,0},{2,3},{3,2},{4,5},{5,4},{6,7},{7,6},{8,9},{9,8},{10,11... | collective-permute-start | bytes 602120 | tf_op jit(solution)/shard_map/ppermute | solution.py:320
  23.5 23.4 %collective-permute-start.5 = (bf16[272,256]{1,0:T(8,128)(2,1)S(1)}, bf16[272,256]{1,0:T(8,128)(2,1)S(1)}, u32[]{:S(2)}, u32[]{:S(2)}) collective-permute-start(bf16[272,256]{1,0:T(8,128)(2,1)S(1)} %get-tuple-element.18.p0_ref), channel_id=1, source_target_pairs={{0,16},{16,32},{32,48},{48,0},{1,17},{17,33},{33,49},{49,1},{2,18}... | collective-permute-start | bytes 417800 | tf_op jit(solution)/shard_map/ppermute | solution.py:331
  27.6 24.2 %collective-permute-start.6 = (bf16[272,256]{1,0:T(8,128)(2,1)S(1)}, bf16[272,256]{1,0:T(8,128)(2,1)S(1)}, u32[]{:S(2)}, u32[]{:S(2)}) collective-permute-start(bf16[272,256]{1,0:T(8,128)(2,1)S(1)} %get-tuple-element.18.p0_ref), channel_id=1, source_target_pairs={{0,32},{16,48},{32,0},{48,16},{1,33},{17,49},{33,1},{49,17},{2,34}... | collective-permute-start | bytes 417800 | tf_op jit(solution)/shard_map/ppermute | solution.py:331
  33.1 18.9 %collective-permute-start.7 = (bf16[272,256]{1,0:T(8,128)(2,1)S(1)}, bf16[272,256]{1,0:T(8,128)(2,1)S(1)}, u32[]{:S(2)}, u32[]{:S(2)}) collective-permute-start(bf16[272,256]{1,0:T(8,128)(2,1)S(1)} %get-tuple-element.18.p0_ref), channel_id=1, source_target_pairs={{0,48},{16,0},{32,16},{48,32},{1,49},{17,1},{33,17},{49,33},{2,50}... | collective-permute-start | bytes 417800 | tf_op jit(solution)/shard_map/ppermute | solution.py:331
  80.2 66.5 %all-to-all-start.3 = ((bf16[4,8,96,128]{3,2,1,0:T(8,128)(2,1)}), bf16[4,8,96,128]{3,2,1,0:T(8,128)(2,1)S(1)}, u32[]{:S(2)}, u32[]{:S(2)}) async-start(bf16[4,8,96,128]{3,2,1,0:T(8,128)(2,1)} %widen.1), calls=%async_computation.3 | async-start | bytes 1572864 | tf_op jit(solution)/shard_map/all_to_all | solution.py:363
  85.8 30.4 %collective-permute-start.1 = (bf16[2,256,256]{2,1,0:T(8,128)(2,1)S(1)}, bf16[2,256,256]{2,1,0:T(8,128)(2,1)S(1)}, u32[]{:S(2)}, u32[]{:S(2)}) collective-permute-start(bf16[2,256,256]{2,1,0:T(8,128)(2,1)S(1)} %get-tuple-element.17), channel_id=1, source_target_pairs={{0,2},{2,4},{4,6},{6,8},{8,10},{10,12},{12,14},{14,16},{16,18},{18... | collective-permute-start | bytes 786440 | tf_op jit(solution)/shard_map/ppermute | solution.py:333
  116.2 15.5 %collective-permute-start.2 = (bf16[2,256,256]{2,1,0:T(8,128)(2,1)S(1)}, bf16[2,256,256]{2,1,0:T(8,128)(2,1)S(1)}, u32[]{:S(2)}, u32[]{:S(2)}) collective-permute-start(bf16[2,256,256]{2,1,0:T(8,128)(2,1)S(1)} %collective-permute-done.1), channel_id=1, source_target_pairs={{0,2},{2,4},{4,6},{6,8},{8,10},{10,12},{12,14},{14,16},{16,18},{18... | collective-permute-start | bytes 786440 | tf_op jit(solution)/shard_map/ppermute | solution.py:344
  131.6 13.2 %collective-permute-start.3 = (bf16[2,256,256]{2,1,0:T(8,128)(2,1)S(1)}, bf16[2,256,256]{2,1,0:T(8,128)(2,1)S(1)}, u32[]{:S(2)}, u32[]{:S(2)}) collective-permute-start(bf16[2,256,256]{2,1,0:T(8,128)(2,1)S(1)} %collective-permute-done.2), channel_id=1, source_target_pairs={{0,2},{2,4},{4,6},{6,8},{8,10},{10,12},{12,14},{14,16},{16,18},{18... | collective-permute-start | bytes 786440 | tf_op jit(solution)/shard_map/ppermute | solution.py:354
  133.6 0.7 copy-start.3
  144.8 14.7 %collective-permute-start.4 = (bf16[2,256,256]{2,1,0:T(8,128)(2,1)S(1)}, bf16[2,256,256]{2,1,0:T(8,128)(2,1)S(1)}, u32[]{:S(2)}, u32[]{:S(2)}) collective-permute-start(bf16[2,256,256]{2,1,0:T(8,128)(2,1)S(1)} %collective-permute-done.3._), channel_id=1, source_target_pairs={{0,2},{2,4},{4,6},{6,8},{8,10},{10,12},{12,14},{14,16},{16,18},{18... | collective-permute-start | bytes 786440 | tf_op jit(solution)/shard_map/ppermute | solution.py:378
  160.8 19.2 %copy-start.1 = (f32[4096]{0:T(1024)S(1)}, f32[4096]{0:T(1024)}, u32[]{:S(2)}) copy-start(f32[4096]{0:T(1024)} %param.17) | copy-start | bytes 49156
